TPU v7x, 768 devices: a whole 4x8x12 slice. The times are simulated.
768 devices in a mesh: rep: 16 (over x_hi, y), row: 4 (over x_lo, core), col: 12 (over z).
Axes of the slice: x: 4 (x_hi: 2, x_lo: 2; x = x_hi * 2 + x_lo), y: 8, z: 12, core: 2. Of those that a mesh axis runs over, the one named last changes fastest.
Arguments:
- normed: bfloat16 [8192, 5120], P('rep', 'row'), may hold values from -6 to 6
- up_weight: bfloat16 [4, 1280, 13824], P('row', 'rep', 'col'), may hold values from -0.078125 to 0.078125
- cotangent: bfloat16 [8192, 13824], P('rep', 'col'), may hold values from -6 to 6
- lengths: int32 [16], P('rep'), may hold values from 128 to 512
Outputs:
- up_out: bfloat16 [8192, 13824], P(('rep', 'row'), 'col')
- normed_grad: bfloat16 [8192, 5120], P('rep', 'row')
- weight_grad: bfloat16 [4, 1280, 13824], P('row', 'rep', 'col')
All inputs are finite; a program needn't handle non-finite values.
Results may differ from a plain program's by a relative error of at most 0.02.
Values may be sent and summed in bfloat16 or wider, within the bound.
No kernel may reach another device: no remote copies, remote signals or barrier semaphores. Data moves between devices by JAX's collectives and lax.ppermute only.
A program may use at most 32 MiB of HBM per device.

v0:
```python
import math

import jax
import jax.numpy as jnp
from jax import lax
from jax.sharding import PartitionSpec as P


def body(normed, up_weight, cotangent, lengths):
    row_count = normed.shape[0]
    pair_count = lengths.shape[0]
    pair_len = row_count // pair_count
    unit_count = up_weight.shape[2]
    positions = lax.broadcasted_iota(jnp.int32, (pair_count, pair_len), 1)
    valid_rows = (positions < lengths[:, None]).reshape(row_count, 1)
    masked = jnp.where(valid_rows, cotangent, jnp.zeros_like(cotangent))
    columns = normed
    up_partial = jnp.dot(
        columns,
        lax.all_gather(up_weight, "rep", axis=1, tiled=True)[0],
        preferred_element_type=jnp.float32,
    )
    product = lax.dot_general(
        masked,
        lax.all_gather(up_weight, "rep", axis=1, tiled=True)[0],
        (((1,), (1,)), ((), ())),
        preferred_element_type=jnp.float32,
    )
    grad_partial = product
    up_out = lax.psum_scatter(
        up_partial.astype(jnp.bfloat16), "row", scatter_dimension=0, tiled=True
    )
    normed_grad = lax.psum(grad_partial.astype(jnp.bfloat16), "col")
    factor = 1.0 / math.sqrt(row_count * lax.axis_size("rep"))
    keep_rows = up_weight.shape[1]
    columns = normed
    product = lax.dot_general(
        columns, masked, (((0,), (0,)), ((), ())), preferred_element_type=jnp.float32
    )
    weight_sum = lax.psum_scatter(
        (product * factor).astype(jnp.bfloat16), "rep", scatter_dimension=0, tiled=True
    )
    weight_grad = weight_sum.reshape(1, keep_rows, unit_count)
    return (up_out, normed_grad, weight_grad)


def solution(mesh):
    placed = (P("rep", "row"), P("row", "rep", "col"), P("rep", "col"), P("rep"))
    return jax.shard_map(
        body,
        mesh=mesh,
        in_specs=placed,
        out_specs=(P(("rep", "row"), "col"), P("rep", "row"), P("row", "rep", "col")),
        check_vma=False,
    )
```

profile of v0, /device:TPU:6, one launch (start us, length us, event | category | flops | bytes accessed | tf_op | source)
XLA Modules:
  0.0 482.4 jit_solution(3236801333140334413)
XLA Ops:
  7.2 0.0 copy-start
  7.2 0.0 all-gather.2.cloned.1.call-start
  7.2 0.7 all-gather.2.cloned.1.call-update
  7.9 0.0 reduce-scatter.7.cloned.1.call-start
  8.6 0.0 copy-done
  8.6 4.8 fusion.1
  13.4 5.5 %copy.9 = bf16[1280,1152]{1,0:T(8,128)(2,1)} copy(bf16[1280,1152]{0,1:T(8,128)(2,1)} %fusion.1) | data formatting | bytes 5898240
  18.8 0.0 copy-start.1
  18.8 0.0 reduce-scatter.7.cloned.1.call-update
  18.9 0.0 all-reduce.2.cloned.1.call-start
  18.9 100.1 %all-gather.2.cloned.1.call-done = bf16[1,1280,1152]{2,1,0:T(8,128)(2,1)} async-done(((bf16[1,80,1152]{2,1,0:T(8,128)(2,1)}), bf16[1,1280,1152]{2,1,0:T(8,128)(2,1)}) %all-gather.2.cloned.1.call-update) | async-done | bytes 2949136 | tf_op jit(solution)/shard_map/all_gather | solution.py:20
  119.1 0.0 copy-done.1
  119.1 4.8 convolution_convert_fusion
  123.9 0.0 all-reduce.2.cloned.1.call-update
  123.9 0.0 reduce-scatter.5.cloned.1.call-start
  124.0 4.7 convolution_convert_fusion.1
  128.7 0.0 reduce-scatter.5.cloned.1.call-update
  128.7 195.6 %reduce-scatter.7.cloned.1.call-done = bf16[80,1152]{1,0:T(8,128)(2,1)} async-done(((bf16[1280,1152]{1,0:T(8,128)(2,1)}), bf16[80,1152]{1,0:T(8,128)(2,1)}) %reduce-scatter.7.cloned.1.call-update) | async-done | bytes 184336
  324.3 1.1 copy.10
  325.4 0.8 copy.8
  326.3 117.7 %all-reduce.2.cloned.1.call-done = bf16[512,1280]{1,0:T(8,128)(2,1)} async-done(((bf16[512,1280]{1,0:T(8,128)(2,1)}), bf16[512,1280]{1,0:T(8,128)(2,1)}) %all-reduce.2.cloned.1.call-update) | async-done | bytes 1310736 | tf_op jit(solution)/shard_map/psum | solution.py:33
  444.0 29.4 %reduce-scatter.5.cloned.1.call-done = bf16[128,1152]{1,0:T(8,128)(2,1)} async-done(((bf16[512,1152]{1,0:T(8,128)(2,1)}), bf16[128,1152]{1,0:T(8,128)(2,1)}) %reduce-scatter.5.cloned.1.call-update) | async-done | bytes 294928 | tf_op jit(solution)/shard_map/reduce_scatter | solution.py:30
  473.4 2.5 copy.13
  (1 shorter events, 0.0 us)
Async XLA Ops:
  7.2 1.5 copy-start
  7.2 111.9 %all-gather.2.cloned.1.call-start = ((), (), s32[]{:S(2)}) async-start(), calls=%async_computation.2 | async-start | bytes 3133440 | tf_op jit(solution)/shard_map/all_gather | solution.py:20
  7.9 316.4 %reduce-scatter.7.cloned.1.call-start = ((), (), s32[]{:S(2)}) async-start(), calls=%async_computation.5 | async-start | bytes 3133440
  18.8 100.2 %copy-start.1 = (bf16[512,1152]{1,0:T(8,128)(2,1)S(1)}, bf16[512,1152]{1,0:T(8,128)(2,1)}, u32[]{:S(2)}) copy-start(bf16[512,1152]{1,0:T(8,128)(2,1)} %param.6) | copy-start | bytes 3538948
  18.9 425.1 %all-reduce.2.cloned.1.call-start = ((), (), s32[]{:S(2)}) async-start(), calls=%async_computation.4 | async-start | bytes 2621440 | tf_op jit(solution)/shard_map/psum | solution.py:33
  123.9 349.4 %reduce-scatter.5.cloned.1.call-start = ((), (), s32[]{:S(2)}) async-start(), calls=%async_computation.3 | async-start | bytes 1474560 | tf_op jit(solution)/shard_map/reduce_scatter | solution.py:30
Sparse Core Ops, SparseCore 0:
  11.8 107.2 all-gather.1
  124.3 199.9 reduce-scatter.6
  327.3 116.6 all-reduce.1
  447.9 25.4 reduce-scatter.4
where the time goes:
time: 484 us; the launch traced here: 482 us
  waiting for transfers between devices  444 us (92%)
  between operations  14.4 us (3%)
  matrix products  14.3 us (3%)
  local copies, waits for them, and re-layouts  9.91 us (2%)
    unnamed x5, waiting for transfers between devices  196 us
    psum x1, waiting for transfers between devices, body(): normed_grad = lax.psum(grad_partial.astype(jnp.bfloat16), 'col')  118 us
    all_gather x1, waiting for transfers between devices, body(): lax.all_gather(up_weight, 'rep', axis=1, tiled=True)[0]  100 us
    reduce_scatter x1, waiting for transfers between devices, body(): lax.psum_scatter(up_partial.astype(jnp.bfloat16), 'row', scatter_dimensio...  29.4 us
    unnamed x8, local copies, waits for them, and re-layouts  9.91 us
  transfers between devices with their start and end apart: 4, of which 4 were waited for; matrix products, arithmetic and copies ran while one was open for 5% of the time, Pallas kernels for 0%

commit v1 on v0

v1 whole, which is shorter than its diff:
```python
import math

import jax
import jax.numpy as jnp
from jax import lax
from jax.sharding import PartitionSpec as P

NY = 8
NZ = 12
F32 = jnp.float32
BF16 = jnp.bfloat16

X_SWAP = [(i, (i + NY) % (2 * NY)) for i in range(2 * NY)]


def y_shift(step):
    return [(h * NY + y, h * NY + (y + step) % NY) for h in range(2) for y in range(NY)]


def z_shift(step):
    return [(z, (z + step) % NZ) for z in range(NZ)]


def over_rep(value, pairs):
    return lax.ppermute(value, "rep", pairs)


def over_col(value, step):
    return lax.ppermute(value, "col", z_shift(step))


def add(*terms):
    total = terms[0].astype(F32)
    for term in terms[1:]:
        total = total + term.astype(F32)
    return total.astype(BF16)


def pick(blocks, index):
    return lax.dynamic_index_in_dim(blocks, index, 0, keepdims=True)


def gather_weight(w0, x_hi, y):
    from_m3 = over_rep(w0, y_shift(3))
    from_p3 = over_rep(w0, y_shift(-3))
    three = jnp.concatenate([w0, from_p3, from_m3])
    from_m1 = over_rep(three, y_shift(1))
    from_p1 = over_rep(jnp.concatenate([w0, from_m3]), y_shift(-1))
    other_three = over_rep(three, X_SWAP)
    five = jnp.concatenate([from_m1, from_p1])
    other_five = over_rep(five, X_SWAP)
    whole = jnp.zeros((16,) + w0.shape[1:], w0.dtype)
    for half, low, high in ((x_hi, three, five), (1 - x_hi, other_three, other_five)):
        for source, steps in ((low, (0, 3, -3)), (high, (-1, 2, 4, 1, -2))):
            for slot, step in enumerate(steps):
                place = half * NY + lax.rem(y + step + NY, NY)
                whole = lax.dynamic_update_slice(
                    whole, source[slot : slot + 1], (place, 0, 0)
                )
    return whole.reshape(-1, w0.shape[2])


def scatter_wgrad(normed, masked, factor, x_hi, y, keep_rows):
    half = normed.shape[1] // 2
    left, right = normed[:, :half], normed[:, half:]
    first = x_hi == 0

    def product(columns):
        value = lax.dot_general(
            columns, masked, (((0,), (0,)), ((), ())), preferred_element_type=F32
        )
        return (value * factor).astype(BF16).reshape(NY, keep_rows, -1)

    sent = product(jnp.where(first, right, left))
    came = over_rep(sent, X_SWAP)
    mine = product(jnp.where(first, left, right))
    both = add(mine, came)

    def block(step):
        return pick(both, lax.rem(y + step + NY, NY))

    up1 = over_rep(jnp.concatenate([block(1), block(4), block(-2)]), y_shift(1))
    down1 = over_rep(jnp.concatenate([block(-1), block(2)]), y_shift(-1))
    plus3 = over_rep(add(block(3), up1[1:2], down1[1:2]), y_shift(3))
    minus3 = over_rep(add(block(-3), up1[2:3]), y_shift(-3))
    return add(block(0), up1[0:1], down1[0:1], plus3, minus3)


def body(normed, up_weight, cotangent, lengths):
    row_count, width = normed.shape
    pair_count = lengths.shape[0]
    pair_len = row_count // pair_count
    keep_rows, unit_count = up_weight.shape[1:]
    rep = lax.axis_index("rep")
    x_hi, y = rep // NY, lax.rem(rep, NY)
    row = lax.axis_index("row")
    z = lax.axis_index("col")

    weight = gather_weight(up_weight, x_hi, y)

    positions = lax.broadcasted_iota(jnp.int32, (pair_count, pair_len), 1)
    valid_rows = (positions < lengths[:, None]).reshape(row_count, 1)
    masked = jnp.where(valid_rows, cotangent, jnp.zeros_like(cotangent))

    factor = 1.0 / math.sqrt(row_count * lax.axis_size("rep"))
    weight_grad = scatter_wgrad(normed, masked, factor, x_hi, y, keep_rows)

    unit_rows = -(-row_count // (NZ * 16)) * 16
    padded = jnp.pad(masked, ((0, NZ * unit_rows - row_count), (0, 0)))
    grid = padded.reshape(NZ // 3, 3, unit_rows, unit_count)

    def partial_grad(step):
        tokens = lax.dynamic_index_in_dim(grid, lax.rem(z + step + NZ, 3), 1, keepdims=False)
        value = lax.dot_general(
            tokens.reshape(-1, unit_count),
            weight,
            (((1,), (1,)), ((), ())),
            preferred_element_type=F32,
        )
        return value.astype(BF16).reshape(NZ // 3, unit_rows, width)

    up1 = over_col(partial_grad(1), 1)
    down1 = over_col(partial_grad(-1), -1)
    four = add(partial_grad(0), up1, down1)
    q = z // 3

    def unit(step):
        return pick(four, lax.rem(q + step + 4, 4))

    plus3 = over_col(unit(1), 3)
    minus3 = over_col(unit(-1), -3)
    plus6 = over_col(unit(2), 6)
    own = add(unit(0), plus3, minus3, plus6)
    got = jnp.zeros((NZ // 3, unit_rows, width), BF16)
    for step, value in (
        (0, own),
        (-1, over_col(own, 3)),
        (1, over_col(own, -3)),
        (2, over_col(own, 6)),
    ):
        got = lax.dynamic_update_slice(got, value, (lax.rem(q + step + 4, 4), 0, 0))
    result = jnp.zeros((NZ // 3, 3, unit_rows, width), BF16)
    for step, value in ((0, got), (-1, over_col(got, 1)), (1, over_col(got, -1))):
        result = lax.dynamic_update_slice(
            result, value[:, None], (0, lax.rem(z + step + NZ, 3), 0, 0)
        )
    normed_grad = result.reshape(NZ * unit_rows, width)[:row_count]

    parts = normed.reshape(4, row_count // 4, width)
    parts = jnp.where(row // 2 == 0, parts, jnp.concatenate([parts[2:], parts[:2]]))
    even = jnp.concatenate([parts[0:1], parts[2:3]])
    odd = jnp.concatenate([parts[1:2], parts[3:4]])
    core = lax.rem(row, 2)

    def partial_up(tokens):
        value = jnp.dot(tokens.reshape(-1, width), weight, preferred_element_type=F32)
        return value.astype(BF16).reshape(2, row_count // 4, unit_count)

    came = lax.ppermute(
        partial_up(jnp.where(core == 0, odd, even)), "row", [(r, r ^ 1) for r in range(4)]
    )
    two = add(partial_up(jnp.where(core == 0, even, odd)), came)
    came = lax.ppermute(two[1], "row", [(r, r ^ 2) for r in range(4)])
    up_out = add(two[0], came)
    return (up_out, normed_grad, weight_grad)


def solution(mesh):
    placed = (P("rep", "row"), P("row", "rep", "col"), P("rep", "col"), P("rep"))
    return jax.shard_map(
        body,
        mesh=mesh,
        in_specs=placed,
        out_specs=(P(("rep", "row"), "col"), P("rep", "row"), P("row", "rep", "col")),
        check_vma=False,
    )
```

time: 484 us -> 194 us (0.40)
  waiting for transfers between devices: 444 us -> 54.5 us
  starting transfers between devices: 0.16 us -> 100 us
  between operations: 14.4 us -> 2.03 us
  other arithmetic: 0.01 us -> 10.9 us
    unnamed x5 -> x0, waiting for transfers between devices: 196 us -> none
    psum x1 -> x0, waiting for transfers between devices: 118 us -> none  [body(): normed_grad = lax.psum(grad_partial.astype(jnp.bfloat16), 'col')]
    ppermute x0 -> x23, starting transfers between devices: none -> 100 us  [the longest x10 51.9 us: over_col(): return lax.ppermute(value, 'col', z_shift(step))]
    all_gather x1 -> x0, waiting for transfers between devices: 100 us -> none  [body(): lax.all_gather(up_weight, 'rep', axis=1, tiled=True)[0]]
    ppermute x0 -> x23, waiting for transfers between devices: none -> 54.5 us  [the longest x10 30.4 us: over_col(): return lax.ppermute(value, 'col', z_shift(step))]
    reduce_scatter x1 -> x0, waiting for transfers between devices: 29.4 us -> none  [body(): lax.psum_scatter(up_partial.astype(jnp.bfloat16), 'row', scatter_dimensio...]
    unnamed x8 -> x30, local copies, waits for them, and re-layouts: 9.91 us -> 1.47 us
    dot_general x3 -> x7, matrix products: 14.3 us -> 11.9 us  [the longest x2 6.66 us: product(): lax.dot_general(columns, masked, (((0,), (0,)), ((), ())), preferred_elem...]
  transfers between devices with their start and end apart: 4 -> 23, of which waited for: 4 -> 10; matrix products, arithmetic and copies ran while one was open for 5% -> 17% of each run, Pallas kernels for 0% -> 0%
where the time goes in v1:
time: 194 us; the launch traced here: 191 us
  starting transfers between devices  100 us (52%)
  waiting for transfers between devices  54.5 us (28%)
  matrix products  11.9 us (6%)
  other arithmetic  10.9 us (6%)
  local copies, waits for them, and re-layouts  10.9 us (6%)
  between operations  2.03 us (1%)
    ppermute x10, starting transfers between devices, over_col(): return lax.ppermute(value, 'col', z_shift(step))  51.9 us
    ppermute x11, starting transfers between devices, over_rep(): return lax.ppermute(value, 'rep', pairs)  43.8 us
    ppermute x10, waiting for transfers between devices, over_col(): return lax.ppermute(value, 'col', z_shift(step))  30.4 us
    ppermute x11, waiting for transfers between devices, over_rep(): return lax.ppermute(value, 'rep', pairs)  24 us
    dot_general x2, matrix products, product(): lax.dot_general(columns, masked, (((0,), (0,)), ((), ())), preferred_elem...  6.66 us
  transfers between devices with their start and end apart: 23, of which 10 were waited for; matrix products, arithmetic and copies ran while one was open for 17% of the time, Pallas kernels for 0%

profile of v1, /device:TPU:6, one launch (start us, length us, event | category | flops | bytes accessed | tf_op | source)
XLA Modules:
  0.0 190.6 jit_solution(18333746767484037013)
XLA Ops:
  0.6 7.0 %collective-permute-start = (bf16[1,80,1152]{2,1,0:T(8,128)(2,1)}, bf16[1,80,1152]{2,1,0:T(8,128)(2,1)S(1)}, u32[]{:S(2)}, u32[]{:S(2)}) collective-permute-start(bf16[1,80,1152]{2,1,0:T(8,128)(2,1)} %param.5), channel_id=1, source_target_pairs={{0,240},{48,288},{96,336},{144,0},{192,48},{240,96},{288,144},{336... | collective-permute-start | bytes 552968 | tf_op jit(solution)/shard_map/ppermute | solution.py:25
  7.6 1.9 %collective-permute-start.1 = (bf16[1,80,1152]{2,1,0:T(8,128)(2,1)}, bf16[1,80,1152]{2,1,0:T(8,128)(2,1)S(1)}, u32[]{:S(2)}, u32[]{:S(2)}) collective-permute-start(bf16[1,80,1152]{2,1,0:T(8,128)(2,1)} %param.5), channel_id=1, source_target_pairs={{0,144},{48,192},{96,240},{144,288},{192,336},{240,0},{288,48},{33... | collective-permute-start | bytes 552968 | tf_op jit(solution)/shard_map/ppermute | solution.py:25
  11.7 3.9 %fusion.1 = bf16[640,1152]{1,0:T(8,128)(2,1)} fusion(bf16[512,1152]{1,0:T(8,128)(2,1)S(1)} %broadcast_select_fusion, pred[]{:T(512)S(6)} %eq.12, bf16[512,1280]{1,0:T(8,128)(2,1)} %param.4), kind=kOutput, calls=%fused_computation.3 | convolution fusion | flops 756776960 | bytes 3964929 | tf_op jit(solution)/shard_map/dot_general | solution.py:69
  15.6 3.3 %collective-permute-start.18 = (bf16[8,80,1152]{2,1,0:T(8,128)(2,1)}, bf16[8,80,1152]{2,1,0:T(8,128)(2,1)}, u32[]{:S(2)}, u32[]{:S(2)}) collective-permute-start(bf16[8,80,1152]{2,1,0:T(8,128)(2,1)} %bitcast.25), channel_id=1, source_target_pairs={{0,384},{48,432},{96,480},{144,528},{192,576},{240,624},{288,672},... | collective-permute-start | bytes 4423688 | tf_op jit(solution)/shard_map/ppermute | solution.py:25
  27.7 3.5 %collective-permute-start.2 = (bf16[3,80,1152]{2,1,0:T(8,128)(2,1)}, bf16[3,80,1152]{2,1,0:T(8,128)(2,1)S(1)}, u32[]{:S(2)}, u32[]{:S(2)}) collective-permute-start(bf16[3,80,1152]{2,1,0:T(8,128)(2,1)} %get-tuple-element.26), channel_id=1, source_target_pairs={{0,48},{48,96},{96,144},{144,192},{192,240},{240,288},{288,336},{3... | collective-permute-start | bytes 1658888 | tf_op jit(solution)/shard_map/ppermute | solution.py:25
  32.9 3.8 %collective-permute-start.3 = (bf16[2,80,1152]{2,1,0:T(8,128)(2,1)}, bf16[2,80,1152]{2,1,0:T(8,128)(2,1)}, u32[]{:S(2)}, u32[]{:S(2)}) collective-permute-start(bf16[2,80,1152]{2,1,0:T(8,128)(2,1)} %pad_maximum_fusion.4), channel_id=1, source_target_pairs={{0,336},{48,0},{96,48},{144,96},{192,144},{240,192},{288,240},{336... | collective-permute-start | bytes 1105928 | tf_op jit(solution)/shard_map/ppermute | solution.py:25
  37.9 2.7 %fusion = bf16[640,1152]{1,0:T(8,128)(2,1)S(1)} fusion(bf16[512,1152]{1,0:T(8,128)(2,1)} %copy-done.1, pred[]{:T(512)S(6)} %eq.12, bf16[512,1280]{1,0:T(8,128)(2,1)} %param.4), kind=kOutput, calls=%fused_computation.2 | convolution fusion | flops 756776960 | bytes 3964929 | tf_op jit(solution)/shard_map/dot_general | solution.py:69
  40.6 4.0 %collective-permute-start.4 = (bf16[3,80,1152]{2,1,0:T(8,128)(2,1)}, bf16[3,80,1152]{2,1,0:T(8,128)(2,1)S(1)}, u32[]{:S(2)}, u32[]{:S(2)}) collective-permute-start(bf16[3,80,1152]{2,1,0:T(8,128)(2,1)} %get-tuple-element.26), channel_id=1, source_target_pairs={{0,384},{48,432},{96,480},{144,528},{192,576},{240,624},{288,672},... | collective-permute-start | bytes 1658888 | tf_op jit(solution)/shard_map/ppermute | solution.py:25
  46.0 4.0 %collective-permute-start.5 = (bf16[5,80,1152]{2,1,0:T(8,128)(2,1)S(1)}, bf16[5,80,1152]{2,1,0:T(8,128)(2,1)S(1)}, u32[]{:S(2)}, u32[]{:S(2)}) collective-permute-start(bf16[5,80,1152]{2,1,0:T(8,128)(2,1)S(1)} %pad_maximum_fusion), channel_id=1, source_target_pairs={{0,384},{48,432},{96,480},{144,528},{192,576},{240,624},{288,672},... | collective-permute-start | bytes 2764808 | tf_op jit(solution)/shard_map/ppermute | solution.py:25
  52.1 14.2 %collective-permute-done.4 = bf16[3,80,1152]{2,1,0:T(8,128)(2,1)S(1)} collective-permute-done((bf16[3,80,1152]{2,1,0:T(8,128)(2,1)}, bf16[3,80,1152]{2,1,0:T(8,128)(2,1)S(1)}, u32[]{:S(2)}, u32[]{:S(2)}) %collective-permute-start.4) | collective-permute-done | bytes 552992 | tf_op jit(solution)/shard_map/ppermute | solution.py:25
  66.4 1.8 fusion.2
  68.4 3.5 %collective-permute-start.19 = (bf16[3,80,1152]{2,1,0:T(8,128)(2,1)S(1)}, bf16[3,80,1152]{2,1,0:T(8,128)(2,1)S(1)}, u32[]{:S(2)}, u32[]{:S(2)}) collective-permute-start(bf16[3,80,1152]{2,1,0:T(8,128)(2,1)S(1)} %pad_maximum_fusion.3), channel_id=1, source_target_pairs={{0,48},{48,96},{96,144},{144,192},{192,240},{240,288},{288,336},{3... | collective-permute-start | bytes 1658888 | tf_op jit(solution)/shard_map/ppermute | solution.py:25
  71.9 4.0 %collective-permute-start.20 = (bf16[2,80,1152]{2,1,0:T(8,128)(2,1)S(1)}, bf16[2,80,1152]{2,1,0:T(8,128)(2,1)S(1)}, u32[]{:S(2)}, u32[]{:S(2)}) collective-permute-start(bf16[2,80,1152]{2,1,0:T(8,128)(2,1)S(1)} %pad_maximum_fusion.5), channel_id=1, source_target_pairs={{0,336},{48,0},{96,48},{144,96},{192,144},{240,192},{288,240},{336... | collective-permute-start | bytes 1105928 | tf_op jit(solution)/shard_map/ppermute | solution.py:25
  75.9 8.7 %collective-permute-done.5 = bf16[5,80,1152]{2,1,0:T(8,128)(2,1)S(1)} collective-permute-done((bf16[5,80,1152]{2,1,0:T(8,128)(2,1)S(1)}, bf16[5,80,1152]{2,1,0:T(8,128)(2,1)S(1)}, u32[]{:S(2)}, u32[]{:S(2)}) %collective-permute-start.5) | collective-permute-done | bytes 921632 | tf_op jit(solution)/shard_map/ppermute | solution.py:25
  85.8 4.3 %collective-permute-start.8 = (bf16[4,48,1280]{2,1,0:T(8,128)(2,1)S(1)}, bf16[4,48,1280]{2,1,0:T(8,128)(2,1)S(1)}, u32[]{:S(2)}, u32[]{:S(2)}) collective-permute-start(bf16[4,48,1280]{2,1,0:T(8,128)(2,1)S(1)} %bitcast.70), channel_id=1, source_target_pairs={{0,1},{1,2},{2,3},{3,4},{4,5},{5,6},{6,7},{7,8},{8,9},{9,10},{10,1... | collective-permute-start | bytes 1474568 | tf_op jit(solution)/shard_map/ppermute | solution.py:29
  91.2 12.4 %collective-permute-start.9 = (bf16[4,48,1280]{2,1,0:T(8,128)(2,1)S(1)}, bf16[4,48,1280]{2,1,0:T(8,128)(2,1)S(1)}, u32[]{:S(2)}, u32[]{:S(2)}) collective-permute-start(bf16[4,48,1280]{2,1,0:T(8,128)(2,1)S(1)} %bitcast.71), channel_id=1, source_target_pairs={{0,11},{1,0},{2,1},{3,2},{4,3},{5,4},{6,5},{7,6},{8,7},{9,8},{10,9... | collective-permute-start | bytes 1474568 | tf_op jit(solution)/shard_map/ppermute | solution.py:29
  105.7 1.9 %collective-permute-start.6 = (bf16[2,128,1152]{2,1,0:T(8,128)(2,1)S(1)}, bf16[2,128,1152]{2,1,0:T(8,128)(2,1)S(1)}, u32[]{:S(2)}, u32[]{:S(2)}) collective-permute-start(bf16[2,128,1152]{2,1,0:T(8,128)(2,1)S(1)} %bitcast.72), channel_id=1, source_target_pairs={{0,12},{12,0},{24,36},{36,24},{1,13},{13,1},{25,37},{37,25},{2,14}... | collective-permute-start | bytes 1769480 | tf_op jit(solution)/shard_map/ppermute | solution.py:159
  108.9 5.2 %collective-permute-start.21 = (bf16[1,80,1152]{2,1,0:T(8,128)(2,1)S(1)}, bf16[1,80,1152]{2,1,0:T(8,128)(2,1)S(1)}, u32[]{:S(2)}, u32[]{:S(2)}) collective-permute-start(bf16[1,80,1152]{2,1,0:T(8,128)(2,1)S(1)} %get-tuple-element.5), channel_id=1, source_target_pairs={{0,144},{48,192},{96,240},{144,288},{192,336},{240,0},{288,48},{33... | collective-permute-start | bytes 552968 | tf_op jit(solution)/shard_map/ppermute | solution.py:25
  114.1 3.6 %collective-permute-start.22 = (bf16[1,80,1152]{2,1,0:T(8,128)(2,1)S(1)}, bf16[1,80,1152]{2,1,0:T(8,128)(2,1)S(1)}, u32[]{:S(2)}, u32[]{:S(2)}) collective-permute-start(bf16[1,80,1152]{2,1,0:T(8,128)(2,1)S(1)} %get-tuple-element.6), channel_id=1, source_target_pairs={{0,240},{48,288},{96,336},{144,0},{192,48},{240,96},{288,144},{336... | collective-permute-start | bytes 552968 | tf_op jit(solution)/shard_map/ppermute | solution.py:25
  118.0 1.9 %collective-permute-start.10 = (bf16[1,48,1280]{2,1,0:T(8,128)(2,1)S(1)}, bf16[1,48,1280]{2,1,0:T(8,128)(2,1)S(1)}, u32[]{:S(2)}, u32[]{:S(2)}) collective-permute-start(bf16[1,48,1280]{2,1,0:T(8,128)(2,1)S(1)} %get-tuple-element.23), channel_id=1, source_target_pairs={{0,3},{1,4},{2,5},{3,6},{4,7},{5,8},{6,9},{7,10},{8,11},{9,0},{10,... | collective-permute-start | bytes 368648 | tf_op jit(solution)/shard_map/ppermute | solution.py:29
  119.9 6.9 %collective-permute-start.11 = (bf16[1,48,1280]{2,1,0:T(8,128)(2,1)S(1)}, bf16[1,48,1280]{2,1,0:T(8,128)(2,1)S(1)}, u32[]{:S(2)}, u32[]{:S(2)}) collective-permute-start(bf16[1,48,1280]{2,1,0:T(8,128)(2,1)S(1)} %get-tuple-element.25), channel_id=1, source_target_pairs={{0,9},{1,10},{2,11},{3,0},{4,1},{5,2},{6,3},{7,4},{8,5},{9,6},{10,... | collective-permute-start | bytes 368648 | tf_op jit(solution)/shard_map/ppermute | solution.py:29
  127.7 4.5 %collective-permute-start.12 = (bf16[1,48,1280]{2,1,0:T(8,128)(2,1)S(1)}, bf16[1,48,1280]{2,1,0:T(8,128)(2,1)S(1)}, u32[]{:S(2)}, u32[]{:S(2)}) collective-permute-start(bf16[1,48,1280]{2,1,0:T(8,128)(2,1)S(1)} %get-tuple-element.24), channel_id=1, source_target_pairs={{0,6},{1,7},{2,8},{3,9},{4,10},{5,11},{6,0},{7,1},{8,2},{9,3},{10,... | collective-permute-start | bytes 368648 | tf_op jit(solution)/shard_map/ppermute | solution.py:29
  133.4 11.3 %collective-permute-done.12 = bf16[1,48,1280]{2,1,0:T(8,128)(2,1)S(1)} collective-permute-done((bf16[1,48,1280]{2,1,0:T(8,128)(2,1)S(1)}, bf16[1,48,1280]{2,1,0:T(8,128)(2,1)S(1)}, u32[]{:S(2)}, u32[]{:S(2)}) %collective-permute-start.12) | collective-permute-done | bytes 122912 | tf_op jit(solution)/shard_map/ppermute | solution.py:29
  144.9 5.9 %collective-permute-start.13 = (bf16[1,48,1280]{2,1,0:T(8,128)(2,1)S(1)}, bf16[1,48,1280]{2,1,0:T(8,128)(2,1)S(1)}, u32[]{:S(2)}, u32[]{:S(2)}) collective-permute-start(bf16[1,48,1280]{2,1,0:T(8,128)(2,1)S(1)} %get-tuple-element.4), channel_id=1, source_target_pairs={{0,3},{1,4},{2,5},{3,6},{4,7},{5,8},{6,9},{7,10},{8,11},{9,0},{10,... | collective-permute-start | bytes 368648 | tf_op jit(solution)/shard_map/ppermute | solution.py:29
  150.8 2.7 %collective-permute-start.7 = (bf16[128,1152]{1,0:T(8,128)(2,1)S(1)}, bf16[128,1152]{1,0:T(8,128)(2,1)S(1)}, u32[]{:S(2)}, u32[]{:S(2)}) collective-permute-start(bf16[128,1152]{1,0:T(8,128)(2,1)S(1)} %slice_bitcast_fusion), channel_id=1, source_target_pairs={{0,24},{12,36},{24,0},{36,12},{1,25},{13,37},{25,1},{37,13},{2,26}... | collective-permute-start | bytes 884744 | tf_op jit(solution)/shard_map/ppermute | solution.py:163
  153.5 3.4 %collective-permute-start.14 = (bf16[1,48,1280]{2,1,0:T(8,128)(2,1)S(1)}, bf16[1,48,1280]{2,1,0:T(8,128)(2,1)S(1)}, u32[]{:S(2)}, u32[]{:S(2)}) collective-permute-start(bf16[1,48,1280]{2,1,0:T(8,128)(2,1)S(1)} %get-tuple-element.4), channel_id=1, source_target_pairs={{0,9},{1,10},{2,11},{3,0},{4,1},{5,2},{6,3},{7,4},{8,5},{9,6},{10,... | collective-permute-start | bytes 368648 | tf_op jit(solution)/shard_map/ppermute | solution.py:29
  157.0 5.5 %collective-permute-start.15 = (bf16[1,48,1280]{2,1,0:T(8,128)(2,1)S(1)}, bf16[1,48,1280]{2,1,0:T(8,128)(2,1)S(1)}, u32[]{:S(2)}, u32[]{:S(2)}) collective-permute-start(bf16[1,48,1280]{2,1,0:T(8,128)(2,1)S(1)} %get-tuple-element.4), channel_id=1, source_target_pairs={{0,6},{1,7},{2,8},{3,9},{4,10},{5,11},{6,0},{7,1},{8,2},{9,3},{10,... | collective-permute-start | bytes 368648 | tf_op jit(solution)/shard_map/ppermute | solution.py:29
  162.5 2.5 %collective-permute-done.14 = bf16[1,48,1280]{2,1,0:T(8,128)(2,1)S(1)} collective-permute-done((bf16[1,48,1280]{2,1,0:T(8,128)(2,1)S(1)}, bf16[1,48,1280]{2,1,0:T(8,128)(2,1)S(1)}, u32[]{:S(2)}, u32[]{:S(2)}) %collective-permute-start.14) | collective-permute-done | bytes 122912 | tf_op jit(solution)/shard_map/ppermute | solution.py:29
  165.0 7.8 %collective-permute-done.15 = bf16[1,48,1280]{2,1,0:T(8,128)(2,1)S(1)} collective-permute-done((bf16[1,48,1280]{2,1,0:T(8,128)(2,1)S(1)}, bf16[1,48,1280]{2,1,0:T(8,128)(2,1)S(1)}, u32[]{:S(2)}, u32[]{:S(2)}) %collective-permute-start.15) | collective-permute-done | bytes 122912 | tf_op jit(solution)/shard_map/ppermute | solution.py:29
  172.8 1.9 %collective-permute-start.16 = (bf16[4,48,1280]{2,1,0:T(8,128)(2,1)S(1)}, bf16[4,48,1280]{2,1,0:T(8,128)(2,1)S(1)}, u32[]{:S(2)}, u32[]{:S(2)}) collective-permute-start(bf16[4,48,1280]{2,1,0:T(8,128)(2,1)S(1)} %constant_dynamic-update-slice_fusion), channel_id=1, source_target_pairs={{0,1},{1,2},{2,3},{3,4},{4,5},{5,6},{6,7},{7,8},{8,9},{9,10},{10,1... | collective-permute-start | bytes 1474568 | tf_op jit(solution)/shard_map/ppermute | solution.py:29
  174.8 5.1 %collective-permute-start.17 = (bf16[4,48,1280]{2,1,0:T(8,128)(2,1)S(1)}, bf16[4,48,1280]{2,1,0:T(8,128)(2,1)S(1)}, u32[]{:S(2)}, u32[]{:S(2)}) collective-permute-start(bf16[4,48,1280]{2,1,0:T(8,128)(2,1)S(1)} %constant_dynamic-update-slice_fusion), channel_id=1, source_target_pairs={{0,11},{1,0},{2,1},{3,2},{4,3},{5,4},{6,5},{7,6},{8,7},{9,8},{10,9... | collective-permute-start | bytes 1474568 | tf_op jit(solution)/shard_map/ppermute | solution.py:29
  180.8 7.4 %collective-permute-done.16 = bf16[4,48,1280]{2,1,0:T(8,128)(2,1)S(1)} collective-permute-done((bf16[4,48,1280]{2,1,0:T(8,128)(2,1)S(1)}, bf16[4,48,1280]{2,1,0:T(8,128)(2,1)S(1)}, u32[]{:S(2)}, u32[]{:S(2)}) %collective-permute-start.16) | collective-permute-done | bytes 491552 | tf_op jit(solution)/shard_map/ppermute | solution.py:29
  (97 shorter events, 27.9 us)
Async XLA Ops:
  0.6 25.6 %collective-permute-start = (bf16[1,80,1152]{2,1,0:T(8,128)(2,1)}, bf16[1,80,1152]{2,1,0:T(8,128)(2,1)S(1)}, u32[]{:S(2)}, u32[]{:S(2)}) collective-permute-start(bf16[1,80,1152]{2,1,0:T(8,128)(2,1)} %param.5), channel_id=1, source_target_pairs={{0,240},{48,288},{96,336},{144,0},{192,48},{240,96},{288,144},{336... | collective-permute-start | bytes 552968 | tf_op jit(solution)/shard_map/ppermute | solution.py:25
  7.6 19.4 %collective-permute-start.1 = (bf16[1,80,1152]{2,1,0:T(8,128)(2,1)}, bf16[1,80,1152]{2,1,0:T(8,128)(2,1)S(1)}, u32[]{:S(2)}, u32[]{:S(2)}) collective-permute-start(bf16[1,80,1152]{2,1,0:T(8,128)(2,1)} %param.5), channel_id=1, source_target_pairs={{0,144},{48,192},{96,240},{144,288},{192,336},{240,0},{288,48},{33... | collective-permute-start | bytes 552968 | tf_op jit(solution)/shard_map/ppermute | solution.py:25
  11.7 7.4 %copy-start = (bf16[512,1280]{1,0:T(8,128)(2,1)S(1)}, bf16[512,1280]{1,0:T(8,128)(2,1)}, u32[]{:S(2)}) copy-start(bf16[512,1280]{1,0:T(8,128)(2,1)} %param.4) | copy-start | bytes 3932164
  15.6 50.8 %collective-permute-start.18 = (bf16[8,80,1152]{2,1,0:T(8,128)(2,1)}, bf16[8,80,1152]{2,1,0:T(8,128)(2,1)}, u32[]{:S(2)}, u32[]{:S(2)}) collective-permute-start(bf16[8,80,1152]{2,1,0:T(8,128)(2,1)} %bitcast.25), channel_id=1, source_target_pairs={{0,384},{48,432},{96,480},{144,528},{192,576},{240,624},{288,672},... | collective-permute-start | bytes 4423688 | tf_op jit(solution)/shard_map/ppermute | solution.py:25
  25.3 11.4 %copy-start.5 = (bf16[1,128,1280]{2,1,0:T(8,128)(2,1)S(1)}, bf16[1,128,1280]{2,1,0:T(8,128)(2,1)}, u32[]{:S(2)}) copy-start(bf16[1,128,1280]{2,1,0:T(8,128)(2,1)} %get-tuple-element.17) | copy-start | bytes 983044
  25.3 11.4 %copy-start.6 = (bf16[1,128,1280]{2,1,0:T(8,128)(2,1)S(1)}, bf16[1,128,1280]{2,1,0:T(8,128)(2,1)}, u32[]{:S(2)}) copy-start(bf16[1,128,1280]{2,1,0:T(8,128)(2,1)} %get-tuple-element.18) | copy-start | bytes 983044
  25.3 11.4 %copy-start.7 = (bf16[1,128,1280]{2,1,0:T(8,128)(2,1)S(1)}, bf16[1,128,1280]{2,1,0:T(8,128)(2,1)}, u32[]{:S(2)}) copy-start(bf16[1,128,1280]{2,1,0:T(8,128)(2,1)} %get-tuple-element.19) | copy-start | bytes 983044
  25.3 11.4 %copy-start.8 = (bf16[1,128,1280]{2,1,0:T(8,128)(2,1)S(1)}, bf16[1,128,1280]{2,1,0:T(8,128)(2,1)}, u32[]{:S(2)}) copy-start(bf16[1,128,1280]{2,1,0:T(8,128)(2,1)} %get-tuple-element.20) | copy-start | bytes 983044
  27.7 17.2 %collective-permute-start.2 = (bf16[3,80,1152]{2,1,0:T(8,128)(2,1)}, bf16[3,80,1152]{2,1,0:T(8,128)(2,1)S(1)}, u32[]{:S(2)}, u32[]{:S(2)}) collective-permute-start(bf16[3,80,1152]{2,1,0:T(8,128)(2,1)} %get-tuple-element.26), channel_id=1, source_target_pairs={{0,48},{48,96},{96,144},{144,192},{192,240},{240,288},{288,336},{3... | collective-permute-start | bytes 1658888 | tf_op jit(solution)/shard_map/ppermute | solution.py:25
  32.9 11.8 %collective-permute-start.3 = (bf16[2,80,1152]{2,1,0:T(8,128)(2,1)}, bf16[2,80,1152]{2,1,0:T(8,128)(2,1)}, u32[]{:S(2)}, u32[]{:S(2)}) collective-permute-start(bf16[2,80,1152]{2,1,0:T(8,128)(2,1)} %pad_maximum_fusion.4), channel_id=1, source_target_pairs={{0,336},{48,0},{96,48},{144,96},{192,144},{240,192},{288,240},{336... | collective-permute-start | bytes 1105928 | tf_op jit(solution)/shard_map/ppermute | solution.py:25
  40.6 25.7 %collective-permute-start.4 = (bf16[3,80,1152]{2,1,0:T(8,128)(2,1)}, bf16[3,80,1152]{2,1,0:T(8,128)(2,1)S(1)}, u32[]{:S(2)}, u32[]{:S(2)}) collective-permute-start(bf16[3,80,1152]{2,1,0:T(8,128)(2,1)} %get-tuple-element.26), channel_id=1, source_target_pairs={{0,384},{48,432},{96,480},{144,528},{192,576},{240,624},{288,672},... | collective-permute-start | bytes 1658888 | tf_op jit(solution)/shard_map/ppermute | solution.py:25
  46.0 38.6 %collective-permute-start.5 = (bf16[5,80,1152]{2,1,0:T(8,128)(2,1)S(1)}, bf16[5,80,1152]{2,1,0:T(8,128)(2,1)S(1)}, u32[]{:S(2)}, u32[]{:S(2)}) collective-permute-start(bf16[5,80,1152]{2,1,0:T(8,128)(2,1)S(1)} %pad_maximum_fusion), channel_id=1, source_target_pairs={{0,384},{48,432},{96,480},{144,528},{192,576},{240,624},{288,672},... | collective-permute-start | bytes 2764808 | tf_op jit(solution)/shard_map/ppermute | solution.py:25
  68.2 16.6 %copy-start.4 = (bf16[4,1,48,1152]{3,2,1,0:T(8,128)(2,1)S(1)}, bf16[4,1,48,1152]{3,2,1,0:T(8,128)(2,1)}, u32[]{:S(2)}) copy-start(bf16[4,1,48,1152]{3,2,1,0:T(8,128)(2,1)} %get-tuple-element.12) | copy-start | bytes 1327108
  68.4 40.4 %collective-permute-start.19 = (bf16[3,80,1152]{2,1,0:T(8,128)(2,1)S(1)}, bf16[3,80,1152]{2,1,0:T(8,128)(2,1)S(1)}, u32[]{:S(2)}, u32[]{:S(2)}) collective-permute-start(bf16[3,80,1152]{2,1,0:T(8,128)(2,1)S(1)} %pad_maximum_fusion.3), channel_id=1, source_target_pairs={{0,48},{48,96},{96,144},{144,192},{192,240},{240,288},{288,336},{3... | collective-permute-start | bytes 1658888 | tf_op jit(solution)/shard_map/ppermute | solution.py:25
  71.9 18.2 %copy-start.3 = (bf16[4,1,48,1152]{3,2,1,0:T(8,128)(2,1)S(1)}, bf16[4,1,48,1152]{3,2,1,0:T(8,128)(2,1)}, u32[]{:S(2)}) copy-start(bf16[4,1,48,1152]{3,2,1,0:T(8,128)(2,1)} %get-tuple-element.13) | copy-start | bytes 1327108
  71.9 36.8 %collective-permute-start.20 = (bf16[2,80,1152]{2,1,0:T(8,128)(2,1)S(1)}, bf16[2,80,1152]{2,1,0:T(8,128)(2,1)S(1)}, u32[]{:S(2)}, u32[]{:S(2)}) collective-permute-start(bf16[2,80,1152]{2,1,0:T(8,128)(2,1)S(1)} %pad_maximum_fusion.5), channel_id=1, source_target_pairs={{0,336},{48,0},{96,48},{144,96},{192,144},{240,192},{288,240},{336... | collective-permute-start | bytes 1105928 | tf_op jit(solution)/shard_map/ppermute | solution.py:25
  84.8 18.8 %copy-start.13 = (bf16[2,128,1280]{2,1,0:T(8,128)(2,1)S(1)}, bf16[2,128,1280]{2,1,0:T(8,128)(2,1)}, u32[]{:S(2)}) copy-start(bf16[2,128,1280]{2,1,0:T(8,128)(2,1)} %get-tuple-element.15) | copy-start | bytes 1966084
  85.8 31.9 %collective-permute-start.8 = (bf16[4,48,1280]{2,1,0:T(8,128)(2,1)S(1)}, bf16[4,48,1280]{2,1,0:T(8,128)(2,1)S(1)}, u32[]{:S(2)}, u32[]{:S(2)}) collective-permute-start(bf16[4,48,1280]{2,1,0:T(8,128)(2,1)S(1)} %bitcast.70), channel_id=1, source_target_pairs={{0,1},{1,2},{2,3},{3,4},{4,5},{5,6},{6,7},{7,8},{8,9},{9,10},{10,1... | collective-permute-start | bytes 1474568 | tf_op jit(solution)/shard_map/ppermute | solution.py:29
  91.2 13.5 %copy-start.2 = (bf16[4,1,48,1152]{3,2,1,0:T(8,128)(2,1)S(1)}, bf16[4,1,48,1152]{3,2,1,0:T(8,128)(2,1)}, u32[]{:S(2)}) copy-start(bf16[4,1,48,1152]{3,2,1,0:T(8,128)(2,1)} %get-tuple-element.14) | copy-start | bytes 1327108
  91.2 26.6 %collective-permute-start.9 = (bf16[4,48,1280]{2,1,0:T(8,128)(2,1)S(1)}, bf16[4,48,1280]{2,1,0:T(8,128)(2,1)S(1)}, u32[]{:S(2)}, u32[]{:S(2)}) collective-permute-start(bf16[4,48,1280]{2,1,0:T(8,128)(2,1)S(1)} %bitcast.71), channel_id=1, source_target_pairs={{0,11},{1,0},{2,1},{3,2},{4,3},{5,4},{6,5},{7,6},{8,7},{9,8},{10,9... | collective-permute-start | bytes 1474568 | tf_op jit(solution)/shard_map/ppermute | solution.py:29
  105.7 27.3 %collective-permute-start.6 = (bf16[2,128,1152]{2,1,0:T(8,128)(2,1)S(1)}, bf16[2,128,1152]{2,1,0:T(8,128)(2,1)S(1)}, u32[]{:S(2)}, u32[]{:S(2)}) collective-permute-start(bf16[2,128,1152]{2,1,0:T(8,128)(2,1)S(1)} %bitcast.72), channel_id=1, source_target_pairs={{0,12},{12,0},{24,36},{36,24},{1,13},{13,1},{25,37},{37,25},{2,14}... | collective-permute-start | bytes 1769480 | tf_op jit(solution)/shard_map/ppermute | solution.py:159
  108.9 18.8 %collective-permute-start.21 = (bf16[1,80,1152]{2,1,0:T(8,128)(2,1)S(1)}, bf16[1,80,1152]{2,1,0:T(8,128)(2,1)S(1)}, u32[]{:S(2)}, u32[]{:S(2)}) collective-permute-start(bf16[1,80,1152]{2,1,0:T(8,128)(2,1)S(1)} %get-tuple-element.5), channel_id=1, source_target_pairs={{0,144},{48,192},{96,240},{144,288},{192,336},{240,0},{288,48},{33... | collective-permute-start | bytes 552968 | tf_op jit(solution)/shard_map/ppermute | solution.py:25
  114.1 18.1 %collective-permute-start.22 = (bf16[1,80,1152]{2,1,0:T(8,128)(2,1)S(1)}, bf16[1,80,1152]{2,1,0:T(8,128)(2,1)S(1)}, u32[]{:S(2)}, u32[]{:S(2)}) collective-permute-start(bf16[1,80,1152]{2,1,0:T(8,128)(2,1)S(1)} %get-tuple-element.6), channel_id=1, source_target_pairs={{0,240},{48,288},{96,336},{144,0},{192,48},{240,96},{288,144},{336... | collective-permute-start | bytes 552968 | tf_op jit(solution)/shard_map/ppermute | solution.py:25
  118.0 15.4 %collective-permute-start.10 = (bf16[1,48,1280]{2,1,0:T(8,128)(2,1)S(1)}, bf16[1,48,1280]{2,1,0:T(8,128)(2,1)S(1)}, u32[]{:S(2)}, u32[]{:S(2)}) collective-permute-start(bf16[1,48,1280]{2,1,0:T(8,128)(2,1)S(1)} %get-tuple-element.23), channel_id=1, source_target_pairs={{0,3},{1,4},{2,5},{3,6},{4,7},{5,8},{6,9},{7,10},{8,11},{9,0},{10,... | collective-permute-start | bytes 368648 | tf_op jit(solution)/shard_map/ppermute | solution.py:29
  119.9 13.5 %collective-permute-start.11 = (bf16[1,48,1280]{2,1,0:T(8,128)(2,1)S(1)}, bf16[1,48,1280]{2,1,0:T(8,128)(2,1)S(1)}, u32[]{:S(2)}, u32[]{:S(2)}) collective-permute-start(bf16[1,48,1280]{2,1,0:T(8,128)(2,1)S(1)} %get-tuple-element.25), channel_id=1, source_target_pairs={{0,9},{1,10},{2,11},{3,0},{4,1},{5,2},{6,3},{7,4},{8,5},{9,6},{10,... | collective-permute-start | bytes 368648 | tf_op jit(solution)/shard_map/ppermute | solution.py:29
  127.7 17.1 %collective-permute-start.12 = (bf16[1,48,1280]{2,1,0:T(8,128)(2,1)S(1)}, bf16[1,48,1280]{2,1,0:T(8,128)(2,1)S(1)}, u32[]{:S(2)}, u32[]{:S(2)}) collective-permute-start(bf16[1,48,1280]{2,1,0:T(8,128)(2,1)S(1)} %get-tuple-element.24), channel_id=1, source_target_pairs={{0,6},{1,7},{2,8},{3,9},{4,10},{5,11},{6,0},{7,1},{8,2},{9,3},{10,... | collective-permute-start | bytes 368648 | tf_op jit(solution)/shard_map/ppermute | solution.py:29
  144.9 17.6 %collective-permute-start.13 = (bf16[1,48,1280]{2,1,0:T(8,128)(2,1)S(1)}, bf16[1,48,1280]{2,1,0:T(8,128)(2,1)S(1)}, u32[]{:S(2)}, u32[]{:S(2)}) collective-permute-start(bf16[1,48,1280]{2,1,0:T(8,128)(2,1)S(1)} %get-tuple-element.4), channel_id=1, source_target_pairs={{0,3},{1,4},{2,5},{3,6},{4,7},{5,8},{6,9},{7,10},{8,11},{9,0},{10,... | collective-permute-start | bytes 368648 | tf_op jit(solution)/shard_map/ppermute | solution.py:29
  150.8 29.2 %collective-permute-start.7 = (bf16[128,1152]{1,0:T(8,128)(2,1)S(1)}, bf16[128,1152]{1,0:T(8,128)(2,1)S(1)}, u32[]{:S(2)}, u32[]{:S(2)}) collective-permute-start(bf16[128,1152]{1,0:T(8,128)(2,1)S(1)} %slice_bitcast_fusion), channel_id=1, source_target_pairs={{0,24},{12,36},{24,0},{36,12},{1,25},{13,37},{25,1},{37,13},{2,26}... | collective-permute-start | bytes 884744 | tf_op jit(solution)/shard_map/ppermute | solution.py:163
  153.5 11.4 %collective-permute-start.14 = (bf16[1,48,1280]{2,1,0:T(8,128)(2,1)S(1)}, bf16[1,48,1280]{2,1,0:T(8,128)(2,1)S(1)}, u32[]{:S(2)}, u32[]{:S(2)}) collective-permute-start(bf16[1,48,1280]{2,1,0:T(8,128)(2,1)S(1)} %get-tuple-element.4), channel_id=1, source_target_pairs={{0,9},{1,10},{2,11},{3,0},{4,1},{5,2},{6,3},{7,4},{8,5},{9,6},{10,... | collective-permute-start | bytes 368648 | tf_op jit(solution)/shard_map/ppermute | solution.py:29
  157.0 15.8 %collective-permute-start.15 = (bf16[1,48,1280]{2,1,0:T(8,128)(2,1)S(1)}, bf16[1,48,1280]{2,1,0:T(8,128)(2,1)S(1)}, u32[]{:S(2)}, u32[]{:S(2)}) collective-permute-start(bf16[1,48,1280]{2,1,0:T(8,128)(2,1)S(1)} %get-tuple-element.4), channel_id=1, source_target_pairs={{0,6},{1,7},{2,8},{3,9},{4,10},{5,11},{6,0},{7,1},{8,2},{9,3},{10,... | collective-permute-start | bytes 368648 | tf_op jit(solution)/shard_map/ppermute | solution.py:29
  172.8 15.4 %collective-permute-start.16 = (bf16[4,48,1280]{2,1,0:T(8,128)(2,1)S(1)}, bf16[4,48,1280]{2,1,0:T(8,128)(2,1)S(1)}, u32[]{:S(2)}, u32[]{:S(2)}) collective-permute-start(bf16[4,48,1280]{2,1,0:T(8,128)(2,1)S(1)} %constant_dynamic-update-slice_fusion), channel_id=1, source_target_pairs={{0,1},{1,2},{2,3},{3,4},{4,5},{5,6},{6,7},{7,8},{8,9},{9,10},{10,1... | collective-permute-start | bytes 1474568 | tf_op jit(solution)/shard_map/ppermute | solution.py:29
  174.8 14.7 %collective-permute-start.17 = (bf16[4,48,1280]{2,1,0:T(8,128)(2,1)S(1)}, bf16[4,48,1280]{2,1,0:T(8,128)(2,1)S(1)}, u32[]{:S(2)}, u32[]{:S(2)}) collective-permute-start(bf16[4,48,1280]{2,1,0:T(8,128)(2,1)S(1)} %constant_dynamic-update-slice_fusion), channel_id=1, source_target_pairs={{0,11},{1,0},{2,1},{3,2},{4,3},{5,4},{6,5},{7,6},{8,7},{9,8},{10,9... | collective-permute-start | bytes 1474568 | tf_op jit(solution)/shard_map/ppermute | solution.py:29
  (5 other events, 15.0 us)

commit v2 on v1

--- a/solution.py
+++ b/solution.py
@@ -10,11 +10,9 @@
 F32 = jnp.float32
 BF16 = jnp.bfloat16
 
+X_PAIRS = [[y, y + NY] for y in range(NY)]
+Y_RINGS = [[h * NY + y for y in range(NY)] for h in range(2)]
 X_SWAP = [(i, (i + NY) % (2 * NY)) for i in range(2 * NY)]
-
-
-def y_shift(step):
-    return [(h * NY + y, h * NY + (y + step) % NY) for h in range(2) for y in range(NY)]
 
 
 def z_shift(step):
@@ -40,50 +38,23 @@
     return lax.dynamic_index_in_dim(blocks, index, 0, keepdims=True)
 
 
-def gather_weight(w0, x_hi, y):
-    from_m3 = over_rep(w0, y_shift(3))
-    from_p3 = over_rep(w0, y_shift(-3))
-    three = jnp.concatenate([w0, from_p3, from_m3])
-    from_m1 = over_rep(three, y_shift(1))
-    from_p1 = over_rep(jnp.concatenate([w0, from_m3]), y_shift(-1))
-    other_three = over_rep(three, X_SWAP)
-    five = jnp.concatenate([from_m1, from_p1])
-    other_five = over_rep(five, X_SWAP)
-    whole = jnp.zeros((16,) + w0.shape[1:], w0.dtype)
-    for half, low, high in ((x_hi, three, five), (1 - x_hi, other_three, other_five)):
-        for source, steps in ((low, (0, 3, -3)), (high, (-1, 2, 4, 1, -2))):
-            for slot, step in enumerate(steps):
-                place = half * NY + lax.rem(y + step + NY, NY)
-                whole = lax.dynamic_update_slice(
-                    whole, source[slot : slot + 1], (place, 0, 0)
-                )
+def gather_weight(w0):
+    pair = lax.all_gather(w0, "rep", axis=0, tiled=True, axis_index_groups=X_PAIRS)
+    whole = lax.all_gather(pair, "rep", axis=1, tiled=True, axis_index_groups=Y_RINGS)
     return whole.reshape(-1, w0.shape[2])
 
 
-def scatter_wgrad(normed, masked, factor, x_hi, y, keep_rows):
-    half = normed.shape[1] // 2
-    left, right = normed[:, :half], normed[:, half:]
-    first = x_hi == 0
-
-    def product(columns):
-        value = lax.dot_general(
-            columns, masked, (((0,), (0,)), ((), ())), preferred_element_type=F32
-        )
-        return (value * factor).astype(BF16).reshape(NY, keep_rows, -1)
-
-    sent = product(jnp.where(first, right, left))
-    came = over_rep(sent, X_SWAP)
-    mine = product(jnp.where(first, left, right))
-    both = add(mine, came)
-
-    def block(step):
-        return pick(both, lax.rem(y + step + NY, NY))
-
-    up1 = over_rep(jnp.concatenate([block(1), block(4), block(-2)]), y_shift(1))
-    down1 = over_rep(jnp.concatenate([block(-1), block(2)]), y_shift(-1))
-    plus3 = over_rep(add(block(3), up1[1:2], down1[1:2]), y_shift(3))
-    minus3 = over_rep(add(block(-3), up1[2:3]), y_shift(-3))
-    return add(block(0), up1[0:1], down1[0:1], plus3, minus3)
+def scatter_wgrad(normed, masked, factor, x_hi, keep_rows):
+    value = lax.dot_general(
+        normed, masked, (((0,), (0,)), ((), ())), preferred_element_type=F32
+    )
+    value = (value * factor).astype(BF16).reshape(2, NY, keep_rows, -1)
+    value = value.transpose(1, 0, 2, 3).reshape(NY * 2, keep_rows, -1)
+    pair = lax.psum_scatter(
+        value, "rep", scatter_dimension=0, tiled=True, axis_index_groups=Y_RINGS
+    )
+    came = over_rep(pick(pair, 1 - x_hi), X_SWAP)
+    return add(pick(pair, x_hi), came)
 
 
 def body(normed, up_weight, cotangent, lengths):
@@ -92,18 +63,18 @@
     pair_len = row_count // pair_count
     keep_rows, unit_count = up_weight.shape[1:]
     rep = lax.axis_index("rep")
-    x_hi, y = rep // NY, lax.rem(rep, NY)
+    x_hi = rep // NY
     row = lax.axis_index("row")
     z = lax.axis_index("col")
 
-    weight = gather_weight(up_weight, x_hi, y)
+    weight = gather_weight(up_weight)
 
     positions = lax.broadcasted_iota(jnp.int32, (pair_count, pair_len), 1)
     valid_rows = (positions < lengths[:, None]).reshape(row_count, 1)
     masked = jnp.where(valid_rows, cotangent, jnp.zeros_like(cotangent))
 
     factor = 1.0 / math.sqrt(row_count * lax.axis_size("rep"))
-    weight_grad = scatter_wgrad(normed, masked, factor, x_hi, y, keep_rows)
+    weight_grad = scatter_wgrad(normed, masked, factor, x_hi, keep_rows)
 
     unit_rows = -(-row_count // (NZ * 16)) * 16
     padded = jnp.pad(masked, ((0, NZ * unit_rows - row_count), (0, 0)))

time: 194 us -> 188 us (0.969)
  the two profiles are of different devices: /device:TPU:6 before, /device:TPU:4 now
where the time goes in v2:
time: 188 us; the launch traced here: 187 us
  starting transfers between devices  65.9 us (35%)
  waiting for transfers between devices  59.7 us (32%)
  blocking collectives  16.3 us (9%)
  between operations  15.3 us (8%)
  local copies, waits for them, and re-layouts  13.2 us (7%)
  matrix products  10.7 us (6%)
  other arithmetic  5.85 us (3%)
    ppermute x10, starting transfers between devices, over_col(): return lax.ppermute(value, 'col', z_shift(step))  58.8 us
    all_gather x1, waiting for transfers between devices, gather_weight(): lax.all_gather(pair, 'rep', axis=1, tiled=True, axis_index_groups=Y_RINGS)  29.5 us
    ppermute x10, waiting for transfers between devices, over_col(): return lax.ppermute(value, 'col', z_shift(step))  23.6 us
    all_gather x1, blocking collectives, gather_weight(): lax.all_gather(w0, 'rep', axis=0, tiled=True, axis_index_groups=X_PAIRS)  16.3 us
    ppermute x1, waiting for transfers between devices, over_rep(): return lax.ppermute(value, 'rep', pairs)  6.57 us
    dot_general x2, matrix products, partial_up(): jnp.dot(tokens.reshape(-1, width), weight, preferred_element_type=F32)  4.22 us
    convert_element_type x1, local copies, waits for them, and re-layouts, scatter_wgrad(): value = (value * factor).astype(BF16).reshape(2, NY, keep_rows, -1)  4.1 us
  transfers between devices with their start and end apart: 15, of which 8 were waited for; matrix products, arithmetic and copies ran while one was open for 14% of the time, Pallas kernels for 0%

profile of v2, /device:TPU:4, one launch (start us, length us, event | category | flops | bytes accessed | tf_op | source)
XLA Modules:
  0.0 187.1 jit_solution(8572366394105240097)
XLA Ops:
  7.2 16.3 %all_gather.6 = bf16[2,80,1152]{2,1,0:T(8,128)(2,1)} all-gather(bf16[1,80,1152]{2,1,0:T(8,128)(2,1)} %param.5), channel_id=1, replica_groups={{0,384},{48,432},{96,480},{144,528},{192,576},{240,624},{288,672},{336,..., dimensions={0}, use_global_device_ids=true | all-gather | bytes 552960 | tf_op jit(solution)/shard_map/all_gather | solution.py:42
  24.3 1.5 broadcast_select_fusion
  26.8 3.4 %fusion.1 = bf16[1280,1152]{0,1:T(8,128)(2,1)} fusion(bf16[512,1152]{1,0:T(8,128)(2,1)S(1)} %broadcast_select_fusion, bf16[512,1280]{1,0:T(8,128)(2,1)S(1)} %copy-done.1), kind=kOutput, calls=%fused_computation.2 | convolution fusion | flops 1512898560 | bytes 5439488 | tf_op jit(solution)/shard_map/dot_general | solution.py:48
  30.2 4.1 %copy.19 = bf16[1280,1152]{1,0:T(8,128)(2,1)S(1)} copy(bf16[1280,1152]{0,1:T(8,128)(2,1)} %fusion.1) | data formatting | bytes 5898240 | tf_op jit(solution)/shard_map/convert_element_type | solution.py:51
  34.3 1.8 copy.20
  36.2 1.3 copy-done.2
  38.4 1.3 maximum_select_fusion
  39.8 1.4 pad.4
  41.3 1.2 broadcast_select_fusion.1
  42.7 29.5 %all-gather.2.cloned.1.call-done = bf16[2,640,1152]{2,1,0:T(8,128)(2,1)} async-done(((bf16[2,80,1152]{2,1,0:T(8,128)(2,1)}), bf16[2,640,1152]{2,1,0:T(8,128)(2,1)}) %all-gather.2.cloned.1.call-update) | async-done | bytes 2949136 | tf_op jit(solution)/shard_map/all_gather | solution.py:43
  72.2 3.2 %convolution_convert_fusion = bf16[256,1152]{1,0:T(8,128)(2,1)S(1)} fusion(bf16[256,1280]{1,0:T(8,128)(2,1)} %bitcast.72, bf16[1280,1152]{1,0:T(8,128)(2,1)} %bitcast.55), kind=kOutput, calls=%fused_computation.3 | convolution fusion | flops 755269632 | bytes 4194304 | tf_op jit(solution)/shard_map/dot_general | solution.py:127
  75.4 1.9 %collective-permute-start = (bf16[2,128,1152]{2,1,0:T(8,128)(2,1)S(1)}, bf16[2,128,1152]{2,1,0:T(8,128)(2,1)S(1)}, u32[]{:S(2)}, u32[]{:S(2)}) collective-permute-start(bf16[2,128,1152]{2,1,0:T(8,128)(2,1)S(1)} %bitcast.76), channel_id=1, source_target_pairs={{0,12},{12,0},{24,36},{36,24},{1,13},{13,1},{25,37},{37,25},{2,14}... | collective-permute-start | bytes 1769480 | tf_op jit(solution)/shard_map/ppermute | solution.py:130
  78.4 3.6 %collective-permute-start.2 = (bf16[4,48,1280]{2,1,0:T(8,128)(2,1)S(1)}, bf16[4,48,1280]{2,1,0:T(8,128)(2,1)S(1)}, u32[]{:S(2)}, u32[]{:S(2)}) collective-permute-start(bf16[4,48,1280]{2,1,0:T(8,128)(2,1)S(1)} %bitcast.74), channel_id=1, source_target_pairs={{0,1},{1,2},{2,3},{3,4},{4,5},{5,6},{6,7},{7,8},{8,9},{9,10},{10,1... | collective-permute-start | bytes 1474568 | tf_op jit(solution)/shard_map/ppermute | solution.py:27
  83.1 4.9 %collective-permute-start.3 = (bf16[4,48,1280]{2,1,0:T(8,128)(2,1)S(1)}, bf16[4,48,1280]{2,1,0:T(8,128)(2,1)S(1)}, u32[]{:S(2)}, u32[]{:S(2)}) collective-permute-start(bf16[4,48,1280]{2,1,0:T(8,128)(2,1)S(1)} %bitcast.75), channel_id=1, source_target_pairs={{0,11},{1,0},{2,1},{3,2},{4,3},{5,4},{6,5},{7,6},{8,7},{9,8},{10,9... | collective-permute-start | bytes 1474568 | tf_op jit(solution)/shard_map/ppermute | solution.py:27
  88.0 1.0 convolution_convert_fusion.4
  90.1 6.8 %collective-permute-done.2 = bf16[4,48,1280]{2,1,0:T(8,128)(2,1)S(1)} collective-permute-done((bf16[4,48,1280]{2,1,0:T(8,128)(2,1)S(1)}, bf16[4,48,1280]{2,1,0:T(8,128)(2,1)S(1)}, u32[]{:S(2)}, u32[]{:S(2)}) %collective-permute-start.2) | collective-permute-done | bytes 491552 | tf_op jit(solution)/shard_map/ppermute | solution.py:27
  96.9 2.2 %collective-permute-done.3 = bf16[4,48,1280]{2,1,0:T(8,128)(2,1)S(1)} collective-permute-done((bf16[4,48,1280]{2,1,0:T(8,128)(2,1)S(1)}, bf16[4,48,1280]{2,1,0:T(8,128)(2,1)S(1)}, u32[]{:S(2)}, u32[]{:S(2)}) %collective-permute-start.3) | collective-permute-done | bytes 491552 | tf_op jit(solution)/shard_map/ppermute | solution.py:27
  99.3 7.3 %collective-permute-start.4 = (bf16[1,48,1280]{2,1,0:T(8,128)(2,1)S(1)}, bf16[1,48,1280]{2,1,0:T(8,128)(2,1)S(1)}, u32[]{:S(2)}, u32[]{:S(2)}) collective-permute-start(bf16[1,48,1280]{2,1,0:T(8,128)(2,1)S(1)} %get-tuple-element.16), channel_id=1, source_target_pairs={{0,3},{1,4},{2,5},{3,6},{4,7},{5,8},{6,9},{7,10},{8,11},{9,0},{10,... | collective-permute-start | bytes 368648 | tf_op jit(solution)/shard_map/ppermute | solution.py:27
  106.6 5.4 %collective-permute-start.6 = (bf16[1,48,1280]{2,1,0:T(8,128)(2,1)S(1)}, bf16[1,48,1280]{2,1,0:T(8,128)(2,1)S(1)}, u32[]{:S(2)}, u32[]{:S(2)}) collective-permute-start(bf16[1,48,1280]{2,1,0:T(8,128)(2,1)S(1)} %get-tuple-element.17), channel_id=1, source_target_pairs={{0,6},{1,7},{2,8},{3,9},{4,10},{5,11},{6,0},{7,1},{8,2},{9,3},{10,... | collective-permute-start | bytes 368648 | tf_op jit(solution)/shard_map/ppermute | solution.py:27
  112.1 5.2 %collective-permute-start.5 = (bf16[1,48,1280]{2,1,0:T(8,128)(2,1)S(1)}, bf16[1,48,1280]{2,1,0:T(8,128)(2,1)S(1)}, u32[]{:S(2)}, u32[]{:S(2)}) collective-permute-start(bf16[1,48,1280]{2,1,0:T(8,128)(2,1)S(1)} %get-tuple-element.18), channel_id=1, source_target_pairs={{0,9},{1,10},{2,11},{3,0},{4,1},{5,2},{6,3},{7,4},{8,5},{9,6},{10,... | collective-permute-start | bytes 368648 | tf_op jit(solution)/shard_map/ppermute | solution.py:27
  117.4 4.1 %collective-permute-done.6 = bf16[1,48,1280]{2,1,0:T(8,128)(2,1)S(1)} collective-permute-done((bf16[1,48,1280]{2,1,0:T(8,128)(2,1)S(1)}, bf16[1,48,1280]{2,1,0:T(8,128)(2,1)S(1)}, u32[]{:S(2)}, u32[]{:S(2)}) %collective-permute-start.6) | collective-permute-done | bytes 122912 | tf_op jit(solution)/shard_map/ppermute | solution.py:27
  122.2 9.3 %collective-permute-start.7 = (bf16[1,48,1280]{2,1,0:T(8,128)(2,1)S(1)}, bf16[1,48,1280]{2,1,0:T(8,128)(2,1)S(1)}, u32[]{:S(2)}, u32[]{:S(2)}) collective-permute-start(bf16[1,48,1280]{2,1,0:T(8,128)(2,1)S(1)} %get-tuple-element.4), channel_id=1, source_target_pairs={{0,3},{1,4},{2,5},{3,6},{4,7},{5,8},{6,9},{7,10},{8,11},{9,0},{10,... | collective-permute-start | bytes 368648 | tf_op jit(solution)/shard_map/ppermute | solution.py:27
  131.5 3.1 %collective-permute-start.1 = (bf16[128,1152]{1,0:T(8,128)(2,1)S(1)}, bf16[128,1152]{1,0:T(8,128)(2,1)S(1)}, u32[]{:S(2)}, u32[]{:S(2)}) collective-permute-start(bf16[128,1152]{1,0:T(8,128)(2,1)S(1)} %slice_bitcast_fusion), channel_id=1, source_target_pairs={{0,24},{12,36},{24,0},{36,12},{1,25},{13,37},{25,1},{37,13},{2,26}... | collective-permute-start | bytes 884744 | tf_op jit(solution)/shard_map/ppermute | solution.py:134
  134.7 4.7 %collective-permute-start.8 = (bf16[1,48,1280]{2,1,0:T(8,128)(2,1)S(1)}, bf16[1,48,1280]{2,1,0:T(8,128)(2,1)S(1)}, u32[]{:S(2)}, u32[]{:S(2)}) collective-permute-start(bf16[1,48,1280]{2,1,0:T(8,128)(2,1)S(1)} %get-tuple-element.4), channel_id=1, source_target_pairs={{0,9},{1,10},{2,11},{3,0},{4,1},{5,2},{6,3},{7,4},{8,5},{9,6},{10,... | collective-permute-start | bytes 368648 | tf_op jit(solution)/shard_map/ppermute | solution.py:27
  139.4 6.4 %collective-permute-start.9 = (bf16[1,48,1280]{2,1,0:T(8,128)(2,1)S(1)}, bf16[1,48,1280]{2,1,0:T(8,128)(2,1)S(1)}, u32[]{:S(2)}, u32[]{:S(2)}) collective-permute-start(bf16[1,48,1280]{2,1,0:T(8,128)(2,1)S(1)} %get-tuple-element.4), channel_id=1, source_target_pairs={{0,6},{1,7},{2,8},{3,9},{4,10},{5,11},{6,0},{7,1},{8,2},{9,3},{10,... | collective-permute-start | bytes 368648 | tf_op jit(solution)/shard_map/ppermute | solution.py:27
  145.8 7.4 %collective-permute-done.9 = bf16[1,48,1280]{2,1,0:T(8,128)(2,1)S(1)} collective-permute-done((bf16[1,48,1280]{2,1,0:T(8,128)(2,1)S(1)}, bf16[1,48,1280]{2,1,0:T(8,128)(2,1)S(1)}, u32[]{:S(2)}, u32[]{:S(2)}) %collective-permute-start.9) | collective-permute-done | bytes 122912 | tf_op jit(solution)/shard_map/ppermute | solution.py:27
  153.3 10.0 %collective-permute-start.11 = (bf16[4,48,1280]{2,1,0:T(8,128)(2,1)S(1)}, bf16[4,48,1280]{2,1,0:T(8,128)(2,1)S(1)}, u32[]{:S(2)}, u32[]{:S(2)}) collective-permute-start(bf16[4,48,1280]{2,1,0:T(8,128)(2,1)S(1)} %constant_dynamic-update-slice_fusion), channel_id=1, source_target_pairs={{0,11},{1,0},{2,1},{3,2},{4,3},{5,4},{6,5},{7,6},{8,7},{9,8},{10,9... | collective-permute-start | bytes 1474568 | tf_op jit(solution)/shard_map/ppermute | solution.py:27
  163.3 1.9 %collective-permute-start.10 = (bf16[4,48,1280]{2,1,0:T(8,128)(2,1)S(1)}, bf16[4,48,1280]{2,1,0:T(8,128)(2,1)S(1)}, u32[]{:S(2)}, u32[]{:S(2)}) collective-permute-start(bf16[4,48,1280]{2,1,0:T(8,128)(2,1)S(1)} %constant_dynamic-update-slice_fusion), channel_id=1, source_target_pairs={{0,1},{1,2},{2,3},{3,4},{4,5},{5,6},{6,7},{7,8},{8,9},{9,10},{10,1... | collective-permute-start | bytes 1474568 | tf_op jit(solution)/shard_map/ppermute | solution.py:27
  166.2 2.1 %collective-permute-start.12 = (bf16[1,80,1152]{2,1,0:T(8,128)(2,1)S(1)}, bf16[1,80,1152]{2,1,0:T(8,128)(2,1)S(1)}, u32[]{:S(2)}, u32[]{:S(2)}) collective-permute-start(bf16[1,80,1152]{2,1,0:T(8,128)(2,1)S(1)} %constant_dynamic-slice_fusion), channel_id=1, source_target_pairs={{0,384},{48,432},{96,480},{144,528},{192,576},{240,624},{288,672},... | collective-permute-start | bytes 552968 | tf_op jit(solution)/shard_map/ppermute | solution.py:23
  169.2 6.6 %collective-permute-done.12 = bf16[1,80,1152]{2,1,0:T(8,128)(2,1)S(1)} collective-permute-done((bf16[1,80,1152]{2,1,0:T(8,128)(2,1)S(1)}, bf16[1,80,1152]{2,1,0:T(8,128)(2,1)S(1)}, u32[]{:S(2)}, u32[]{:S(2)}) %collective-permute-start.12) | collective-permute-done | bytes 184352 | tf_op jit(solution)/shard_map/ppermute | solution.py:23
  176.5 2.5 %collective-permute-done.10 = bf16[4,48,1280]{2,1,0:T(8,128)(2,1)S(1)} collective-permute-done((bf16[4,48,1280]{2,1,0:T(8,128)(2,1)S(1)}, bf16[4,48,1280]{2,1,0:T(8,128)(2,1)S(1)}, u32[]{:S(2)}, u32[]{:S(2)}) %collective-permute-start.10) | collective-permute-done | bytes 491552 | tf_op jit(solution)/shard_map/ppermute | solution.py:27
  179.1 1.1 slice.50
  (46 shorter events, 9.2 us)
Async XLA Ops:
  7.2 65.0 %all-gather.2.cloned.1.call-start = ((), (), s32[]{:S(2)}) async-start(), calls=%async_computation.1 | async-start | bytes 3317760 | tf_op jit(solution)/shard_map/all_gather | solution.py:43
  23.5 3.3 %copy-start.1 = (bf16[512,1280]{1,0:T(8,128)(2,1)S(1)}, bf16[512,1280]{1,0:T(8,128)(2,1)}, u32[]{:S(2)}) copy-start(bf16[512,1280]{1,0:T(8,128)(2,1)} %param.4) | copy-start | bytes 3932164
  23.5 141.7 %reduce-scatter.2.cloned.1.call-start = ((), (), s32[]{:S(2)}) async-start(), calls=%async_computation.2 | async-start | bytes 3317760 | tf_op jit(solution)/shard_map/reduce_scatter | solution.py:53
  25.8 1.0 copy-start.3
  36.1 1.3 copy-start.2
  72.2 5.1 %copy-start = (bf16[2,640,1152]{2,1,0:T(8,128)(2,1)S(1)}, bf16[2,640,1152]{2,1,0:T(8,128)(2,1)}, u32[]{:S(2)}) copy-start(bf16[2,640,1152]{2,1,0:T(8,128)(2,1)} %all-gather.2.cloned.1.call-done) | copy-start | bytes 8847364
  75.4 41.9 %collective-permute-start = (bf16[2,128,1152]{2,1,0:T(8,128)(2,1)S(1)}, bf16[2,128,1152]{2,1,0:T(8,128)(2,1)S(1)}, u32[]{:S(2)}, u32[]{:S(2)}) collective-permute-start(bf16[2,128,1152]{2,1,0:T(8,128)(2,1)S(1)} %bitcast.76), channel_id=1, source_target_pairs={{0,12},{12,0},{24,36},{36,24},{1,13},{13,1},{25,37},{37,25},{2,14}... | collective-permute-start | bytes 1769480 | tf_op jit(solution)/shard_map/ppermute | solution.py:130
  78.4 18.5 %collective-permute-start.2 = (bf16[4,48,1280]{2,1,0:T(8,128)(2,1)S(1)}, bf16[4,48,1280]{2,1,0:T(8,128)(2,1)S(1)}, u32[]{:S(2)}, u32[]{:S(2)}) collective-permute-start(bf16[4,48,1280]{2,1,0:T(8,128)(2,1)S(1)} %bitcast.74), channel_id=1, source_target_pairs={{0,1},{1,2},{2,3},{3,4},{4,5},{5,6},{6,7},{7,8},{8,9},{9,10},{10,1... | collective-permute-start | bytes 1474568 | tf_op jit(solution)/shard_map/ppermute | solution.py:27
  83.1 16.0 %collective-permute-start.3 = (bf16[4,48,1280]{2,1,0:T(8,128)(2,1)S(1)}, bf16[4,48,1280]{2,1,0:T(8,128)(2,1)S(1)}, u32[]{:S(2)}, u32[]{:S(2)}) collective-permute-start(bf16[4,48,1280]{2,1,0:T(8,128)(2,1)S(1)} %bitcast.75), channel_id=1, source_target_pairs={{0,11},{1,0},{2,1},{3,2},{4,3},{5,4},{6,5},{7,6},{8,7},{9,8},{10,9... | collective-permute-start | bytes 1474568 | tf_op jit(solution)/shard_map/ppermute | solution.py:27
  88.0 1.1 copy-start.4
  99.3 18.1 %collective-permute-start.4 = (bf16[1,48,1280]{2,1,0:T(8,128)(2,1)S(1)}, bf16[1,48,1280]{2,1,0:T(8,128)(2,1)S(1)}, u32[]{:S(2)}, u32[]{:S(2)}) collective-permute-start(bf16[1,48,1280]{2,1,0:T(8,128)(2,1)S(1)} %get-tuple-element.16), channel_id=1, source_target_pairs={{0,3},{1,4},{2,5},{3,6},{4,7},{5,8},{6,9},{7,10},{8,11},{9,0},{10,... | collective-permute-start | bytes 368648 | tf_op jit(solution)/shard_map/ppermute | solution.py:27
  106.6 14.9 %collective-permute-start.6 = (bf16[1,48,1280]{2,1,0:T(8,128)(2,1)S(1)}, bf16[1,48,1280]{2,1,0:T(8,128)(2,1)S(1)}, u32[]{:S(2)}, u32[]{:S(2)}) collective-permute-start(bf16[1,48,1280]{2,1,0:T(8,128)(2,1)S(1)} %get-tuple-element.17), channel_id=1, source_target_pairs={{0,6},{1,7},{2,8},{3,9},{4,10},{5,11},{6,0},{7,1},{8,2},{9,3},{10,... | collective-permute-start | bytes 368648 | tf_op jit(solution)/shard_map/ppermute | solution.py:27
  112.1 10.0 %collective-permute-start.5 = (bf16[1,48,1280]{2,1,0:T(8,128)(2,1)S(1)}, bf16[1,48,1280]{2,1,0:T(8,128)(2,1)S(1)}, u32[]{:S(2)}, u32[]{:S(2)}) collective-permute-start(bf16[1,48,1280]{2,1,0:T(8,128)(2,1)S(1)} %get-tuple-element.18), channel_id=1, source_target_pairs={{0,9},{1,10},{2,11},{3,0},{4,1},{5,2},{6,3},{7,4},{8,5},{9,6},{10,... | collective-permute-start | bytes 368648 | tf_op jit(solution)/shard_map/ppermute | solution.py:27
  122.2 23.6 %collective-permute-start.7 = (bf16[1,48,1280]{2,1,0:T(8,128)(2,1)S(1)}, bf16[1,48,1280]{2,1,0:T(8,128)(2,1)S(1)}, u32[]{:S(2)}, u32[]{:S(2)}) collective-permute-start(bf16[1,48,1280]{2,1,0:T(8,128)(2,1)S(1)} %get-tuple-element.4), channel_id=1, source_target_pairs={{0,3},{1,4},{2,5},{3,6},{4,7},{5,8},{6,9},{7,10},{8,11},{9,0},{10,... | collective-permute-start | bytes 368648 | tf_op jit(solution)/shard_map/ppermute | solution.py:27
  131.5 36.9 %collective-permute-start.1 = (bf16[128,1152]{1,0:T(8,128)(2,1)S(1)}, bf16[128,1152]{1,0:T(8,128)(2,1)S(1)}, u32[]{:S(2)}, u32[]{:S(2)}) collective-permute-start(bf16[128,1152]{1,0:T(8,128)(2,1)S(1)} %slice_bitcast_fusion), channel_id=1, source_target_pairs={{0,24},{12,36},{24,0},{36,12},{1,25},{13,37},{25,1},{37,13},{2,26}... | collective-permute-start | bytes 884744 | tf_op jit(solution)/shard_map/ppermute | solution.py:134
  134.7 11.1 %collective-permute-start.8 = (bf16[1,48,1280]{2,1,0:T(8,128)(2,1)S(1)}, bf16[1,48,1280]{2,1,0:T(8,128)(2,1)S(1)}, u32[]{:S(2)}, u32[]{:S(2)}) collective-permute-start(bf16[1,48,1280]{2,1,0:T(8,128)(2,1)S(1)} %get-tuple-element.4), channel_id=1, source_target_pairs={{0,9},{1,10},{2,11},{3,0},{4,1},{5,2},{6,3},{7,4},{8,5},{9,6},{10,... | collective-permute-start | bytes 368648 | tf_op jit(solution)/shard_map/ppermute | solution.py:27
  139.4 13.9 %collective-permute-start.9 = (bf16[1,48,1280]{2,1,0:T(8,128)(2,1)S(1)}, bf16[1,48,1280]{2,1,0:T(8,128)(2,1)S(1)}, u32[]{:S(2)}, u32[]{:S(2)}) collective-permute-start(bf16[1,48,1280]{2,1,0:T(8,128)(2,1)S(1)} %get-tuple-element.4), channel_id=1, source_target_pairs={{0,6},{1,7},{2,8},{3,9},{4,10},{5,11},{6,0},{7,1},{8,2},{9,3},{10,... | collective-permute-start | bytes 368648 | tf_op jit(solution)/shard_map/ppermute | solution.py:27
  153.3 25.8 %collective-permute-start.11 = (bf16[4,48,1280]{2,1,0:T(8,128)(2,1)S(1)}, bf16[4,48,1280]{2,1,0:T(8,128)(2,1)S(1)}, u32[]{:S(2)}, u32[]{:S(2)}) collective-permute-start(bf16[4,48,1280]{2,1,0:T(8,128)(2,1)S(1)} %constant_dynamic-update-slice_fusion), channel_id=1, source_target_pairs={{0,11},{1,0},{2,1},{3,2},{4,3},{5,4},{6,5},{7,6},{8,7},{9,8},{10,9... | collective-permute-start | bytes 1474568 | tf_op jit(solution)/shard_map/ppermute | solution.py:27
  163.3 15.7 %collective-permute-start.10 = (bf16[4,48,1280]{2,1,0:T(8,128)(2,1)S(1)}, bf16[4,48,1280]{2,1,0:T(8,128)(2,1)S(1)}, u32[]{:S(2)}, u32[]{:S(2)}) collective-permute-start(bf16[4,48,1280]{2,1,0:T(8,128)(2,1)S(1)} %constant_dynamic-update-slice_fusion), channel_id=1, source_target_pairs={{0,1},{1,2},{2,3},{3,4},{4,5},{5,6},{6,7},{7,8},{8,9},{9,10},{10,1... | collective-permute-start | bytes 1474568 | tf_op jit(solution)/shard_map/ppermute | solution.py:27
  166.2 9.6 %copy-start.5 = (bf16[2,80,1152]{2,1,0:T(8,128)(2,1)S(1)}, bf16[2,80,1152]{2,1,0:T(8,128)(2,1)}, u32[]{:S(2)}) copy-start(bf16[2,80,1152]{2,1,0:T(8,128)(2,1)} %reduce-scatter.2.cloned.1.call-done) | copy-start | bytes 1105924
  166.2 9.6 %collective-permute-start.12 = (bf16[1,80,1152]{2,1,0:T(8,128)(2,1)S(1)}, bf16[1,80,1152]{2,1,0:T(8,128)(2,1)S(1)}, u32[]{:S(2)}, u32[]{:S(2)}) collective-permute-start(bf16[1,80,1152]{2,1,0:T(8,128)(2,1)S(1)} %constant_dynamic-slice_fusion), channel_id=1, source_target_pairs={{0,384},{48,432},{96,480},{144,528},{192,576},{240,624},{288,672},... | collective-permute-start | bytes 552968 | tf_op jit(solution)/shard_map/ppermute | solution.py:23
Sparse Core Ops, SparseCore 0:
  23.7 48.4 all-gather.1
  75.3 49.8 reduce-scatter.1

commit v3 on v2

--- a/solution.py
+++ b/solution.py
@@ -10,9 +10,12 @@
 F32 = jnp.float32
 BF16 = jnp.bfloat16
 
-X_PAIRS = [[y, y + NY] for y in range(NY)]
 Y_RINGS = [[h * NY + y for y in range(NY)] for h in range(2)]
 X_SWAP = [(i, (i + NY) % (2 * NY)) for i in range(2 * NY)]
+
+
+def y_shift(step):
+    return [(h * NY + y, h * NY + (y + step) % NY) for h in range(2) for y in range(NY)]
 
 
 def z_shift(step):
@@ -38,23 +41,41 @@
     return lax.dynamic_index_in_dim(blocks, index, 0, keepdims=True)
 
 
-def gather_weight(w0):
-    pair = lax.all_gather(w0, "rep", axis=0, tiled=True, axis_index_groups=X_PAIRS)
-    whole = lax.all_gather(pair, "rep", axis=1, tiled=True, axis_index_groups=Y_RINGS)
-    return whole.reshape(-1, w0.shape[2])
+def gather_weight(w0, y):
+    own = lax.all_gather(w0, "rep", axis=1, tiled=True, axis_index_groups=Y_RINGS)
+    there = over_rep(w0, X_SWAP)
+    from_m3 = over_rep(there, y_shift(3))
+    from_p3 = over_rep(there, y_shift(-3))
+    from_m1 = over_rep(jnp.concatenate([there, from_p3, from_m3]), y_shift(1))
+    from_p1 = over_rep(jnp.concatenate([there, from_m3]), y_shift(-1))
+    other = jnp.zeros((NY,) + w0.shape[1:], w0.dtype)
+    for source, steps in (
+        (there, (0,)),
+        (from_m3, (-3,)),
+        (from_p3, (3,)),
+        (from_m1, (-1, 2, 4)),
+        (from_p1, (1, -2)),
+    ):
+        for slot, step in enumerate(steps):
+            place = lax.rem(y + step + NY, NY)
+            other = lax.dynamic_update_slice(
+                other, source[slot : slot + 1], (place, 0, 0)
+            )
+    return jnp.concatenate([own[0], other.reshape(own.shape[1:])])
 
 
-def scatter_wgrad(normed, masked, factor, x_hi, keep_rows):
-    value = lax.dot_general(
-        normed, masked, (((0,), (0,)), ((), ())), preferred_element_type=F32
+def scatter_wgrad(halves, masked, factor):
+    def product(columns):
+        value = lax.dot_general(
+            columns, masked, (((0,), (0,)), ((), ())), preferred_element_type=F32
+        )
+        return (value * factor).astype(BF16)
+
+    came = over_rep(product(halves[1]), X_SWAP)
+    both = add(product(halves[0]), came)
+    return lax.psum_scatter(
+        both, "rep", scatter_dimension=0, tiled=True, axis_index_groups=Y_RINGS
     )
-    value = (value * factor).astype(BF16).reshape(2, NY, keep_rows, -1)
-    value = value.transpose(1, 0, 2, 3).reshape(NY * 2, keep_rows, -1)
-    pair = lax.psum_scatter(
-        value, "rep", scatter_dimension=0, tiled=True, axis_index_groups=Y_RINGS
-    )
-    came = over_rep(pick(pair, 1 - x_hi), X_SWAP)
-    return add(pick(pair, x_hi), came)
 
 
 def body(normed, up_weight, cotangent, lengths):
@@ -63,18 +84,24 @@
     pair_len = row_count // pair_count
     keep_rows, unit_count = up_weight.shape[1:]
     rep = lax.axis_index("rep")
-    x_hi = rep // NY
-    row = lax.axis_index("row")
+    y = lax.rem(rep, NY)
+    first = rep < NY
     z = lax.axis_index("col")
 
-    weight = gather_weight(up_weight)
+    def swap_halves(columns):
+        left, right = columns[:, : width // 2], columns[:, width // 2 :]
+        return jnp.where(first, left, right), jnp.where(first, right, left)
+
+    weight = gather_weight(up_weight, y)
 
     positions = lax.broadcasted_iota(jnp.int32, (pair_count, pair_len), 1)
     valid_rows = (positions < lengths[:, None]).reshape(row_count, 1)
     masked = jnp.where(valid_rows, cotangent, jnp.zeros_like(cotangent))
 
     factor = 1.0 / math.sqrt(row_count * lax.axis_size("rep"))
-    weight_grad = scatter_wgrad(normed, masked, factor, x_hi, keep_rows)
+    halves = swap_halves(normed)
+    weight_grad = scatter_wgrad(halves, masked, factor)
+    weight_grad = weight_grad.reshape(1, keep_rows, unit_count)
 
     unit_rows = -(-row_count // (NZ * 16)) * 16
     padded = jnp.pad(masked, ((0, NZ * unit_rows - row_count), (0, 0)))
@@ -115,24 +142,15 @@
         result = lax.dynamic_update_slice(
             result, value[:, None], (0, lax.rem(z + step + NZ, 3), 0, 0)
         )
-    normed_grad = result.reshape(NZ * unit_rows, width)[:row_count]
+    result = result.reshape(NZ * unit_rows, width)[:row_count]
+    normed_grad = jnp.concatenate(swap_halves(result), axis=1)
 
-    parts = normed.reshape(4, row_count // 4, width)
-    parts = jnp.where(row // 2 == 0, parts, jnp.concatenate([parts[2:], parts[:2]]))
-    even = jnp.concatenate([parts[0:1], parts[2:3]])
-    odd = jnp.concatenate([parts[1:2], parts[3:4]])
-    core = lax.rem(row, 2)
-
-    def partial_up(tokens):
-        value = jnp.dot(tokens.reshape(-1, width), weight, preferred_element_type=F32)
-        return value.astype(BF16).reshape(2, row_count // 4, unit_count)
-
-    came = lax.ppermute(
-        partial_up(jnp.where(core == 0, odd, even)), "row", [(r, r ^ 1) for r in range(4)]
+    up_partial = jnp.dot(
+        jnp.concatenate(halves, axis=1), weight, preferred_element_type=F32
     )
-    two = add(partial_up(jnp.where(core == 0, even, odd)), came)
-    came = lax.ppermute(two[1], "row", [(r, r ^ 2) for r in range(4)])
-    up_out = add(two[0], came)
+    up_out = lax.psum_scatter(
+        up_partial.astype(BF16), "row", scatter_dimension=0, tiled=True
+    )
     return (up_out, normed_grad, weight_grad)
 
 

time: 188 us -> 197 us (1.048)
  the two profiles are of different devices: /device:TPU:4 before, /device:TPU:6 now
where the time goes in v3:
time: 197 us; the launch traced here: 196 us
  starting transfers between devices  92.8 us (47%)
  waiting for transfers between devices  55.2 us (28%)
  matrix products  19.8 us (10%)
  between operations  15 us (8%)
  local copies, waits for them, and re-layouts  10 us (5%)
  other arithmetic  3.28 us (2%)
    ppermute x10, starting transfers between devices, over_col(): return lax.ppermute(value, 'col', z_shift(step))  59.9 us
    ppermute x10, waiting for transfers between devices, over_col(): return lax.ppermute(value, 'col', z_shift(step))  34.3 us
    ppermute x6, starting transfers between devices, over_rep(): return lax.ppermute(value, 'rep', pairs)  32.8 us
    ppermute x6, waiting for transfers between devices, over_rep(): return lax.ppermute(value, 'rep', pairs)  20.9 us
    dot_general x3, matrix products, partial_grad(): lax.dot_general(tokens.reshape(-1, unit_count), weight, (((1,), (1,)), ((...  9.4 us
    dot_general x2, matrix products, product(): lax.dot_general(columns, masked, (((0,), (0,)), ((), ())), preferred_elem...  5.73 us
    dynamic_update_slice x8, local copies, waits for them, and re-layouts, gather_weight(): lax.dynamic_update_slice(other, source[slot:slot + 1], (place, 0, 0))  5.57 us
    dot_general x1, matrix products, body(): jnp.dot(jnp.concatenate(halves, axis=1), weight, preferred_element_type=F32)  4.72 us
  transfers between devices with their start and end apart: 19, of which 9 were waited for; matrix products, arithmetic and copies ran while one was open for 16% of the time, Pallas kernels for 0%

profile of v3, /device:TPU:6, one launch (start us, length us, event | category | flops | bytes accessed | tf_op | source)
XLA Modules:
  0.0 196.2 jit_solution(1813971597103608912)
XLA Ops:
  7.2 3.4 %collective-permute-start = (bf16[1,80,1152]{2,1,0:T(8,128)(2,1)}, bf16[1,80,1152]{2,1,0:T(8,128)(2,1)S(1)}, u32[]{:S(2)}, u32[]{:S(2)}) collective-permute-start(bf16[1,80,1152]{2,1,0:T(8,128)(2,1)} %param.5), channel_id=1, source_target_pairs={{0,384},{48,432},{96,480},{144,528},{192,576},{240,624},{288,672},... | collective-permute-start | bytes 552968 | tf_op jit(solution)/shard_map/ppermute | solution.py:26
  11.4 1.5 broadcast_select_fusion
  13.1 2.2 %fusion.2 = bf16[640,1152]{1,0:T(8,128)(2,1)} fusion(bf16[512,640]{1,0:T(8,128)(2,1)S(1)} %get-tuple-element.11, bf16[512,1152]{1,0:T(8,128)(2,1)S(1)} %broadcast_select_fusion), kind=kOutput, calls=%fused_computation.4 | convolution fusion | flops 756449280 | bytes 3309568 | tf_op jit(solution)/shard_map/dot_general | solution.py:69
  15.2 4.0 %collective-permute-start.15 = (bf16[640,1152]{1,0:T(8,128)(2,1)}, bf16[640,1152]{1,0:T(8,128)(2,1)}, u32[]{:S(2)}, u32[]{:S(2)}) collective-permute-start(bf16[640,1152]{1,0:T(8,128)(2,1)} %fusion.2), channel_id=1, source_target_pairs={{0,384},{48,432},{96,480},{144,528},{192,576},{240,624},{288,672},... | collective-permute-start | bytes 4423688 | tf_op jit(solution)/shard_map/ppermute | solution.py:26
  20.6 5.5 %collective-permute-start.1 = (bf16[1,80,1152]{2,1,0:T(8,128)(2,1)S(1)}, bf16[1,80,1152]{2,1,0:T(8,128)(2,1)S(1)}, u32[]{:S(2)}, u32[]{:S(2)}) collective-permute-start(bf16[1,80,1152]{2,1,0:T(8,128)(2,1)S(1)} %collective-permute-done), channel_id=1, source_target_pairs={{0,144},{48,192},{96,240},{144,288},{192,336},{240,0},{288,48},{33... | collective-permute-start | bytes 552968 | tf_op jit(solution)/shard_map/ppermute | solution.py:26
  26.2 3.4 %collective-permute-start.2 = (bf16[1,80,1152]{2,1,0:T(8,128)(2,1)S(1)}, bf16[1,80,1152]{2,1,0:T(8,128)(2,1)S(1)}, u32[]{:S(2)}, u32[]{:S(2)}) collective-permute-start(bf16[1,80,1152]{2,1,0:T(8,128)(2,1)S(1)} %collective-permute-done), channel_id=1, source_target_pairs={{0,240},{48,288},{96,336},{144,0},{192,48},{240,96},{288,144},{336... | collective-permute-start | bytes 552968 | tf_op jit(solution)/shard_map/ppermute | solution.py:26
  29.5 1.2 broadcast_in_dim.30
  31.5 7.2 %collective-permute-done.1 = bf16[1,80,1152]{2,1,0:T(8,128)(2,1)S(1)} collective-permute-done((bf16[1,80,1152]{2,1,0:T(8,128)(2,1)S(1)}, bf16[1,80,1152]{2,1,0:T(8,128)(2,1)S(1)}, u32[]{:S(2)}, u32[]{:S(2)}) %collective-permute-start.1) | collective-permute-done | bytes 184352 | tf_op jit(solution)/shard_map/ppermute | solution.py:26
  38.7 14.5 %collective-permute-start.3 = (bf16[3,80,1152]{2,1,0:T(8,128)(2,1)S(1)}, bf16[3,80,1152]{2,1,0:T(8,128)(2,1)S(1)}, u32[]{:S(2)}, u32[]{:S(2)}) collective-permute-start(bf16[3,80,1152]{2,1,0:T(8,128)(2,1)S(1)} %pad_maximum_fusion.2), channel_id=1, source_target_pairs={{0,48},{48,96},{96,144},{144,192},{192,240},{240,288},{288,336},{3... | collective-permute-start | bytes 1658888 | tf_op jit(solution)/shard_map/ppermute | solution.py:26
  53.3 1.9 collective-permute-start.4
  56.6 13.7 %collective-permute-done.3 = bf16[3,80,1152]{2,1,0:T(8,128)(2,1)S(1)} collective-permute-done((bf16[3,80,1152]{2,1,0:T(8,128)(2,1)S(1)}, bf16[3,80,1152]{2,1,0:T(8,128)(2,1)S(1)}, u32[]{:S(2)}, u32[]{:S(2)}) %collective-permute-start.3) | collective-permute-done | bytes 552992 | tf_op jit(solution)/shard_map/ppermute | solution.py:26
  73.8 3.6 %add_convert_fusion = bf16[640,1152]{1,0:T(8,128)(2,1)} fusion(bf16[640,1152]{1,0:T(8,128)(2,1)} %collective-permute-done.15, bf16[512,640]{1,0:T(8,128)(2,1)S(1)} %get-tuple-element.10, bf16[512,1152]{1,0:T(8,128)(2,1)S(1)} %broadcast_select_fusion), kind=kOutput, calls=%fused_computation.7 | convolution fusion | flops 759398400 | bytes 4784128 | tf_op jit(solution)/shard_map/dot_general | solution.py:69
  79.1 3.8 %convolution_convert_fusion.2 = bf16[192,1280]{1,0:T(8,128)(2,1)} fusion(bf16[192,1152]{1,0:T(8,128)(2,1)S(1)} %bitcast.36, bf16[640,1152]{1,0:T(8,128)(2,1)} %bitcast.1, bf16[640,1152]{1,0:T(8,128)(2,1)} %bitcast.37), kind=kOutput, calls=%fused_computation.9 | convolution fusion | flops 572375040 | bytes 3883008 | tf_op jit(solution)/shard_map/dot_general | solution.py:112
  82.8 4.1 %collective-permute-start.5 = (bf16[4,48,1280]{2,1,0:T(8,128)(2,1)}, bf16[4,48,1280]{2,1,0:T(8,128)(2,1)S(1)}, u32[]{:S(2)}, u32[]{:S(2)}) collective-permute-start(bf16[4,48,1280]{2,1,0:T(8,128)(2,1)} %bitcast.7), channel_id=1, source_target_pairs={{0,1},{1,2},{2,3},{3,4},{4,5},{5,6},{6,7},{7,8},{8,9},{9,10},{10,1... | collective-permute-start | bytes 1474568 | tf_op jit(solution)/shard_map/ppermute | solution.py:30
  86.9 3.2 %convolution_convert_fusion.1 = bf16[192,1280]{1,0:T(8,128)(2,1)} fusion(bf16[192,1152]{1,0:T(8,128)(2,1)S(1)} %bitcast.35, bf16[640,1152]{1,0:T(8,128)(2,1)} %bitcast.1, bf16[640,1152]{1,0:T(8,128)(2,1)S(1)} %bitcast.39), kind=kOutput, calls=%fused_computation.8 | convolution fusion | flops 572375040 | bytes 3883008 | tf_op jit(solution)/shard_map/dot_general | solution.py:112
  90.2 10.5 %collective-permute-start.6 = (bf16[4,48,1280]{2,1,0:T(8,128)(2,1)}, bf16[4,48,1280]{2,1,0:T(8,128)(2,1)S(1)}, u32[]{:S(2)}, u32[]{:S(2)}) collective-permute-start(bf16[4,48,1280]{2,1,0:T(8,128)(2,1)} %bitcast.9), channel_id=1, source_target_pairs={{0,11},{1,0},{2,1},{3,2},{4,3},{5,4},{6,5},{7,6},{8,7},{9,8},{10,9... | collective-permute-start | bytes 1474568 | tf_op jit(solution)/shard_map/ppermute | solution.py:30
  100.8 2.4 %convolution_convert_fusion.3 = bf16[192,1280]{1,0:T(8,128)(2,1)S(1)} fusion(bf16[192,1152]{1,0:T(8,128)(2,1)S(1)} %bitcast.34, bf16[640,1152]{1,0:T(8,128)(2,1)} %bitcast.1, bf16[640,1152]{1,0:T(8,128)(2,1)S(1)} %bitcast.40), kind=kOutput, calls=%fused_computation.10 | convolution fusion | flops 572375040 | bytes 3883008 | tf_op jit(solution)/shard_map/dot_general | solution.py:112
  103.2 3.7 %collective-permute-done.5 = bf16[4,48,1280]{2,1,0:T(8,128)(2,1)S(1)} collective-permute-done((bf16[4,48,1280]{2,1,0:T(8,128)(2,1)}, bf16[4,48,1280]{2,1,0:T(8,128)(2,1)S(1)}, u32[]{:S(2)}, u32[]{:S(2)}) %collective-permute-start.5) | collective-permute-done | bytes 491552 | tf_op jit(solution)/shard_map/ppermute | solution.py:30
  106.9 4.5 %collective-permute-done.6 = bf16[4,48,1280]{2,1,0:T(8,128)(2,1)S(1)} collective-permute-done((bf16[4,48,1280]{2,1,0:T(8,128)(2,1)}, bf16[4,48,1280]{2,1,0:T(8,128)(2,1)S(1)}, u32[]{:S(2)}, u32[]{:S(2)}) %collective-permute-start.6) | collective-permute-done | bytes 491552 | tf_op jit(solution)/shard_map/ppermute | solution.py:30
  111.7 3.4 %collective-permute-start.7 = (bf16[1,48,1280]{2,1,0:T(8,128)(2,1)S(1)}, bf16[1,48,1280]{2,1,0:T(8,128)(2,1)S(1)}, u32[]{:S(2)}, u32[]{:S(2)}) collective-permute-start(bf16[1,48,1280]{2,1,0:T(8,128)(2,1)S(1)} %get-tuple-element.12), channel_id=1, source_target_pairs={{0,3},{1,4},{2,5},{3,6},{4,7},{5,8},{6,9},{7,10},{8,11},{9,0},{10,... | collective-permute-start | bytes 368648 | tf_op jit(solution)/shard_map/ppermute | solution.py:30
  115.1 5.6 %collective-permute-start.8 = (bf16[1,48,1280]{2,1,0:T(8,128)(2,1)S(1)}, bf16[1,48,1280]{2,1,0:T(8,128)(2,1)S(1)}, u32[]{:S(2)}, u32[]{:S(2)}) collective-permute-start(bf16[1,48,1280]{2,1,0:T(8,128)(2,1)S(1)} %get-tuple-element.14), channel_id=1, source_target_pairs={{0,9},{1,10},{2,11},{3,0},{4,1},{5,2},{6,3},{7,4},{8,5},{9,6},{10,... | collective-permute-start | bytes 368648 | tf_op jit(solution)/shard_map/ppermute | solution.py:30
  120.7 7.5 %collective-permute-start.9 = (bf16[1,48,1280]{2,1,0:T(8,128)(2,1)S(1)}, bf16[1,48,1280]{2,1,0:T(8,128)(2,1)S(1)}, u32[]{:S(2)}, u32[]{:S(2)}) collective-permute-start(bf16[1,48,1280]{2,1,0:T(8,128)(2,1)S(1)} %get-tuple-element.13), channel_id=1, source_target_pairs={{0,6},{1,7},{2,8},{3,9},{4,10},{5,11},{6,0},{7,1},{8,2},{9,3},{10,... | collective-permute-start | bytes 368648 | tf_op jit(solution)/shard_map/ppermute | solution.py:30
  128.3 9.2 %collective-permute-done.9 = bf16[1,48,1280]{2,1,0:T(8,128)(2,1)S(1)} collective-permute-done((bf16[1,48,1280]{2,1,0:T(8,128)(2,1)S(1)}, bf16[1,48,1280]{2,1,0:T(8,128)(2,1)S(1)}, u32[]{:S(2)}, u32[]{:S(2)}) %collective-permute-start.9) | collective-permute-done | bytes 122912 | tf_op jit(solution)/shard_map/ppermute | solution.py:30
  137.6 7.0 %collective-permute-start.10 = (bf16[1,48,1280]{2,1,0:T(8,128)(2,1)S(1)}, bf16[1,48,1280]{2,1,0:T(8,128)(2,1)S(1)}, u32[]{:S(2)}, u32[]{:S(2)}) collective-permute-start(bf16[1,48,1280]{2,1,0:T(8,128)(2,1)S(1)} %get-tuple-element.4), channel_id=1, source_target_pairs={{0,3},{1,4},{2,5},{3,6},{4,7},{5,8},{6,9},{7,10},{8,11},{9,0},{10,... | collective-permute-start | bytes 368648 | tf_op jit(solution)/shard_map/ppermute | solution.py:30
  144.7 4.7 %convolution_convert_fusion = bf16[512,1152]{1,0:T(8,128)(2,1)} fusion(bf16[512,640]{1,0:T(8,128)(2,1)S(1)} %copy-done.2, bf16[512,640]{1,0:T(8,128)(2,1)S(1)} %get-tuple-element.10, bf16[640,1152]{1,0:T(8,128)(2,1)} %bitcast.1, bf16[640,1152]{1,0:T(8,128)(2,1)} %bitcast.38), kind=kOutput, calls=%fused_computation.5 | convolution fusion | flops 1519058944 | bytes 5439488 | tf_op jit(solution)/shard_map/dot_general | solution.py:148
  149.4 1.9 collective-permute-start.11
  151.3 7.0 %collective-permute-start.12 = (bf16[1,48,1280]{2,1,0:T(8,128)(2,1)S(1)}, bf16[1,48,1280]{2,1,0:T(8,128)(2,1)S(1)}, u32[]{:S(2)}, u32[]{:S(2)}) collective-permute-start(bf16[1,48,1280]{2,1,0:T(8,128)(2,1)S(1)} %get-tuple-element.4), channel_id=1, source_target_pairs={{0,6},{1,7},{2,8},{3,9},{4,10},{5,11},{6,0},{7,1},{8,2},{9,3},{10,... | collective-permute-start | bytes 368648 | tf_op jit(solution)/shard_map/ppermute | solution.py:30
  158.4 4.4 %collective-permute-done.11 = bf16[1,48,1280]{2,1,0:T(8,128)(2,1)S(1)} collective-permute-done((bf16[1,48,1280]{2,1,0:T(8,128)(2,1)S(1)}, bf16[1,48,1280]{2,1,0:T(8,128)(2,1)S(1)}, u32[]{:S(2)}, u32[]{:S(2)}) %collective-permute-start.11) | collective-permute-done | bytes 122912 | tf_op jit(solution)/shard_map/ppermute | solution.py:30
  162.8 2.5 %collective-permute-done.12 = bf16[1,48,1280]{2,1,0:T(8,128)(2,1)S(1)} collective-permute-done((bf16[1,48,1280]{2,1,0:T(8,128)(2,1)S(1)}, bf16[1,48,1280]{2,1,0:T(8,128)(2,1)S(1)}, u32[]{:S(2)}, u32[]{:S(2)}) %collective-permute-start.12) | collective-permute-done | bytes 122912 | tf_op jit(solution)/shard_map/ppermute | solution.py:30
  165.3 8.0 %collective-permute-start.13 = (bf16[4,48,1280]{2,1,0:T(8,128)(2,1)S(1)}, bf16[4,48,1280]{2,1,0:T(8,128)(2,1)S(1)}, u32[]{:S(2)}, u32[]{:S(2)}) collective-permute-start(bf16[4,48,1280]{2,1,0:T(8,128)(2,1)S(1)} %constant_dynamic-update-slice_fusion), channel_id=1, source_target_pairs={{0,1},{1,2},{2,3},{3,4},{4,5},{5,6},{6,7},{7,8},{8,9},{9,10},{10,1... | collective-permute-start | bytes 1474568 | tf_op jit(solution)/shard_map/ppermute | solution.py:30
  173.4 4.9 %collective-permute-start.14 = (bf16[4,48,1280]{2,1,0:T(8,128)(2,1)S(1)}, bf16[4,48,1280]{2,1,0:T(8,128)(2,1)S(1)}, u32[]{:S(2)}, u32[]{:S(2)}) collective-permute-start(bf16[4,48,1280]{2,1,0:T(8,128)(2,1)S(1)} %constant_dynamic-update-slice_fusion), channel_id=1, source_target_pairs={{0,11},{1,0},{2,1},{3,2},{4,3},{5,4},{6,5},{7,6},{8,7},{9,8},{10,9... | collective-permute-start | bytes 1474568 | tf_op jit(solution)/shard_map/ppermute | solution.py:30
  178.4 8.7 %collective-permute-done.13 = bf16[4,48,1280]{2,1,0:T(8,128)(2,1)S(1)} collective-permute-done((bf16[4,48,1280]{2,1,0:T(8,128)(2,1)S(1)}, bf16[4,48,1280]{2,1,0:T(8,128)(2,1)S(1)}, u32[]{:S(2)}, u32[]{:S(2)}) %collective-permute-start.13) | collective-permute-done | bytes 491552 | tf_op jit(solution)/shard_map/ppermute | solution.py:30
  (62 shorter events, 11.9 us)
Async XLA Ops:
  7.2 5.7 %copy-start = (bf16[512,1280]{1,0:T(8,128)(2,1)S(1)}, bf16[512,1280]{1,0:T(8,128)(2,1)}, u32[]{:S(2)}) copy-start(bf16[512,1280]{1,0:T(8,128)(2,1)} %param.4) | copy-start | bytes 3932164
  7.2 71.9 %all-gather.2.cloned.1.call-start = ((), (), s32[]{:S(2)}) async-start(), calls=%async_computation.2 | async-start | bytes 1658880 | tf_op jit(solution)/shard_map/all_gather | solution.py:45
  7.2 13.4 %collective-permute-start = (bf16[1,80,1152]{2,1,0:T(8,128)(2,1)}, bf16[1,80,1152]{2,1,0:T(8,128)(2,1)S(1)}, u32[]{:S(2)}, u32[]{:S(2)}) collective-permute-start(bf16[1,80,1152]{2,1,0:T(8,128)(2,1)} %param.5), channel_id=1, source_target_pairs={{0,384},{48,432},{96,480},{144,528},{192,576},{240,624},{288,672},... | collective-permute-start | bytes 552968 | tf_op jit(solution)/shard_map/ppermute | solution.py:26
  10.7 178.9 %reduce-scatter.5.cloned.1.call-start = ((), (), s32[]{:S(2)}) async-start(), calls=%async_computation.4 | async-start | bytes 1658880 | tf_op jit(solution)/shard_map/reduce_scatter | solution.py:76
  13.0 2.2 %copy-start.1 = (bf16[512,640]{1,0:T(8,128)(2,1)}, bf16[512,640]{1,0:T(8,128)(2,1)S(1)}, u32[]{:S(2)}) copy-start(bf16[512,640]{1,0:T(8,128)(2,1)S(1)} %get-tuple-element.11) | copy-start | bytes 1966084
  15.2 58.6 %collective-permute-start.15 = (bf16[640,1152]{1,0:T(8,128)(2,1)}, bf16[640,1152]{1,0:T(8,128)(2,1)}, u32[]{:S(2)}, u32[]{:S(2)}) collective-permute-start(bf16[640,1152]{1,0:T(8,128)(2,1)} %fusion.2), channel_id=1, source_target_pairs={{0,384},{48,432},{96,480},{144,528},{192,576},{240,624},{288,672},... | collective-permute-start | bytes 4423688 | tf_op jit(solution)/shard_map/ppermute | solution.py:26
  20.6 18.0 %collective-permute-start.1 = (bf16[1,80,1152]{2,1,0:T(8,128)(2,1)S(1)}, bf16[1,80,1152]{2,1,0:T(8,128)(2,1)S(1)}, u32[]{:S(2)}, u32[]{:S(2)}) collective-permute-start(bf16[1,80,1152]{2,1,0:T(8,128)(2,1)S(1)} %collective-permute-done), channel_id=1, source_target_pairs={{0,144},{48,192},{96,240},{144,288},{192,336},{240,0},{288,48},{33... | collective-permute-start | bytes 552968 | tf_op jit(solution)/shard_map/ppermute | solution.py:26
  26.2 12.5 %collective-permute-start.2 = (bf16[1,80,1152]{2,1,0:T(8,128)(2,1)S(1)}, bf16[1,80,1152]{2,1,0:T(8,128)(2,1)S(1)}, u32[]{:S(2)}, u32[]{:S(2)}) collective-permute-start(bf16[1,80,1152]{2,1,0:T(8,128)(2,1)S(1)} %collective-permute-done), channel_id=1, source_target_pairs={{0,240},{48,288},{96,336},{144,0},{192,48},{240,96},{288,144},{336... | collective-permute-start | bytes 552968 | tf_op jit(solution)/shard_map/ppermute | solution.py:26
  38.7 31.6 %collective-permute-start.3 = (bf16[3,80,1152]{2,1,0:T(8,128)(2,1)S(1)}, bf16[3,80,1152]{2,1,0:T(8,128)(2,1)S(1)}, u32[]{:S(2)}, u32[]{:S(2)}) collective-permute-start(bf16[3,80,1152]{2,1,0:T(8,128)(2,1)S(1)} %pad_maximum_fusion.2), channel_id=1, source_target_pairs={{0,48},{48,96},{96,144},{144,192},{192,240},{240,288},{288,336},{3... | collective-permute-start | bytes 1658888 | tf_op jit(solution)/shard_map/ppermute | solution.py:26
  53.3 19.1 %collective-permute-start.4 = (bf16[2,80,1152]{2,1,0:T(8,128)(2,1)S(1)}, bf16[2,80,1152]{2,1,0:T(8,128)(2,1)S(1)}, u32[]{:S(2)}, u32[]{:S(2)}) collective-permute-start(bf16[2,80,1152]{2,1,0:T(8,128)(2,1)S(1)} %pad_maximum_fusion.3), channel_id=1, source_target_pairs={{0,336},{48,0},{96,48},{144,96},{192,144},{240,192},{288,240},{336... | collective-permute-start | bytes 1105928 | tf_op jit(solution)/shard_map/ppermute | solution.py:26
  72.4 0.7 copy-start.6
  77.4 1.0 copy-start.7
  77.4 1.7 copy-start.5
  77.4 112.3 %reduce-scatter.3.cloned.1.call-start = ((), (), s32[]{:S(2)}) async-start(), calls=%async_computation.3 | async-start | bytes 1474560 | tf_op jit(solution)/shard_map/reduce_scatter | solution.py:151
  79.1 7.9 %copy-start.4 = (bf16[4,1,48,1152]{3,2,1,0:T(8,128)(2,1)S(1)}, bf16[4,1,48,1152]{3,2,1,0:T(8,128)(2,1)}, u32[]{:S(2)}) copy-start(bf16[4,1,48,1152]{3,2,1,0:T(8,128)(2,1)} %get-tuple-element.8) | copy-start | bytes 1327108
  79.1 7.9 %copy-start.8 = (bf16[1,640,1152]{2,1,0:T(8,128)(2,1)S(1)}, bf16[1,640,1152]{2,1,0:T(8,128)(2,1)}, u32[]{:S(2)}) copy-start(bf16[1,640,1152]{2,1,0:T(8,128)(2,1)} %all-gather.2.cloned.1.call-done) | copy-start | bytes 4423684
  82.8 24.1 %collective-permute-start.5 = (bf16[4,48,1280]{2,1,0:T(8,128)(2,1)}, bf16[4,48,1280]{2,1,0:T(8,128)(2,1)S(1)}, u32[]{:S(2)}, u32[]{:S(2)}) collective-permute-start(bf16[4,48,1280]{2,1,0:T(8,128)(2,1)} %bitcast.7), channel_id=1, source_target_pairs={{0,1},{1,2},{2,3},{3,4},{4,5},{5,6},{6,7},{7,8},{8,9},{9,10},{10,1... | collective-permute-start | bytes 1474568 | tf_op jit(solution)/shard_map/ppermute | solution.py:30
  86.9 13.8 %copy-start.3 = (bf16[4,1,48,1152]{3,2,1,0:T(8,128)(2,1)S(1)}, bf16[4,1,48,1152]{3,2,1,0:T(8,128)(2,1)}, u32[]{:S(2)}) copy-start(bf16[4,1,48,1152]{3,2,1,0:T(8,128)(2,1)} %get-tuple-element.9) | copy-start | bytes 1327108
  90.2 21.3 %collective-permute-start.6 = (bf16[4,48,1280]{2,1,0:T(8,128)(2,1)}, bf16[4,48,1280]{2,1,0:T(8,128)(2,1)S(1)}, u32[]{:S(2)}, u32[]{:S(2)}) collective-permute-start(bf16[4,48,1280]{2,1,0:T(8,128)(2,1)} %bitcast.9), channel_id=1, source_target_pairs={{0,11},{1,0},{2,1},{3,2},{4,3},{5,4},{6,5},{7,6},{8,7},{9,8},{10,9... | collective-permute-start | bytes 1474568 | tf_op jit(solution)/shard_map/ppermute | solution.py:30
  111.7 33.0 %copy-start.2 = (bf16[512,640]{1,0:T(8,128)(2,1)S(1)}, bf16[512,640]{1,0:T(8,128)(2,1)}, u32[]{:S(2)}) copy-start(bf16[512,640]{1,0:T(8,128)(2,1)} %copy-done.1) | copy-start | bytes 1966084
  111.7 16.5 %collective-permute-start.7 = (bf16[1,48,1280]{2,1,0:T(8,128)(2,1)S(1)}, bf16[1,48,1280]{2,1,0:T(8,128)(2,1)S(1)}, u32[]{:S(2)}, u32[]{:S(2)}) collective-permute-start(bf16[1,48,1280]{2,1,0:T(8,128)(2,1)S(1)} %get-tuple-element.12), channel_id=1, source_target_pairs={{0,3},{1,4},{2,5},{3,6},{4,7},{5,8},{6,9},{7,10},{8,11},{9,0},{10,... | collective-permute-start | bytes 368648 | tf_op jit(solution)/shard_map/ppermute | solution.py:30
  115.1 13.1 %collective-permute-start.8 = (bf16[1,48,1280]{2,1,0:T(8,128)(2,1)S(1)}, bf16[1,48,1280]{2,1,0:T(8,128)(2,1)S(1)}, u32[]{:S(2)}, u32[]{:S(2)}) collective-permute-start(bf16[1,48,1280]{2,1,0:T(8,128)(2,1)S(1)} %get-tuple-element.14), channel_id=1, source_target_pairs={{0,9},{1,10},{2,11},{3,0},{4,1},{5,2},{6,3},{7,4},{8,5},{9,6},{10,... | collective-permute-start | bytes 368648 | tf_op jit(solution)/shard_map/ppermute | solution.py:30
  120.7 16.8 %collective-permute-start.9 = (bf16[1,48,1280]{2,1,0:T(8,128)(2,1)S(1)}, bf16[1,48,1280]{2,1,0:T(8,128)(2,1)S(1)}, u32[]{:S(2)}, u32[]{:S(2)}) collective-permute-start(bf16[1,48,1280]{2,1,0:T(8,128)(2,1)S(1)} %get-tuple-element.13), channel_id=1, source_target_pairs={{0,6},{1,7},{2,8},{3,9},{4,10},{5,11},{6,0},{7,1},{8,2},{9,3},{10,... | collective-permute-start | bytes 368648 | tf_op jit(solution)/shard_map/ppermute | solution.py:30
  137.6 20.7 %collective-permute-start.10 = (bf16[1,48,1280]{2,1,0:T(8,128)(2,1)S(1)}, bf16[1,48,1280]{2,1,0:T(8,128)(2,1)S(1)}, u32[]{:S(2)}, u32[]{:S(2)}) collective-permute-start(bf16[1,48,1280]{2,1,0:T(8,128)(2,1)S(1)} %get-tuple-element.4), channel_id=1, source_target_pairs={{0,3},{1,4},{2,5},{3,6},{4,7},{5,8},{6,9},{7,10},{8,11},{9,0},{10,... | collective-permute-start | bytes 368648 | tf_op jit(solution)/shard_map/ppermute | solution.py:30
  149.4 13.4 %collective-permute-start.11 = (bf16[1,48,1280]{2,1,0:T(8,128)(2,1)S(1)}, bf16[1,48,1280]{2,1,0:T(8,128)(2,1)S(1)}, u32[]{:S(2)}, u32[]{:S(2)}) collective-permute-start(bf16[1,48,1280]{2,1,0:T(8,128)(2,1)S(1)} %get-tuple-element.4), channel_id=1, source_target_pairs={{0,9},{1,10},{2,11},{3,0},{4,1},{5,2},{6,3},{7,4},{8,5},{9,6},{10,... | collective-permute-start | bytes 368648 | tf_op jit(solution)/shard_map/ppermute | solution.py:30
  151.3 14.0 %collective-permute-start.12 = (bf16[1,48,1280]{2,1,0:T(8,128)(2,1)S(1)}, bf16[1,48,1280]{2,1,0:T(8,128)(2,1)S(1)}, u32[]{:S(2)}, u32[]{:S(2)}) collective-permute-start(bf16[1,48,1280]{2,1,0:T(8,128)(2,1)S(1)} %get-tuple-element.4), channel_id=1, source_target_pairs={{0,6},{1,7},{2,8},{3,9},{4,10},{5,11},{6,0},{7,1},{8,2},{9,3},{10,... | collective-permute-start | bytes 368648 | tf_op jit(solution)/shard_map/ppermute | solution.py:30
  165.3 21.8 %collective-permute-start.13 = (bf16[4,48,1280]{2,1,0:T(8,128)(2,1)S(1)}, bf16[4,48,1280]{2,1,0:T(8,128)(2,1)S(1)}, u32[]{:S(2)}, u32[]{:S(2)}) collective-permute-start(bf16[4,48,1280]{2,1,0:T(8,128)(2,1)S(1)} %constant_dynamic-update-slice_fusion), channel_id=1, source_target_pairs={{0,1},{1,2},{2,3},{3,4},{4,5},{5,6},{6,7},{7,8},{8,9},{9,10},{10,1... | collective-permute-start | bytes 1474568 | tf_op jit(solution)/shard_map/ppermute | solution.py:30
  173.4 14.9 %collective-permute-start.14 = (bf16[4,48,1280]{2,1,0:T(8,128)(2,1)S(1)}, bf16[4,48,1280]{2,1,0:T(8,128)(2,1)S(1)}, u32[]{:S(2)}, u32[]{:S(2)}) collective-permute-start(bf16[4,48,1280]{2,1,0:T(8,128)(2,1)S(1)} %constant_dynamic-update-slice_fusion), channel_id=1, source_target_pairs={{0,11},{1,0},{2,1},{3,2},{4,3},{5,4},{6,5},{7,6},{8,7},{9,8},{10,9... | collective-permute-start | bytes 1474568 | tf_op jit(solution)/shard_map/ppermute | solution.py:30
Sparse Core Ops, SparseCore 0:
  10.8 57.9 all-gather.1
  77.5 50.4 reduce-scatter.4
  149.5 23.0 reduce-scatter.2

commit v4 on v2

v4 whole, which is shorter than its diff:
```python
import math

import jax
import jax.numpy as jnp
from jax import lax
from jax.sharding import PartitionSpec as P

NY = 8
NZ = 12
F32 = jnp.float32
BF16 = jnp.bfloat16

Y_RINGS = [[h * NY + y for y in range(NY)] for h in range(2)]
X_PAIRS = [[y, y + NY] for y in range(NY)]
X_SWAP = [(i, (i + NY) % (2 * NY)) for i in range(2 * NY)]


def z_shift(step):
    return [(z, (z + step) % NZ) for z in range(NZ)]


def over_rep(value, pairs):
    return lax.ppermute(value, "rep", pairs)


def over_col(value, step):
    return lax.ppermute(value, "col", z_shift(step))


def near_two(value):
    pairs = []
    for row in range(4):
        step = 2 - 4 * (row % 2)
        pairs += [(row * NZ + z, row * NZ + (z + step) % NZ) for z in range(NZ)]
    return lax.ppermute(value, ("row", "col"), pairs)


def add(*terms):
    total = terms[0].astype(F32)
    for term in terms[1:]:
        total = total + term.astype(F32)
    return total.astype(BF16)


def gather_weight(w0):
    pair = lax.all_gather(w0, "rep", axis=0, tiled=True, axis_index_groups=X_PAIRS)
    whole = lax.all_gather(pair, "rep", axis=1, tiled=True, axis_index_groups=Y_RINGS)
    return whole.reshape(-1, w0.shape[2])


def scatter_wgrad(normed, masked, factor, first):
    half = normed.shape[1] // 2
    left, right = normed[:, :half], normed[:, half:]

    def product(columns):
        value = lax.dot_general(
            columns, masked, (((0,), (0,)), ((), ())), preferred_element_type=F32
        )
        return (value * factor).astype(BF16)

    came = over_rep(product(jnp.where(first, right, left)), X_SWAP)
    both = add(product(jnp.where(first, left, right)), came)
    return lax.psum_scatter(
        both, "rep", scatter_dimension=0, tiled=True, axis_index_groups=Y_RINGS
    )


def sum_over_col(partial, z):
    def residue(step):
        return lax.rem(z + step + NZ, 4)

    def near(pieces):
        return (
            near_two(pieces[0]),
            over_col(pieces[1], 1),
            over_col(pieces[2], -1),
        )

    arrived = near((partial(residue(2)), partial(residue(1)), partial(residue(-1))))
    three = add(partial(residue(0)), *arrived)
    below = over_col(three, 4)
    above = over_col(three, -4)
    q = z // 4
    last = jnp.where(q == 0, below, jnp.where(q == 1, above, three))
    one = jnp.where(q == 0, three, below)
    two = jnp.where(q == 1, three, above)
    total = add(one, two, last)
    arrived = near((total, total, total))
    result = jnp.zeros((3, 4) + total.shape[1:], total.dtype)
    for step, value in ((0, total), (2, arrived[0]), (-1, arrived[1]), (1, arrived[2])):
        result = lax.dynamic_update_slice(result, value[:, None], (0, residue(step), 0, 0))
    return result.reshape(-1, total.shape[2])


def body(normed, up_weight, cotangent, lengths):
    row_count, width = normed.shape
    pair_count = lengths.shape[0]
    pair_len = row_count // pair_count
    keep_rows, unit_count = up_weight.shape[1:]
    first = lax.axis_index("rep") < NY
    z = lax.axis_index("col")

    weight = gather_weight(up_weight)

    positions = lax.broadcasted_iota(jnp.int32, (pair_count, pair_len), 1)
    valid_rows = (positions < lengths[:, None]).reshape(row_count, 1)
    masked = jnp.where(valid_rows, cotangent, jnp.zeros_like(cotangent))

    factor = 1.0 / math.sqrt(row_count * lax.axis_size("rep"))
    weight_grad = scatter_wgrad(normed, masked, factor, first)
    weight_grad = weight_grad.reshape(1, keep_rows, unit_count)

    unit_rows = -(-row_count // (NZ * 16)) * 16
    padded = jnp.pad(masked, ((0, NZ * unit_rows - row_count), (0, 0)))
    units = padded.reshape(3, 4, unit_rows, unit_count)

    def partial_grad(residue):
        tokens = lax.dynamic_index_in_dim(units, residue, 1, keepdims=False)
        value = lax.dot_general(
            tokens.reshape(-1, unit_count),
            weight,
            (((1,), (1,)), ((), ())),
            preferred_element_type=F32,
        )
        return value.astype(BF16).reshape(3, unit_rows, width)

    normed_grad = sum_over_col(partial_grad, z)[:row_count]

    up_partial = jnp.dot(normed, weight, preferred_element_type=F32)
    up_out = lax.psum_scatter(
        up_partial.astype(BF16), "row", scatter_dimension=0, tiled=True
    )
    return (up_out, normed_grad, weight_grad)


def solution(mesh):
    placed = (P("rep", "row"), P("row", "rep", "col"), P("rep", "col"), P("rep"))
    return jax.shard_map(
        body,
        mesh=mesh,
        in_specs=placed,
        out_specs=(P(("rep", "row"), "col"), P("rep", "row"), P("row", "rep", "col")),
        check_vma=False,
    )
```

time: 188 us -> 176 us (0.936)
  the two profiles are of different devices: /device:TPU:4 before, /device:TPU:6 now
where the time goes in v4:
time: 176 us; the launch traced here: 175 us
  waiting for transfers between devices  91 us (52%)
  starting transfers between devices  43.9 us (25%)
  between operations  14.8 us (8%)
  matrix products  12 us (7%)
  blocking collectives  9.31 us (5%)
  other arithmetic  1.93 us (1%)
    ppermute x6, waiting for transfers between devices, over_col(): return lax.ppermute(value, 'col', z_shift(step))  39 us
    ppermute x1, waiting for transfers between devices, over_rep(): return lax.ppermute(value, 'rep', pairs)  32.8 us
    ppermute x6, starting transfers between devices, over_col(): return lax.ppermute(value, 'col', z_shift(step))  27.6 us
    all_gather x1, waiting for transfers between devices, gather_weight(): lax.all_gather(pair, 'rep', axis=1, tiled=True, axis_index_groups=Y_RINGS)  12.9 us
    ppermute x2, starting transfers between devices, near_two(): return lax.ppermute(value, ('row', 'col'), pairs)  12.1 us
    all_gather x1, blocking collectives, gather_weight(): lax.all_gather(w0, 'rep', axis=0, tiled=True, axis_index_groups=X_PAIRS)  9.31 us
    ppermute x2, waiting for transfers between devices, near_two(): return lax.ppermute(value, ('row', 'col'), pairs)  6.32 us
    dot_general x4, matrix products, partial_grad(): lax.dot_general(tokens.reshape(-1, unit_count), weight, (((1,), (1,)), ((...  5.84 us
  transfers between devices with their start and end apart: 12, of which 7 were waited for; matrix products, arithmetic and copies ran while one was open for 9% of the time, Pallas kernels for 0%

profile of v4, /device:TPU:6, one launch (start us, length us, event | category | flops | bytes accessed | tf_op | source)
XLA Modules:
  0.0 174.5 jit_solution(17555933091753946537)
XLA Ops:
  7.2 9.3 %all_gather.6 = bf16[2,80,1152]{2,1,0:T(8,128)(2,1)} all-gather(bf16[1,80,1152]{2,1,0:T(8,128)(2,1)} %param.5), channel_id=1, replica_groups={{0,384},{48,432},{96,480},{144,528},{192,576},{240,624},{288,672},{336,..., dimensions={0}, use_global_device_ids=true | all-gather | bytes 552960 | tf_op jit(solution)/shard_map/all_gather | solution.py:46
  17.4 1.5 broadcast_select_fusion
  18.8 1.1 fusion.2
  19.9 4.1 %collective-permute-start.8 = (bf16[640,1152]{1,0:T(8,128)(2,1)S(1)}, bf16[640,1152]{1,0:T(8,128)(2,1)S(1)}, u32[]{:S(2)}, u32[]{:S(2)}) collective-permute-start(bf16[640,1152]{1,0:T(8,128)(2,1)S(1)} %fusion.2), channel_id=1, source_target_pairs={{0,384},{48,432},{96,480},{144,528},{192,576},{240,624},{288,672},... | collective-permute-start | bytes 4423688 | tf_op jit(solution)/shard_map/ppermute | solution.py:23
  24.0 32.8 %collective-permute-done.8 = bf16[640,1152]{1,0:T(8,128)(2,1)S(1)} collective-permute-done((bf16[640,1152]{1,0:T(8,128)(2,1)S(1)}, bf16[640,1152]{1,0:T(8,128)(2,1)S(1)}, u32[]{:S(2)}, u32[]{:S(2)}) %collective-permute-start.8) | collective-permute-done | bytes 1474592 | tf_op jit(solution)/shard_map/ppermute | solution.py:23
  56.8 2.2 %add_convert_fusion = bf16[640,1152]{1,0:T(8,128)(2,1)} fusion(bf16[640,1152]{1,0:T(8,128)(2,1)S(1)} %collective-permute-done.8, bf16[512,1152]{1,0:T(8,128)(2,1)S(1)} %broadcast_select_fusion, pred[]{:T(512)S(6)} %lt.43, bf16[512,1280]{1,0:T(8,128)(2,1)S(1)} %copy-done.1), kind=kOutput, calls=%fused_computation.6 | convolution fusion | flops 759726080 | bytes 5439489 | tf_op jit(solution)/shard_map/dot_general | solution.py:56
  59.0 0.0 reduce-scatter.3.cloned.1.call-start
  59.1 0.1 pad.4
  59.2 0.1 constant_dynamic-slice_fusion.2
  59.3 12.9 %all-gather.2.cloned.1.call-done = bf16[2,640,1152]{2,1,0:T(8,128)(2,1)} async-done(((bf16[2,80,1152]{2,1,0:T(8,128)(2,1)}), bf16[2,640,1152]{2,1,0:T(8,128)(2,1)}) %all-gather.2.cloned.1.call-update) | async-done | bytes 2949136 | tf_op jit(solution)/shard_map/all_gather | solution.py:47
  72.2 2.9 %convolution_convert_fusion.2 = bf16[144,1280]{1,0:T(8,128)(2,1)S(1)} fusion(bf16[144,1152]{1,0:T(8,128)(2,1)S(1)} %bitcast.54, bf16[1280,1152]{1,0:T(8,128)(2,1)} %bitcast.43), kind=kOutput, calls=%fused_computation.8 | convolution fusion | flops 424857600 | bytes 3649536 | tf_op jit(solution)/shard_map/dot_general | solution.py:119
  75.2 3.6 %collective-permute-start.1 = (bf16[3,48,1280]{2,1,0:T(8,128)(2,1)S(1)}, bf16[3,48,1280]{2,1,0:T(8,128)(2,1)S(1)}, u32[]{:S(2)}, u32[]{:S(2)}) collective-permute-start(bf16[3,48,1280]{2,1,0:T(8,128)(2,1)S(1)} %bitcast.56), channel_id=1, source_target_pairs={{0,1},{1,2},{2,3},{3,4},{4,5},{5,6},{6,7},{7,8},{8,9},{9,10},{10,1... | collective-permute-start | bytes 1105928 | tf_op jit(solution)/shard_map/ppermute | solution.py:27
  78.8 1.0 convolution_convert_fusion.1
  79.7 1.0 convolution_convert_fusion.3
  80.7 4.6 %collective-permute-start = (bf16[3,48,1280]{2,1,0:T(8,128)(2,1)S(1)}, bf16[3,48,1280]{2,1,0:T(8,128)(2,1)S(1)}, u32[]{:S(2)}, u32[]{:S(2)}) collective-permute-start(bf16[3,48,1280]{2,1,0:T(8,128)(2,1)S(1)} %bitcast.57), channel_id=1, source_target_pairs={{0,2},{1,3},{2,4},{3,5},{4,6},{5,7},{6,8},{7,9},{8,10},{9,11},{10,... | collective-permute-start | bytes 1105928 | tf_op jit(solution)/shard_map/ppermute | solution.py:35
  85.3 3.6 %collective-permute-start.2 = (bf16[3,48,1280]{2,1,0:T(8,128)(2,1)S(1)}, bf16[3,48,1280]{2,1,0:T(8,128)(2,1)S(1)}, u32[]{:S(2)}, u32[]{:S(2)}) collective-permute-start(bf16[3,48,1280]{2,1,0:T(8,128)(2,1)S(1)} %bitcast.55), channel_id=1, source_target_pairs={{0,11},{1,0},{2,1},{3,2},{4,3},{5,4},{6,5},{7,6},{8,7},{9,8},{10,9... | collective-permute-start | bytes 1105928 | tf_op jit(solution)/shard_map/ppermute | solution.py:27
  88.9 1.0 convolution_convert_fusion.4
  89.9 6.3 %collective-permute-done = bf16[3,48,1280]{2,1,0:T(8,128)(2,1)S(1)} collective-permute-done((bf16[3,48,1280]{2,1,0:T(8,128)(2,1)S(1)}, bf16[3,48,1280]{2,1,0:T(8,128)(2,1)S(1)}, u32[]{:S(2)}, u32[]{:S(2)}) %collective-permute-start) | collective-permute-done | bytes 368672 | tf_op jit(solution)/shard_map/ppermute | solution.py:35
  96.2 3.4 %collective-permute-done.2 = bf16[3,48,1280]{2,1,0:T(8,128)(2,1)S(1)} collective-permute-done((bf16[3,48,1280]{2,1,0:T(8,128)(2,1)S(1)}, bf16[3,48,1280]{2,1,0:T(8,128)(2,1)S(1)}, u32[]{:S(2)}, u32[]{:S(2)}) %collective-permute-start.2) | collective-permute-done | bytes 368672 | tf_op jit(solution)/shard_map/ppermute | solution.py:27
  99.6 0.2 fusion.5
  99.8 7.0 %collective-permute-start.4 = (bf16[3,48,1280]{2,1,0:T(8,128)(2,1)S(1)}, bf16[3,48,1280]{2,1,0:T(8,128)(2,1)S(1)}, u32[]{:S(2)}, u32[]{:S(2)}) collective-permute-start(bf16[3,48,1280]{2,1,0:T(8,128)(2,1)S(1)} %fusion.5), channel_id=1, source_target_pairs={{0,8},{1,9},{2,10},{3,11},{4,0},{5,1},{6,2},{7,3},{8,4},{9,5},{10,... | collective-permute-start | bytes 1105928 | tf_op jit(solution)/shard_map/ppermute | solution.py:27
  106.8 3.0 %collective-permute-start.3 = (bf16[3,48,1280]{2,1,0:T(8,128)(2,1)S(1)}, bf16[3,48,1280]{2,1,0:T(8,128)(2,1)S(1)}, u32[]{:S(2)}, u32[]{:S(2)}) collective-permute-start(bf16[3,48,1280]{2,1,0:T(8,128)(2,1)S(1)} %fusion.5), channel_id=1, source_target_pairs={{0,4},{1,5},{2,6},{3,7},{4,8},{5,9},{6,10},{7,11},{8,0},{9,1},{10,... | collective-permute-start | bytes 1105928 | tf_op jit(solution)/shard_map/ppermute | solution.py:27
  109.8 2.9 %convolution_convert_fusion = bf16[512,1152]{1,0:T(8,128)(2,1)} fusion(bf16[512,1280]{1,0:T(8,128)(2,1)S(1)} %copy-done.2, bf16[1280,1152]{1,0:T(8,128)(2,1)S(1)} %bitcast.47), kind=kOutput, calls=%fused_computation.5 | convolution fusion | flops 1510539264 | bytes 5439488 | tf_op jit(solution)/shard_map/dot_general | solution.py:129
  112.8 24.9 %collective-permute-done.4 = bf16[3,48,1280]{2,1,0:T(8,128)(2,1)S(1)} collective-permute-done((bf16[3,48,1280]{2,1,0:T(8,128)(2,1)S(1)}, bf16[3,48,1280]{2,1,0:T(8,128)(2,1)S(1)}, u32[]{:S(2)}, u32[]{:S(2)}) %collective-permute-start.4) | collective-permute-done | bytes 368672 | tf_op jit(solution)/shard_map/ppermute | solution.py:27
  137.6 0.1 broadcast_in_dim.27
  137.7 0.3 bitcast_dynamic-update-slice_fusion.3
  138.0 7.5 %collective-permute-start.5 = (bf16[3,48,1280]{2,1,0:T(8,128)(2,1)S(1)}, bf16[3,48,1280]{2,1,0:T(8,128)(2,1)S(1)}, u32[]{:S(2)}, u32[]{:S(2)}) collective-permute-start(bf16[3,48,1280]{2,1,0:T(8,128)(2,1)S(1)} %get-tuple-element.4), channel_id=1, source_target_pairs={{0,2},{1,3},{2,4},{3,5},{4,6},{5,7},{6,8},{7,9},{8,10},{9,11},{10,... | collective-permute-start | bytes 1105928 | tf_op jit(solution)/shard_map/ppermute | solution.py:35
  145.5 8.2 %collective-permute-start.6 = (bf16[3,48,1280]{2,1,0:T(8,128)(2,1)S(1)}, bf16[3,48,1280]{2,1,0:T(8,128)(2,1)S(1)}, u32[]{:S(2)}, u32[]{:S(2)}) collective-permute-start(bf16[3,48,1280]{2,1,0:T(8,128)(2,1)S(1)} %get-tuple-element.4), channel_id=1, source_target_pairs={{0,1},{1,2},{2,3},{3,4},{4,5},{5,6},{6,7},{7,8},{8,9},{9,10},{10,1... | collective-permute-start | bytes 1105928 | tf_op jit(solution)/shard_map/ppermute | solution.py:27
  153.7 2.3 %collective-permute-start.7 = (bf16[3,48,1280]{2,1,0:T(8,128)(2,1)S(1)}, bf16[3,48,1280]{2,1,0:T(8,128)(2,1)S(1)}, u32[]{:S(2)}, u32[]{:S(2)}) collective-permute-start(bf16[3,48,1280]{2,1,0:T(8,128)(2,1)S(1)} %get-tuple-element.4), channel_id=1, source_target_pairs={{0,11},{1,0},{2,1},{3,2},{4,3},{5,4},{6,5},{7,6},{8,7},{9,8},{10,9... | collective-permute-start | bytes 1105928 | tf_op jit(solution)/shard_map/ppermute | solution.py:27
  156.1 9.5 %collective-permute-done.6 = bf16[3,48,1280]{2,1,0:T(8,128)(2,1)S(1)} collective-permute-done((bf16[3,48,1280]{2,1,0:T(8,128)(2,1)S(1)}, bf16[3,48,1280]{2,1,0:T(8,128)(2,1)S(1)}, u32[]{:S(2)}, u32[]{:S(2)}) %collective-permute-start.6) | collective-permute-done | bytes 368672 | tf_op jit(solution)/shard_map/ppermute | solution.py:27
  165.6 1.2 collective-permute-done.7
  166.9 1.1 slice.12
  (20 shorter events, 0.2 us)
Async XLA Ops:
  7.2 65.1 %all-gather.2.cloned.1.call-start = ((), (), s32[]{:S(2)}) async-start(), calls=%async_computation.2 | async-start | bytes 3317760 | tf_op jit(solution)/shard_map/all_gather | solution.py:47
  16.5 2.3 %copy-start.1 = (bf16[512,1280]{1,0:T(8,128)(2,1)S(1)}, bf16[512,1280]{1,0:T(8,128)(2,1)}, u32[]{:S(2)}) copy-start(bf16[512,1280]{1,0:T(8,128)(2,1)} %param.4) | copy-start | bytes 3932164
  16.5 151.5 %reduce-scatter.5.cloned.1.call-start = ((), (), s32[]{:S(2)}) async-start(), calls=%async_computation.4 | async-start | bytes 1658880 | tf_op jit(solution)/shard_map/reduce_scatter | solution.py:63
  19.9 36.9 %collective-permute-start.8 = (bf16[640,1152]{1,0:T(8,128)(2,1)S(1)}, bf16[640,1152]{1,0:T(8,128)(2,1)S(1)}, u32[]{:S(2)}, u32[]{:S(2)}) collective-permute-start(bf16[640,1152]{1,0:T(8,128)(2,1)S(1)} %fusion.2), channel_id=1, source_target_pairs={{0,384},{48,432},{96,480},{144,528},{192,576},{240,624},{288,672},... | collective-permute-start | bytes 4423688 | tf_op jit(solution)/shard_map/ppermute | solution.py:23
  59.0 109.0 %reduce-scatter.3.cloned.1.call-start = ((), (), s32[]{:S(2)}) async-start(), calls=%async_computation.3 | async-start | bytes 1474560 | tf_op jit(solution)/shard_map/reduce_scatter | solution.py:130
  72.2 6.5 %copy-start = (bf16[2,640,1152]{2,1,0:T(8,128)(2,1)S(1)}, bf16[2,640,1152]{2,1,0:T(8,128)(2,1)}, u32[]{:S(2)}) copy-start(bf16[2,640,1152]{2,1,0:T(8,128)(2,1)} %all-gather.2.cloned.1.call-done) | copy-start | bytes 8847364
  75.2 14.7 %collective-permute-start.1 = (bf16[3,48,1280]{2,1,0:T(8,128)(2,1)S(1)}, bf16[3,48,1280]{2,1,0:T(8,128)(2,1)S(1)}, u32[]{:S(2)}, u32[]{:S(2)}) collective-permute-start(bf16[3,48,1280]{2,1,0:T(8,128)(2,1)S(1)} %bitcast.56), channel_id=1, source_target_pairs={{0,1},{1,2},{2,3},{3,4},{4,5},{5,6},{6,7},{7,8},{8,9},{9,10},{10,1... | collective-permute-start | bytes 1105928 | tf_op jit(solution)/shard_map/ppermute | solution.py:27
  80.7 15.5 %collective-permute-start = (bf16[3,48,1280]{2,1,0:T(8,128)(2,1)S(1)}, bf16[3,48,1280]{2,1,0:T(8,128)(2,1)S(1)}, u32[]{:S(2)}, u32[]{:S(2)}) collective-permute-start(bf16[3,48,1280]{2,1,0:T(8,128)(2,1)S(1)} %bitcast.57), channel_id=1, source_target_pairs={{0,2},{1,3},{2,4},{3,5},{4,6},{5,7},{6,8},{7,9},{8,10},{9,11},{10,... | collective-permute-start | bytes 1105928 | tf_op jit(solution)/shard_map/ppermute | solution.py:35
  85.3 14.3 %collective-permute-start.2 = (bf16[3,48,1280]{2,1,0:T(8,128)(2,1)S(1)}, bf16[3,48,1280]{2,1,0:T(8,128)(2,1)S(1)}, u32[]{:S(2)}, u32[]{:S(2)}) collective-permute-start(bf16[3,48,1280]{2,1,0:T(8,128)(2,1)S(1)} %bitcast.55), channel_id=1, source_target_pairs={{0,11},{1,0},{2,1},{3,2},{4,3},{5,4},{6,5},{7,6},{8,7},{9,8},{10,9... | collective-permute-start | bytes 1105928 | tf_op jit(solution)/shard_map/ppermute | solution.py:27
  89.9 19.9 %copy-start.2 = (bf16[512,1280]{1,0:T(8,128)(2,1)S(1)}, bf16[512,1280]{1,0:T(8,128)(2,1)}, u32[]{:S(2)}) copy-start(bf16[512,1280]{1,0:T(8,128)(2,1)} %param.4) | copy-start | bytes 3932164
  99.8 37.8 %collective-permute-start.4 = (bf16[3,48,1280]{2,1,0:T(8,128)(2,1)S(1)}, bf16[3,48,1280]{2,1,0:T(8,128)(2,1)S(1)}, u32[]{:S(2)}, u32[]{:S(2)}) collective-permute-start(bf16[3,48,1280]{2,1,0:T(8,128)(2,1)S(1)} %fusion.5), channel_id=1, source_target_pairs={{0,8},{1,9},{2,10},{3,11},{4,0},{5,1},{6,2},{7,3},{8,4},{9,5},{10,... | collective-permute-start | bytes 1105928 | tf_op jit(solution)/shard_map/ppermute | solution.py:27
  106.8 30.8 %collective-permute-start.3 = (bf16[3,48,1280]{2,1,0:T(8,128)(2,1)S(1)}, bf16[3,48,1280]{2,1,0:T(8,128)(2,1)S(1)}, u32[]{:S(2)}, u32[]{:S(2)}) collective-permute-start(bf16[3,48,1280]{2,1,0:T(8,128)(2,1)S(1)} %fusion.5), channel_id=1, source_target_pairs={{0,4},{1,5},{2,6},{3,7},{4,8},{5,9},{6,10},{7,11},{8,0},{9,1},{10,... | collective-permute-start | bytes 1105928 | tf_op jit(solution)/shard_map/ppermute | solution.py:27
  138.0 18.1 %collective-permute-start.5 = (bf16[3,48,1280]{2,1,0:T(8,128)(2,1)S(1)}, bf16[3,48,1280]{2,1,0:T(8,128)(2,1)S(1)}, u32[]{:S(2)}, u32[]{:S(2)}) collective-permute-start(bf16[3,48,1280]{2,1,0:T(8,128)(2,1)S(1)} %get-tuple-element.4), channel_id=1, source_target_pairs={{0,2},{1,3},{2,4},{3,5},{4,6},{5,7},{6,8},{7,9},{8,10},{9,11},{10,... | collective-permute-start | bytes 1105928 | tf_op jit(solution)/shard_map/ppermute | solution.py:35
  145.5 20.1 %collective-permute-start.6 = (bf16[3,48,1280]{2,1,0:T(8,128)(2,1)S(1)}, bf16[3,48,1280]{2,1,0:T(8,128)(2,1)S(1)}, u32[]{:S(2)}, u32[]{:S(2)}) collective-permute-start(bf16[3,48,1280]{2,1,0:T(8,128)(2,1)S(1)} %get-tuple-element.4), channel_id=1, source_target_pairs={{0,1},{1,2},{2,3},{3,4},{4,5},{5,6},{6,7},{7,8},{8,9},{9,10},{10,1... | collective-permute-start | bytes 1105928 | tf_op jit(solution)/shard_map/ppermute | solution.py:27
  153.7 13.1 %collective-permute-start.7 = (bf16[3,48,1280]{2,1,0:T(8,128)(2,1)S(1)}, bf16[3,48,1280]{2,1,0:T(8,128)(2,1)S(1)}, u32[]{:S(2)}, u32[]{:S(2)}) collective-permute-start(bf16[3,48,1280]{2,1,0:T(8,128)(2,1)S(1)} %get-tuple-element.4), channel_id=1, source_target_pairs={{0,11},{1,0},{2,1},{3,2},{4,3},{5,4},{6,5},{7,6},{8,7},{9,8},{10,9... | collective-permute-start | bytes 1105928 | tf_op jit(solution)/shard_map/ppermute | solution.py:27
Sparse Core Ops, SparseCore 0:
  16.7 55.5 all-gather.1
  75.9 44.0 reduce-scatter.4
  123.7 27.5 reduce-scatter.2

commit v5 on v4

--- a/solution.py
+++ b/solution.py
@@ -77,19 +77,19 @@
         )
 
     arrived = near((partial(residue(2)), partial(residue(1)), partial(residue(-1))))
-    three = add(partial(residue(0)), *arrived)
-    below = over_col(three, 4)
-    above = over_col(three, -4)
+    mine = add(partial(residue(0)), *arrived)
+    below = over_col(mine, 4)
+    above = over_col(mine, -4)
     q = z // 4
-    last = jnp.where(q == 0, below, jnp.where(q == 1, above, three))
-    one = jnp.where(q == 0, three, below)
-    two = jnp.where(q == 1, three, above)
+    last = jnp.where(q == 0, below, jnp.where(q == 1, above, mine))
+    one = jnp.where(q == 0, mine, below)
+    two = jnp.where(q == 1, mine, above)
     total = add(one, two, last)
     arrived = near((total, total, total))
-    result = jnp.zeros((3, 4) + total.shape[1:], total.dtype)
+    result = jnp.zeros((4,) + total.shape, total.dtype)
     for step, value in ((0, total), (2, arrived[0]), (-1, arrived[1]), (1, arrived[2])):
-        result = lax.dynamic_update_slice(result, value[:, None], (0, residue(step), 0, 0))
-    return result.reshape(-1, total.shape[2])
+        result = lax.dynamic_update_slice(result, value[None], (residue(step), 0, 0))
+    return result.reshape(-1, total.shape[1])
 
 
 def body(normed, up_weight, cotangent, lengths):
@@ -110,21 +110,16 @@
     weight_grad = scatter_wgrad(normed, masked, factor, first)
     weight_grad = weight_grad.reshape(1, keep_rows, unit_count)
 
-    unit_rows = -(-row_count // (NZ * 16)) * 16
-    padded = jnp.pad(masked, ((0, NZ * unit_rows - row_count), (0, 0)))
-    units = padded.reshape(3, 4, unit_rows, unit_count)
+    quarters = masked.reshape(4, row_count // 4, unit_count)
 
-    def partial_grad(residue):
-        tokens = lax.dynamic_index_in_dim(units, residue, 1, keepdims=False)
+    def partial_grad(quarter):
+        tokens = lax.dynamic_index_in_dim(quarters, quarter, 0, keepdims=False)
         value = lax.dot_general(
-            tokens.reshape(-1, unit_count),
-            weight,
-            (((1,), (1,)), ((), ())),
-            preferred_element_type=F32,
+            tokens, weight, (((1,), (1,)), ((), ())), preferred_element_type=F32
         )
-        return value.astype(BF16).reshape(3, unit_rows, width)
+        return value.astype(BF16)
 
-    normed_grad = sum_over_col(partial_grad, z)[:row_count]
+    normed_grad = sum_over_col(partial_grad, z)
 
     up_partial = jnp.dot(normed, weight, preferred_element_type=F32)
     up_out = lax.psum_scatter(

time: 176 us -> 177 us (level)
  the two profiles are of different devices: /device:TPU:6 before, /device:TPU:12 now
where the time goes in v5:
time: 177 us
  waiting for transfers between devices  95.8 us (54%)
  starting transfers between devices  35.9 us (20%)
  matrix products  17.5 us (10%)
  between operations  14.8 us (8%)
  blocking collectives  8.88 us (5%)
  other arithmetic  2.77 us (2%)
    ppermute x6, waiting for transfers between devices, over_col(): return lax.ppermute(value, 'col', z_shift(step))  39.2 us
    ppermute x1, waiting for transfers between devices, over_rep(): return lax.ppermute(value, 'rep', pairs)  32.1 us
    ppermute x6, starting transfers between devices, over_col(): return lax.ppermute(value, 'col', z_shift(step))  24.8 us
    all_gather x1, waiting for transfers between devices, gather_weight(): lax.all_gather(pair, 'rep', axis=1, tiled=True, axis_index_groups=Y_RINGS)  13.5 us
    dot_general x4, matrix products, partial_grad(): lax.dot_general(tokens, weight, (((1,), (1,)), ((), ())), preferred_eleme...  11.3 us
    ppermute x2, waiting for transfers between devices, near_two(): return lax.ppermute(value, ('row', 'col'), pairs)  10.9 us
    all_gather x1, blocking collectives, gather_weight(): lax.all_gather(w0, 'rep', axis=0, tiled=True, axis_index_groups=X_PAIRS)  8.88 us
    ppermute x2, starting transfers between devices, near_two(): return lax.ppermute(value, ('row', 'col'), pairs)  6.55 us
  transfers between devices with their start and end apart: 12, of which 8 were waited for; matrix products, arithmetic and copies ran while one was open for 12% of the time, Pallas kernels for 0%

profile of v5, /device:TPU:12, one launch (start us, length us, event | category | flops | bytes accessed | tf_op | source)
XLA Modules:
  0.0 176.8 jit_solution(5629436766151950773)
XLA Ops:
  7.2 0.0 all-gather.2.cloned.1.call-start
  7.2 8.9 %all_gather.6 = bf16[2,80,1152]{2,1,0:T(8,128)(2,1)} all-gather(bf16[1,80,1152]{2,1,0:T(8,128)(2,1)} %param.5), channel_id=1, replica_groups={{0,384},{48,432},{96,480},{144,528},{192,576},{240,624},{288,672},{336,..., dimensions={0}, use_global_device_ids=true | all-gather | bytes 552960 | tf_op jit(solution)/shard_map/all_gather | solution.py:46
  16.1 0.0 reduce-scatter.5.cloned.1.call-start
  16.9 1.5 broadcast_select_fusion
  18.4 1.1 fusion.2
  19.5 4.5 %collective-permute-start.8 = (bf16[640,1152]{1,0:T(8,128)(2,1)S(1)}, bf16[640,1152]{1,0:T(8,128)(2,1)S(1)}, u32[]{:S(2)}, u32[]{:S(2)}) collective-permute-start(bf16[640,1152]{1,0:T(8,128)(2,1)S(1)} %fusion.2), channel_id=1, source_target_pairs={{0,384},{48,432},{96,480},{144,528},{192,576},{240,624},{288,672},... | collective-permute-start | bytes 4423688 | tf_op jit(solution)/shard_map/ppermute | solution.py:23
  24.0 32.1 %collective-permute-done.8 = bf16[640,1152]{1,0:T(8,128)(2,1)S(1)} collective-permute-done((bf16[640,1152]{1,0:T(8,128)(2,1)S(1)}, bf16[640,1152]{1,0:T(8,128)(2,1)S(1)}, u32[]{:S(2)}, u32[]{:S(2)}) %collective-permute-start.8) | collective-permute-done | bytes 1474592 | tf_op jit(solution)/shard_map/ppermute | solution.py:23
  56.0 2.2 %add_convert_fusion = bf16[640,1152]{1,0:T(8,128)(2,1)} fusion(bf16[640,1152]{1,0:T(8,128)(2,1)S(1)} %collective-permute-done.8, bf16[512,1152]{1,0:T(8,128)(2,1)S(1)} %broadcast_select_fusion, pred[]{:T(512)S(6)} %lt.43, bf16[512,1280]{1,0:T(8,128)(2,1)S(1)} %copy-done.4), kind=kOutput, calls=%fused_computation.6 | convolution fusion | flops 759726080 | bytes 5439489 | tf_op jit(solution)/shard_map/dot_general | solution.py:56
  58.3 0.0 reduce-scatter.3.cloned.1.call-start
  58.4 13.5 %all-gather.2.cloned.1.call-done = bf16[2,640,1152]{2,1,0:T(8,128)(2,1)} async-done(((bf16[2,80,1152]{2,1,0:T(8,128)(2,1)}), bf16[2,640,1152]{2,1,0:T(8,128)(2,1)}) %all-gather.2.cloned.1.call-update) | async-done | bytes 2949136 | tf_op jit(solution)/shard_map/all_gather | solution.py:47
  71.9 3.7 %convolution_convert_fusion.1 = bf16[128,1280]{1,0:T(8,128)(2,1)} fusion(bf16[1280,1152]{1,0:T(8,128)(2,1)} %bitcast.36, bf16[4,128,1152]{2,1,0:T(8,128)(2,1)} %bitcast.41, s32[]{:T(128)S(6)} %select_n.66), kind=kOutput, calls=%fused_computation.7 | convolution fusion | flops 377651200 | bytes 3571716 | tf_op jit(solution)/shard_map/dot_general | solution.py:117
  75.6 2.6 %convolution_convert_fusion.2 = bf16[128,1280]{1,0:T(8,128)(2,1)} fusion(bf16[1280,1152]{1,0:T(8,128)(2,1)S(1)} %bitcast.37, bf16[4,128,1152]{2,1,0:T(8,128)(2,1)} %bitcast.42, s32[]{:T(128)S(6)} %select_n.65), kind=kOutput, calls=%fused_computation.8 | convolution fusion | flops 377651200 | bytes 3571716 | tf_op jit(solution)/shard_map/dot_general | solution.py:117
  78.2 2.6 %convolution_convert_fusion.3 = bf16[128,1280]{1,0:T(8,128)(2,1)} fusion(bf16[1280,1152]{1,0:T(8,128)(2,1)S(1)} %bitcast.38, bf16[4,128,1152]{2,1,0:T(8,128)(2,1)} %bitcast.43, s32[]{:T(128)S(6)} %select_n.64), kind=kOutput, calls=%fused_computation.9 | convolution fusion | flops 377651200 | bytes 3571716 | tf_op jit(solution)/shard_map/dot_general | solution.py:117
  80.9 4.6 %collective-permute-start = (bf16[128,1280]{1,0:T(8,128)(2,1)}, bf16[128,1280]{1,0:T(8,128)(2,1)S(1)}, u32[]{:S(2)}, u32[]{:S(2)}) collective-permute-start(bf16[128,1280]{1,0:T(8,128)(2,1)} %convolution_convert_fusion.3), channel_id=1, source_target_pairs={{0,2},{1,3},{2,4},{3,5},{4,6},{5,7},{6,8},{7,9},{8,10},{9,11},{10,... | collective-permute-start | bytes 983048 | tf_op jit(solution)/shard_map/ppermute | solution.py:35
  85.5 3.8 %collective-permute-start.1 = (bf16[128,1280]{1,0:T(8,128)(2,1)}, bf16[128,1280]{1,0:T(8,128)(2,1)}, u32[]{:S(2)}, u32[]{:S(2)}) collective-permute-start(bf16[128,1280]{1,0:T(8,128)(2,1)} %convolution_convert_fusion.2), channel_id=1, source_target_pairs={{0,1},{1,2},{2,3},{3,4},{4,5},{5,6},{6,7},{7,8},{8,9},{9,10},{10,1... | collective-permute-start | bytes 983048 | tf_op jit(solution)/shard_map/ppermute | solution.py:27
  89.3 3.3 %collective-permute-start.2 = (bf16[128,1280]{1,0:T(8,128)(2,1)}, bf16[128,1280]{1,0:T(8,128)(2,1)}, u32[]{:S(2)}, u32[]{:S(2)}) collective-permute-start(bf16[128,1280]{1,0:T(8,128)(2,1)} %convolution_convert_fusion.1), channel_id=1, source_target_pairs={{0,11},{1,0},{2,1},{3,2},{4,3},{5,4},{6,5},{7,6},{8,7},{9,8},{10,9... | collective-permute-start | bytes 983048 | tf_op jit(solution)/shard_map/ppermute | solution.py:27
  92.6 5.5 %collective-permute-done = bf16[128,1280]{1,0:T(8,128)(2,1)S(1)} collective-permute-done((bf16[128,1280]{1,0:T(8,128)(2,1)}, bf16[128,1280]{1,0:T(8,128)(2,1)S(1)}, u32[]{:S(2)}, u32[]{:S(2)}) %collective-permute-start) | collective-permute-done | bytes 327712 | tf_op jit(solution)/shard_map/ppermute | solution.py:35
  98.2 5.2 %collective-permute-done.1 = bf16[128,1280]{1,0:T(8,128)(2,1)} collective-permute-done((bf16[128,1280]{1,0:T(8,128)(2,1)}, bf16[128,1280]{1,0:T(8,128)(2,1)}, u32[]{:S(2)}, u32[]{:S(2)}) %collective-permute-start.1) | collective-permute-done | bytes 327712 | tf_op jit(solution)/shard_map/ppermute | solution.py:27
  103.4 2.2 %add_convert_fusion.2 = bf16[128,1280]{1,0:T(8,128)(2,1)S(1)} fusion(bf16[128,1280]{1,0:T(8,128)(2,1)} %collective-permute-done.2, bf16[128,1280]{1,0:T(8,128)(2,1)} %collective-permute-done.1, bf16[128,1280]{1,0:T(8,128)(2,1)} %copy-done.3, bf16[1280,1152]{1,0:T(8,128)(2,1)S(1)} %bitcast.39, bf16[4,128,1152]{2,1,0:T(8,128)(2,1)} %bitcast.44, s32[]{:T(128)S(6)} %select_n.63), kind=kOutput, calls=%fused_computation.16 | convolution fusion | flops 378961920 | bytes 4554756 | tf_op jit(solution)/shard_map/dot_general | solution.py:117
  105.6 7.4 %collective-permute-start.4 = (bf16[128,1280]{1,0:T(8,128)(2,1)S(1)}, bf16[128,1280]{1,0:T(8,128)(2,1)}, u32[]{:S(2)}, u32[]{:S(2)}) collective-permute-start(bf16[128,1280]{1,0:T(8,128)(2,1)S(1)} %add_convert_fusion.2), channel_id=1, source_target_pairs={{0,8},{1,9},{2,10},{3,11},{4,0},{5,1},{6,2},{7,3},{8,4},{9,5},{10,... | collective-permute-start | bytes 983048 | tf_op jit(solution)/shard_map/ppermute | solution.py:27
  113.1 2.3 %collective-permute-start.3 = (bf16[128,1280]{1,0:T(8,128)(2,1)S(1)}, bf16[128,1280]{1,0:T(8,128)(2,1)}, u32[]{:S(2)}, u32[]{:S(2)}) collective-permute-start(bf16[128,1280]{1,0:T(8,128)(2,1)S(1)} %add_convert_fusion.2), channel_id=1, source_target_pairs={{0,4},{1,5},{2,6},{3,7},{4,8},{5,9},{6,10},{7,11},{8,0},{9,1},{10,... | collective-permute-start | bytes 983048 | tf_op jit(solution)/shard_map/ppermute | solution.py:27
  115.4 3.0 %convolution_convert_fusion = bf16[512,1152]{1,0:T(8,128)(2,1)} fusion(bf16[512,1280]{1,0:T(8,128)(2,1)S(1)} %copy-done.5, bf16[1280,1152]{1,0:T(8,128)(2,1)S(1)} %bitcast.40), kind=kOutput, calls=%fused_computation.5 | convolution fusion | flops 1510539264 | bytes 5439488 | tf_op jit(solution)/shard_map/dot_general | solution.py:124
  118.4 20.6 %collective-permute-done.4 = bf16[128,1280]{1,0:T(8,128)(2,1)} collective-permute-done((bf16[128,1280]{1,0:T(8,128)(2,1)S(1)}, bf16[128,1280]{1,0:T(8,128)(2,1)}, u32[]{:S(2)}, u32[]{:S(2)}) %collective-permute-start.4) | collective-permute-done | bytes 327712 | tf_op jit(solution)/shard_map/ppermute | solution.py:27
  139.1 7.2 %collective-permute-done.3 = bf16[128,1280]{1,0:T(8,128)(2,1)} collective-permute-done((bf16[128,1280]{1,0:T(8,128)(2,1)S(1)}, bf16[128,1280]{1,0:T(8,128)(2,1)}, u32[]{:S(2)}, u32[]{:S(2)}) %collective-permute-start.3) | collective-permute-done | bytes 327712 | tf_op jit(solution)/shard_map/ppermute | solution.py:27
  146.3 0.1 broadcast_in_dim.27
  146.3 1.3 bitcast_dynamic-update-slice_fusion.3
  147.6 1.9 %collective-permute-start.5 = (bf16[128,1280]{1,0:T(8,128)(2,1)S(1)}, bf16[128,1280]{1,0:T(8,128)(2,1)S(1)}, u32[]{:S(2)}, u32[]{:S(2)}) collective-permute-start(bf16[128,1280]{1,0:T(8,128)(2,1)S(1)} %get-tuple-element.4), channel_id=1, source_target_pairs={{0,2},{1,3},{2,4},{3,5},{4,6},{5,7},{6,8},{7,9},{8,10},{9,11},{10,... | collective-permute-start | bytes 983048 | tf_op jit(solution)/shard_map/ppermute | solution.py:35
  149.6 3.4 %collective-permute-start.6 = (bf16[128,1280]{1,0:T(8,128)(2,1)S(1)}, bf16[128,1280]{1,0:T(8,128)(2,1)S(1)}, u32[]{:S(2)}, u32[]{:S(2)}) collective-permute-start(bf16[128,1280]{1,0:T(8,128)(2,1)S(1)} %get-tuple-element.4), channel_id=1, source_target_pairs={{0,1},{1,2},{2,3},{3,4},{4,5},{5,6},{6,7},{7,8},{8,9},{9,10},{10,1... | collective-permute-start | bytes 983048 | tf_op jit(solution)/shard_map/ppermute | solution.py:27
  153.0 4.6 %collective-permute-start.7 = (bf16[128,1280]{1,0:T(8,128)(2,1)S(1)}, bf16[128,1280]{1,0:T(8,128)(2,1)S(1)}, u32[]{:S(2)}, u32[]{:S(2)}) collective-permute-start(bf16[128,1280]{1,0:T(8,128)(2,1)S(1)} %get-tuple-element.4), channel_id=1, source_target_pairs={{0,11},{1,0},{2,1},{3,2},{4,3},{5,4},{6,5},{7,6},{8,7},{9,8},{10,9... | collective-permute-start | bytes 983048 | tf_op jit(solution)/shard_map/ppermute | solution.py:27
  157.6 5.3 %collective-permute-done.5 = bf16[128,1280]{1,0:T(8,128)(2,1)S(1)} collective-permute-done((bf16[128,1280]{1,0:T(8,128)(2,1)S(1)}, bf16[128,1280]{1,0:T(8,128)(2,1)S(1)}, u32[]{:S(2)}, u32[]{:S(2)}) %collective-permute-start.5) | collective-permute-done | bytes 327712 | tf_op jit(solution)/shard_map/ppermute | solution.py:35
  162.9 6.2 %collective-permute-done.6 = bf16[128,1280]{1,0:T(8,128)(2,1)S(1)} collective-permute-done((bf16[128,1280]{1,0:T(8,128)(2,1)S(1)}, bf16[128,1280]{1,0:T(8,128)(2,1)S(1)}, u32[]{:S(2)}, u32[]{:S(2)}) %collective-permute-start.6) | collective-permute-done | bytes 327712 | tf_op jit(solution)/shard_map/ppermute | solution.py:27
  169.3 1.0 copy-done.2
  (22 shorter events, 0.2 us)
Async XLA Ops:
  7.2 64.7 %all-gather.2.cloned.1.call-start = ((), (), s32[]{:S(2)}) async-start(), calls=%async_computation.2 | async-start | bytes 3317760 | tf_op jit(solution)/shard_map/all_gather | solution.py:47
  16.1 2.3 %copy-start.4 = (bf16[512,1280]{1,0:T(8,128)(2,1)S(1)}, bf16[512,1280]{1,0:T(8,128)(2,1)}, u32[]{:S(2)}) copy-start(bf16[512,1280]{1,0:T(8,128)(2,1)} %param.4) | copy-start | bytes 3932164
  16.1 153.1 %reduce-scatter.5.cloned.1.call-start = ((), (), s32[]{:S(2)}) async-start(), calls=%async_computation.4 | async-start | bytes 1658880 | tf_op jit(solution)/shard_map/reduce_scatter | solution.py:63
  18.4 37.6 %copy-start.1 = (bf16[512,1152]{1,0:T(8,128)(2,1)}, bf16[512,1152]{1,0:T(8,128)(2,1)S(1)}, u32[]{:S(2)}) copy-start(bf16[512,1152]{1,0:T(8,128)(2,1)S(1)} %broadcast_select_fusion) | copy-start | bytes 3538948
  19.5 36.6 %collective-permute-start.8 = (bf16[640,1152]{1,0:T(8,128)(2,1)S(1)}, bf16[640,1152]{1,0:T(8,128)(2,1)S(1)}, u32[]{:S(2)}, u32[]{:S(2)}) collective-permute-start(bf16[640,1152]{1,0:T(8,128)(2,1)S(1)} %fusion.2), channel_id=1, source_target_pairs={{0,384},{48,432},{96,480},{144,528},{192,576},{240,624},{288,672},... | collective-permute-start | bytes 4423688 | tf_op jit(solution)/shard_map/ppermute | solution.py:23
  58.3 111.0 %reduce-scatter.3.cloned.1.call-start = ((), (), s32[]{:S(2)}) async-start(), calls=%async_computation.3 | async-start | bytes 1474560 | tf_op jit(solution)/shard_map/reduce_scatter | solution.py:125
  71.9 3.8 %copy-start = (bf16[2,640,1152]{2,1,0:T(8,128)(2,1)S(1)}, bf16[2,640,1152]{2,1,0:T(8,128)(2,1)}, u32[]{:S(2)}) copy-start(bf16[2,640,1152]{2,1,0:T(8,128)(2,1)} %all-gather.2.cloned.1.call-done) | copy-start | bytes 8847364
  80.9 17.3 %collective-permute-start = (bf16[128,1280]{1,0:T(8,128)(2,1)}, bf16[128,1280]{1,0:T(8,128)(2,1)S(1)}, u32[]{:S(2)}, u32[]{:S(2)}) collective-permute-start(bf16[128,1280]{1,0:T(8,128)(2,1)} %convolution_convert_fusion.3), channel_id=1, source_target_pairs={{0,2},{1,3},{2,4},{3,5},{4,6},{5,7},{6,8},{7,9},{8,10},{9,11},{10,... | collective-permute-start | bytes 983048 | tf_op jit(solution)/shard_map/ppermute | solution.py:35
  85.5 17.8 %collective-permute-start.1 = (bf16[128,1280]{1,0:T(8,128)(2,1)}, bf16[128,1280]{1,0:T(8,128)(2,1)}, u32[]{:S(2)}, u32[]{:S(2)}) collective-permute-start(bf16[128,1280]{1,0:T(8,128)(2,1)} %convolution_convert_fusion.2), channel_id=1, source_target_pairs={{0,1},{1,2},{2,3},{3,4},{4,5},{5,6},{6,7},{7,8},{8,9},{9,10},{10,1... | collective-permute-start | bytes 983048 | tf_op jit(solution)/shard_map/ppermute | solution.py:27
  89.3 14.1 %collective-permute-start.2 = (bf16[128,1280]{1,0:T(8,128)(2,1)}, bf16[128,1280]{1,0:T(8,128)(2,1)}, u32[]{:S(2)}, u32[]{:S(2)}) collective-permute-start(bf16[128,1280]{1,0:T(8,128)(2,1)} %convolution_convert_fusion.1), channel_id=1, source_target_pairs={{0,11},{1,0},{2,1},{3,2},{4,3},{5,4},{6,5},{7,6},{8,7},{9,8},{10,9... | collective-permute-start | bytes 983048 | tf_op jit(solution)/shard_map/ppermute | solution.py:27
  92.6 22.8 %copy-start.5 = (bf16[512,1280]{1,0:T(8,128)(2,1)S(1)}, bf16[512,1280]{1,0:T(8,128)(2,1)}, u32[]{:S(2)}) copy-start(bf16[512,1280]{1,0:T(8,128)(2,1)} %param.4) | copy-start | bytes 3932164
  98.2 5.2 %copy-start.3 = (bf16[128,1280]{1,0:T(8,128)(2,1)}, bf16[128,1280]{1,0:T(8,128)(2,1)S(1)}, u32[]{:S(2)}) copy-start(bf16[128,1280]{1,0:T(8,128)(2,1)S(1)} %collective-permute-done) | copy-start | bytes 983044
  105.6 33.4 %collective-permute-start.4 = (bf16[128,1280]{1,0:T(8,128)(2,1)S(1)}, bf16[128,1280]{1,0:T(8,128)(2,1)}, u32[]{:S(2)}, u32[]{:S(2)}) collective-permute-start(bf16[128,1280]{1,0:T(8,128)(2,1)S(1)} %add_convert_fusion.2), channel_id=1, source_target_pairs={{0,8},{1,9},{2,10},{3,11},{4,0},{5,1},{6,2},{7,3},{8,4},{9,5},{10,... | collective-permute-start | bytes 983048 | tf_op jit(solution)/shard_map/ppermute | solution.py:27
  113.1 33.2 %collective-permute-start.3 = (bf16[128,1280]{1,0:T(8,128)(2,1)S(1)}, bf16[128,1280]{1,0:T(8,128)(2,1)}, u32[]{:S(2)}, u32[]{:S(2)}) collective-permute-start(bf16[128,1280]{1,0:T(8,128)(2,1)S(1)} %add_convert_fusion.2), channel_id=1, source_target_pairs={{0,4},{1,5},{2,6},{3,7},{4,8},{5,9},{6,10},{7,11},{8,0},{9,1},{10,... | collective-permute-start | bytes 983048 | tf_op jit(solution)/shard_map/ppermute | solution.py:27
  147.6 15.3 %collective-permute-start.5 = (bf16[128,1280]{1,0:T(8,128)(2,1)S(1)}, bf16[128,1280]{1,0:T(8,128)(2,1)S(1)}, u32[]{:S(2)}, u32[]{:S(2)}) collective-permute-start(bf16[128,1280]{1,0:T(8,128)(2,1)S(1)} %get-tuple-element.4), channel_id=1, source_target_pairs={{0,2},{1,3},{2,4},{3,5},{4,6},{5,7},{6,8},{7,9},{8,10},{9,11},{10,... | collective-permute-start | bytes 983048 | tf_op jit(solution)/shard_map/ppermute | solution.py:35
  149.6 19.6 %collective-permute-start.6 = (bf16[128,1280]{1,0:T(8,128)(2,1)S(1)}, bf16[128,1280]{1,0:T(8,128)(2,1)S(1)}, u32[]{:S(2)}, u32[]{:S(2)}) collective-permute-start(bf16[128,1280]{1,0:T(8,128)(2,1)S(1)} %get-tuple-element.4), channel_id=1, source_target_pairs={{0,1},{1,2},{2,3},{3,4},{4,5},{5,6},{6,7},{7,8},{8,9},{9,10},{10,1... | collective-permute-start | bytes 983048 | tf_op jit(solution)/shard_map/ppermute | solution.py:27
  153.0 16.2 %collective-permute-start.7 = (bf16[128,1280]{1,0:T(8,128)(2,1)S(1)}, bf16[128,1280]{1,0:T(8,128)(2,1)S(1)}, u32[]{:S(2)}, u32[]{:S(2)}) collective-permute-start(bf16[128,1280]{1,0:T(8,128)(2,1)S(1)} %get-tuple-element.4), channel_id=1, source_target_pairs={{0,11},{1,0},{2,1},{3,2},{4,3},{5,4},{6,5},{7,6},{8,7},{9,8},{10,9... | collective-permute-start | bytes 983048 | tf_op jit(solution)/shard_map/ppermute | solution.py:27
  169.2 1.1 copy-start.2
Sparse Core Ops, SparseCore 0:
  16.2 55.5 all-gather.1
  75.6 43.9 reduce-scatter.4
  123.3 28.0 reduce-scatter.2

commit v6 on v5

--- a/solution.py
+++ b/solution.py
@@ -76,8 +76,8 @@
             over_col(pieces[2], -1),
         )
 
-    arrived = near((partial(residue(2)), partial(residue(1)), partial(residue(-1))))
-    mine = add(partial(residue(0)), *arrived)
+    arrived = near((partial(2), partial(1), partial(-1)))
+    mine = add(partial(0), *arrived)
     below = over_col(mine, 4)
     above = over_col(mine, -4)
     q = z // 4
@@ -112,10 +112,19 @@
 
     quarters = masked.reshape(4, row_count // 4, unit_count)
 
-    def partial_grad(quarter):
-        tokens = lax.dynamic_index_in_dim(quarters, quarter, 0, keepdims=False)
+    turned = lax.optimization_barrier(
+        tuple(
+            lax.dynamic_index_in_dim(quarters, lax.rem(z + s, 4), 0, keepdims=False)
+            for s in range(4)
+        )
+    )
+
+    def partial_grad(step):
         value = lax.dot_general(
-            tokens, weight, (((1,), (1,)), ((), ())), preferred_element_type=F32
+            turned[step % 4],
+            weight,
+            (((1,), (1,)), ((), ())),
+            preferred_element_type=F32,
         )
         return value.astype(BF16)
 

time: 177 us -> 167 us (0.944)
  the two profiles are of different devices: /device:TPU:12 before, /device:TPU:6 now
where the time goes in v6:
time: 167 us; the launch traced here: 166 us
  waiting for transfers between devices  81.8 us (49%)
  starting transfers between devices  44.8 us (27%)
  between operations  14.9 us (9%)
  matrix products  12 us (7%)
  blocking collectives  9.31 us (6%)
  other arithmetic  1.69 us (1%)
    ppermute x1, waiting for transfers between devices, over_rep(): return lax.ppermute(value, 'rep', pairs)  32.8 us
    ppermute x6, waiting for transfers between devices, over_col(): return lax.ppermute(value, 'col', z_shift(step))  32.4 us
    ppermute x6, starting transfers between devices, over_col(): return lax.ppermute(value, 'col', z_shift(step))  28.1 us
    all_gather x1, waiting for transfers between devices, gather_weight(): lax.all_gather(pair, 'rep', axis=1, tiled=True, axis_index_groups=Y_RINGS)  13 us
    ppermute x2, starting transfers between devices, near_two(): return lax.ppermute(value, ('row', 'col'), pairs)  12.5 us
    all_gather x1, blocking collectives, gather_weight(): lax.all_gather(w0, 'rep', axis=0, tiled=True, axis_index_groups=X_PAIRS)  9.31 us
    dot_general x4, matrix products, partial_grad(): lax.dot_general(turned[step % 4], weight, (((1,), (1,)), ((), ())), prefe...  5.82 us
    ppermute x1, starting transfers between devices, over_rep(): return lax.ppermute(value, 'rep', pairs)  4.03 us
  transfers between devices with their start and end apart: 12, of which 9 were waited for; matrix products, arithmetic and copies ran while one was open for 8% of the time, Pallas kernels for 0%

profile of v6, /device:TPU:6, one launch (start us, length us, event | category | flops | bytes accessed | tf_op | source)
XLA Modules:
  0.0 165.7 jit_solution(1742448390134139943)
XLA Ops:
  7.2 9.3 %all_gather.6 = bf16[2,80,1152]{2,1,0:T(8,128)(2,1)} all-gather(bf16[1,80,1152]{2,1,0:T(8,128)(2,1)} %param.5), channel_id=1, replica_groups={{0,384},{48,432},{96,480},{144,528},{192,576},{240,624},{288,672},{336,..., dimensions={0}, use_global_device_ids=true | all-gather | bytes 552960 | tf_op jit(solution)/shard_map/all_gather | solution.py:46
  17.4 1.5 broadcast_select_fusion
  18.8 1.1 fusion.2
  19.9 4.0 %collective-permute-start.8 = (bf16[640,1152]{1,0:T(8,128)(2,1)S(1)}, bf16[640,1152]{1,0:T(8,128)(2,1)S(1)}, u32[]{:S(2)}, u32[]{:S(2)}) collective-permute-start(bf16[640,1152]{1,0:T(8,128)(2,1)S(1)} %fusion.2), channel_id=1, source_target_pairs={{0,384},{48,432},{96,480},{144,528},{192,576},{240,624},{288,672},... | collective-permute-start | bytes 4423688 | tf_op jit(solution)/shard_map/ppermute | solution.py:23
  23.9 32.8 %collective-permute-done.8 = bf16[640,1152]{1,0:T(8,128)(2,1)S(1)} collective-permute-done((bf16[640,1152]{1,0:T(8,128)(2,1)S(1)}, bf16[640,1152]{1,0:T(8,128)(2,1)S(1)}, u32[]{:S(2)}, u32[]{:S(2)}) %collective-permute-start.8) | collective-permute-done | bytes 1474592 | tf_op jit(solution)/shard_map/ppermute | solution.py:23
  56.8 2.2 %add_convert_fusion = bf16[640,1152]{1,0:T(8,128)(2,1)} fusion(bf16[640,1152]{1,0:T(8,128)(2,1)S(1)} %collective-permute-done.8, bf16[512,1152]{1,0:T(8,128)(2,1)S(1)} %broadcast_select_fusion, pred[]{:T(512)S(6)} %lt.55, bf16[512,1280]{1,0:T(8,128)(2,1)S(1)} %copy-done.2), kind=kOutput, calls=%fused_computation.6 | convolution fusion | flops 759726080 | bytes 5439489 | tf_op jit(solution)/shard_map/dot_general | solution.py:56
  59.0 0.0 reduce-scatter.3.cloned.1.call-start
  59.1 0.1 dynamic-slice_bitcast_fusion
  59.2 13.0 %all-gather.2.cloned.1.call-done = bf16[2,640,1152]{2,1,0:T(8,128)(2,1)} async-done(((bf16[2,80,1152]{2,1,0:T(8,128)(2,1)}), bf16[2,640,1152]{2,1,0:T(8,128)(2,1)}) %all-gather.2.cloned.1.call-update) | async-done | bytes 2949136 | tf_op jit(solution)/shard_map/all_gather | solution.py:47
  72.2 2.9 %convolution_convert_fusion.3 = bf16[128,1280]{1,0:T(8,128)(2,1)S(1)} fusion(bf16[128,1152]{1,0:T(8,128)(2,1)S(1)} %get-tuple-element.8, bf16[1280,1152]{1,0:T(8,128)(2,1)} %bitcast.34), kind=kOutput, calls=%fused_computation.9 | convolution fusion | flops 377651200 | bytes 3571712 | tf_op jit(solution)/shard_map/dot_general | solution.py:123
  75.2 1.0 convolution_convert_fusion.2
  76.1 1.0 convolution_convert_fusion.1
  77.1 6.7 %collective-permute-start.2 = (bf16[128,1280]{1,0:T(8,128)(2,1)S(1)}, bf16[128,1280]{1,0:T(8,128)(2,1)S(1)}, u32[]{:S(2)}, u32[]{:S(2)}) collective-permute-start(bf16[128,1280]{1,0:T(8,128)(2,1)S(1)} %convolution_convert_fusion.1), channel_id=1, source_target_pairs={{0,11},{1,0},{2,1},{3,2},{4,3},{5,4},{6,5},{7,6},{8,7},{9,8},{10,9... | collective-permute-start | bytes 983048 | tf_op jit(solution)/shard_map/ppermute | solution.py:27
  83.8 1.9 %collective-permute-start.1 = (bf16[128,1280]{1,0:T(8,128)(2,1)S(1)}, bf16[128,1280]{1,0:T(8,128)(2,1)S(1)}, u32[]{:S(2)}, u32[]{:S(2)}) collective-permute-start(bf16[128,1280]{1,0:T(8,128)(2,1)S(1)} %convolution_convert_fusion.2), channel_id=1, source_target_pairs={{0,1},{1,2},{2,3},{3,4},{4,5},{5,6},{6,7},{7,8},{8,9},{9,10},{10,1... | collective-permute-start | bytes 983048 | tf_op jit(solution)/shard_map/ppermute | solution.py:27
  85.8 2.0 %collective-permute-start = (bf16[128,1280]{1,0:T(8,128)(2,1)S(1)}, bf16[128,1280]{1,0:T(8,128)(2,1)S(1)}, u32[]{:S(2)}, u32[]{:S(2)}) collective-permute-start(bf16[128,1280]{1,0:T(8,128)(2,1)S(1)} %convolution_convert_fusion.3), channel_id=1, source_target_pairs={{0,2},{1,3},{2,4},{3,5},{4,6},{5,7},{6,8},{7,9},{8,10},{9,11},{10,... | collective-permute-start | bytes 983048 | tf_op jit(solution)/shard_map/ppermute | solution.py:35
  87.8 2.5 %collective-permute-done.2 = bf16[128,1280]{1,0:T(8,128)(2,1)S(1)} collective-permute-done((bf16[128,1280]{1,0:T(8,128)(2,1)S(1)}, bf16[128,1280]{1,0:T(8,128)(2,1)S(1)}, u32[]{:S(2)}, u32[]{:S(2)}) %collective-permute-start.2) | collective-permute-done | bytes 327712 | tf_op jit(solution)/shard_map/ppermute | solution.py:27
  90.2 5.2 %collective-permute-done.1 = bf16[128,1280]{1,0:T(8,128)(2,1)S(1)} collective-permute-done((bf16[128,1280]{1,0:T(8,128)(2,1)S(1)}, bf16[128,1280]{1,0:T(8,128)(2,1)S(1)}, u32[]{:S(2)}, u32[]{:S(2)}) %collective-permute-start.1) | collective-permute-done | bytes 327712 | tf_op jit(solution)/shard_map/ppermute | solution.py:27
  95.4 3.5 %collective-permute-done = bf16[128,1280]{1,0:T(8,128)(2,1)S(1)} collective-permute-done((bf16[128,1280]{1,0:T(8,128)(2,1)S(1)}, bf16[128,1280]{1,0:T(8,128)(2,1)S(1)}, u32[]{:S(2)}, u32[]{:S(2)}) %collective-permute-start) | collective-permute-done | bytes 327712 | tf_op jit(solution)/shard_map/ppermute | solution.py:35
  98.9 1.0 add_convert_fusion.2
  99.9 5.6 %collective-permute-start.4 = (bf16[128,1280]{1,0:T(8,128)(2,1)S(1)}, bf16[128,1280]{1,0:T(8,128)(2,1)S(1)}, u32[]{:S(2)}, u32[]{:S(2)}) collective-permute-start(bf16[128,1280]{1,0:T(8,128)(2,1)S(1)} %add_convert_fusion.2), channel_id=1, source_target_pairs={{0,8},{1,9},{2,10},{3,11},{4,0},{5,1},{6,2},{7,3},{8,4},{9,5},{10,... | collective-permute-start | bytes 983048 | tf_op jit(solution)/shard_map/ppermute | solution.py:27
  105.5 4.2 %collective-permute-start.3 = (bf16[128,1280]{1,0:T(8,128)(2,1)S(1)}, bf16[128,1280]{1,0:T(8,128)(2,1)S(1)}, u32[]{:S(2)}, u32[]{:S(2)}) collective-permute-start(bf16[128,1280]{1,0:T(8,128)(2,1)S(1)} %add_convert_fusion.2), channel_id=1, source_target_pairs={{0,4},{1,5},{2,6},{3,7},{4,8},{5,9},{6,10},{7,11},{8,0},{9,1},{10,... | collective-permute-start | bytes 983048 | tf_op jit(solution)/shard_map/ppermute | solution.py:27
  109.7 2.9 %convolution_convert_fusion = bf16[512,1152]{1,0:T(8,128)(2,1)} fusion(bf16[512,1280]{1,0:T(8,128)(2,1)S(1)} %copy-done.3, bf16[1280,1152]{1,0:T(8,128)(2,1)S(1)} %bitcast.38), kind=kOutput, calls=%fused_computation.5 | convolution fusion | flops 1510539264 | bytes 5439488 | tf_op jit(solution)/shard_map/dot_general | solution.py:133
  112.7 9.2 %collective-permute-done.4 = bf16[128,1280]{1,0:T(8,128)(2,1)S(1)} collective-permute-done((bf16[128,1280]{1,0:T(8,128)(2,1)S(1)}, bf16[128,1280]{1,0:T(8,128)(2,1)S(1)}, u32[]{:S(2)}, u32[]{:S(2)}) %collective-permute-start.4) | collective-permute-done | bytes 327712 | tf_op jit(solution)/shard_map/ppermute | solution.py:27
  121.9 5.9 %collective-permute-done.3 = bf16[128,1280]{1,0:T(8,128)(2,1)S(1)} collective-permute-done((bf16[128,1280]{1,0:T(8,128)(2,1)S(1)}, bf16[128,1280]{1,0:T(8,128)(2,1)S(1)}, u32[]{:S(2)}, u32[]{:S(2)}) %collective-permute-start.3) | collective-permute-done | bytes 327712 | tf_op jit(solution)/shard_map/ppermute | solution.py:27
  127.8 0.1 broadcast_in_dim.27
  127.9 0.2 bitcast_dynamic-update-slice_fusion.3
  128.1 10.5 %collective-permute-start.5 = (bf16[128,1280]{1,0:T(8,128)(2,1)S(1)}, bf16[128,1280]{1,0:T(8,128)(2,1)S(1)}, u32[]{:S(2)}, u32[]{:S(2)}) collective-permute-start(bf16[128,1280]{1,0:T(8,128)(2,1)S(1)} %get-tuple-element.12), channel_id=1, source_target_pairs={{0,2},{1,3},{2,4},{3,5},{4,6},{5,7},{6,8},{7,9},{8,10},{9,11},{10,... | collective-permute-start | bytes 983048 | tf_op jit(solution)/shard_map/ppermute | solution.py:35
  138.7 7.8 %collective-permute-start.6 = (bf16[128,1280]{1,0:T(8,128)(2,1)S(1)}, bf16[128,1280]{1,0:T(8,128)(2,1)S(1)}, u32[]{:S(2)}, u32[]{:S(2)}) collective-permute-start(bf16[128,1280]{1,0:T(8,128)(2,1)S(1)} %get-tuple-element.12), channel_id=1, source_target_pairs={{0,1},{1,2},{2,3},{3,4},{4,5},{5,6},{6,7},{7,8},{8,9},{9,10},{10,1... | collective-permute-start | bytes 983048 | tf_op jit(solution)/shard_map/ppermute | solution.py:27
  146.5 1.9 %collective-permute-start.7 = (bf16[128,1280]{1,0:T(8,128)(2,1)S(1)}, bf16[128,1280]{1,0:T(8,128)(2,1)S(1)}, u32[]{:S(2)}, u32[]{:S(2)}) collective-permute-start(bf16[128,1280]{1,0:T(8,128)(2,1)S(1)} %get-tuple-element.12), channel_id=1, source_target_pairs={{0,11},{1,0},{2,1},{3,2},{4,3},{5,4},{6,5},{7,6},{8,7},{9,8},{10,9... | collective-permute-start | bytes 983048 | tf_op jit(solution)/shard_map/ppermute | solution.py:27
  148.5 7.3 %collective-permute-done.6 = bf16[128,1280]{1,0:T(8,128)(2,1)S(1)} collective-permute-done((bf16[128,1280]{1,0:T(8,128)(2,1)S(1)}, bf16[128,1280]{1,0:T(8,128)(2,1)S(1)}, u32[]{:S(2)}, u32[]{:S(2)}) %collective-permute-start.6) | collective-permute-done | bytes 327712 | tf_op jit(solution)/shard_map/ppermute | solution.py:27
  155.8 2.3 %collective-permute-done.7 = bf16[128,1280]{1,0:T(8,128)(2,1)S(1)} collective-permute-done((bf16[128,1280]{1,0:T(8,128)(2,1)S(1)}, bf16[128,1280]{1,0:T(8,128)(2,1)S(1)}, u32[]{:S(2)}, u32[]{:S(2)}) %collective-permute-start.7) | collective-permute-done | bytes 327712 | tf_op jit(solution)/shard_map/ppermute | solution.py:27
  158.2 1.0 copy-done.1
  (19 shorter events, 0.3 us)
Async XLA Ops:
  7.2 65.1 %all-gather.2.cloned.1.call-start = ((), (), s32[]{:S(2)}) async-start(), calls=%async_computation.2 | async-start | bytes 3317760 | tf_op jit(solution)/shard_map/all_gather | solution.py:47
  16.5 2.3 %copy-start.2 = (bf16[512,1280]{1,0:T(8,128)(2,1)S(1)}, bf16[512,1280]{1,0:T(8,128)(2,1)}, u32[]{:S(2)}) copy-start(bf16[512,1280]{1,0:T(8,128)(2,1)} %param.4) | copy-start | bytes 3932164
  16.5 141.6 %reduce-scatter.5.cloned.1.call-start = ((), (), s32[]{:S(2)}) async-start(), calls=%async_computation.4 | async-start | bytes 1658880 | tf_op jit(solution)/shard_map/reduce_scatter | solution.py:63
  19.9 36.9 %collective-permute-start.8 = (bf16[640,1152]{1,0:T(8,128)(2,1)S(1)}, bf16[640,1152]{1,0:T(8,128)(2,1)S(1)}, u32[]{:S(2)}, u32[]{:S(2)}) collective-permute-start(bf16[640,1152]{1,0:T(8,128)(2,1)S(1)} %fusion.2), channel_id=1, source_target_pairs={{0,384},{48,432},{96,480},{144,528},{192,576},{240,624},{288,672},... | collective-permute-start | bytes 4423688 | tf_op jit(solution)/shard_map/ppermute | solution.py:23
  59.0 99.2 %reduce-scatter.3.cloned.1.call-start = ((), (), s32[]{:S(2)}) async-start(), calls=%async_computation.3 | async-start | bytes 1474560 | tf_op jit(solution)/shard_map/reduce_scatter | solution.py:134
  72.2 2.9 %copy-start = (bf16[2,640,1152]{2,1,0:T(8,128)(2,1)S(1)}, bf16[2,640,1152]{2,1,0:T(8,128)(2,1)}, u32[]{:S(2)}) copy-start(bf16[2,640,1152]{2,1,0:T(8,128)(2,1)} %all-gather.2.cloned.1.call-done) | copy-start | bytes 8847364
  77.1 32.6 %copy-start.3 = (bf16[512,1280]{1,0:T(8,128)(2,1)S(1)}, bf16[512,1280]{1,0:T(8,128)(2,1)}, u32[]{:S(2)}) copy-start(bf16[512,1280]{1,0:T(8,128)(2,1)} %param.4) | copy-start | bytes 3932164
  77.1 13.1 %collective-permute-start.2 = (bf16[128,1280]{1,0:T(8,128)(2,1)S(1)}, bf16[128,1280]{1,0:T(8,128)(2,1)S(1)}, u32[]{:S(2)}, u32[]{:S(2)}) collective-permute-start(bf16[128,1280]{1,0:T(8,128)(2,1)S(1)} %convolution_convert_fusion.1), channel_id=1, source_target_pairs={{0,11},{1,0},{2,1},{3,2},{4,3},{5,4},{6,5},{7,6},{8,7},{9,8},{10,9... | collective-permute-start | bytes 983048 | tf_op jit(solution)/shard_map/ppermute | solution.py:27
  83.8 11.6 %collective-permute-start.1 = (bf16[128,1280]{1,0:T(8,128)(2,1)S(1)}, bf16[128,1280]{1,0:T(8,128)(2,1)S(1)}, u32[]{:S(2)}, u32[]{:S(2)}) collective-permute-start(bf16[128,1280]{1,0:T(8,128)(2,1)S(1)} %convolution_convert_fusion.2), channel_id=1, source_target_pairs={{0,1},{1,2},{2,3},{3,4},{4,5},{5,6},{6,7},{7,8},{8,9},{9,10},{10,1... | collective-permute-start | bytes 983048 | tf_op jit(solution)/shard_map/ppermute | solution.py:27
  85.8 13.1 %collective-permute-start = (bf16[128,1280]{1,0:T(8,128)(2,1)S(1)}, bf16[128,1280]{1,0:T(8,128)(2,1)S(1)}, u32[]{:S(2)}, u32[]{:S(2)}) collective-permute-start(bf16[128,1280]{1,0:T(8,128)(2,1)S(1)} %convolution_convert_fusion.3), channel_id=1, source_target_pairs={{0,2},{1,3},{2,4},{3,5},{4,6},{5,7},{6,8},{7,9},{8,10},{9,11},{10,... | collective-permute-start | bytes 983048 | tf_op jit(solution)/shard_map/ppermute | solution.py:35
  99.9 22.0 %collective-permute-start.4 = (bf16[128,1280]{1,0:T(8,128)(2,1)S(1)}, bf16[128,1280]{1,0:T(8,128)(2,1)S(1)}, u32[]{:S(2)}, u32[]{:S(2)}) collective-permute-start(bf16[128,1280]{1,0:T(8,128)(2,1)S(1)} %add_convert_fusion.2), channel_id=1, source_target_pairs={{0,8},{1,9},{2,10},{3,11},{4,0},{5,1},{6,2},{7,3},{8,4},{9,5},{10,... | collective-permute-start | bytes 983048 | tf_op jit(solution)/shard_map/ppermute | solution.py:27
  105.5 22.3 %collective-permute-start.3 = (bf16[128,1280]{1,0:T(8,128)(2,1)S(1)}, bf16[128,1280]{1,0:T(8,128)(2,1)S(1)}, u32[]{:S(2)}, u32[]{:S(2)}) collective-permute-start(bf16[128,1280]{1,0:T(8,128)(2,1)S(1)} %add_convert_fusion.2), channel_id=1, source_target_pairs={{0,4},{1,5},{2,6},{3,7},{4,8},{5,9},{6,10},{7,11},{8,0},{9,1},{10,... | collective-permute-start | bytes 983048 | tf_op jit(solution)/shard_map/ppermute | solution.py:27
  128.1 20.3 %collective-permute-start.5 = (bf16[128,1280]{1,0:T(8,128)(2,1)S(1)}, bf16[128,1280]{1,0:T(8,128)(2,1)S(1)}, u32[]{:S(2)}, u32[]{:S(2)}) collective-permute-start(bf16[128,1280]{1,0:T(8,128)(2,1)S(1)} %get-tuple-element.12), channel_id=1, source_target_pairs={{0,2},{1,3},{2,4},{3,5},{4,6},{5,7},{6,8},{7,9},{8,10},{9,11},{10,... | collective-permute-start | bytes 983048 | tf_op jit(solution)/shard_map/ppermute | solution.py:35
  138.7 17.0 %collective-permute-start.6 = (bf16[128,1280]{1,0:T(8,128)(2,1)S(1)}, bf16[128,1280]{1,0:T(8,128)(2,1)S(1)}, u32[]{:S(2)}, u32[]{:S(2)}) collective-permute-start(bf16[128,1280]{1,0:T(8,128)(2,1)S(1)} %get-tuple-element.12), channel_id=1, source_target_pairs={{0,1},{1,2},{2,3},{3,4},{4,5},{5,6},{6,7},{7,8},{8,9},{9,10},{10,1... | collective-permute-start | bytes 983048 | tf_op jit(solution)/shard_map/ppermute | solution.py:27
  146.5 11.6 %collective-permute-start.7 = (bf16[128,1280]{1,0:T(8,128)(2,1)S(1)}, bf16[128,1280]{1,0:T(8,128)(2,1)S(1)}, u32[]{:S(2)}, u32[]{:S(2)}) collective-permute-start(bf16[128,1280]{1,0:T(8,128)(2,1)S(1)} %get-tuple-element.12), channel_id=1, source_target_pairs={{0,11},{1,0},{2,1},{3,2},{4,3},{5,4},{6,5},{7,6},{8,7},{9,8},{10,9... | collective-permute-start | bytes 983048 | tf_op jit(solution)/shard_map/ppermute | solution.py:27
  158.1 1.1 copy-start.1
Sparse Core Ops, SparseCore 0:
  16.7 55.5 all-gather.1
  75.9 44.0 reduce-scatter.4
  123.8 27.6 reduce-scatter.2

commit v7 on v6

--- a/solution.py
+++ b/solution.py
@@ -119,16 +119,22 @@
         )
     )
 
-    def partial_grad(step):
-        value = lax.dot_general(
-            turned[step % 4],
-            weight,
-            (((1,), (1,)), ((), ())),
-            preferred_element_type=F32,
-        )
-        return value.astype(BF16)
+    def grad_of(rows):
+        def partial(step):
+            value = lax.dot_general(
+                turned[step % 4],
+                rows,
+                (((1,), (1,)), ((), ())),
+                preferred_element_type=F32,
+            )
+            return value.astype(BF16)
 
-    normed_grad = sum_over_col(partial_grad, z)
+        return sum_over_col(partial, z)
+
+    half = width // 2
+    normed_grad = jnp.concatenate(
+        [grad_of(weight[:half]), grad_of(weight[half:])], axis=1
+    )
 
     up_partial = jnp.dot(normed, weight, preferred_element_type=F32)
     up_out = lax.psum_scatter(

time: 167 us -> 173 us (1.036)
  starting transfers between devices: 44.8 us -> 70.3 us
  waiting for transfers between devices: 81.8 us -> 57.1 us
  matrix products: 12 us -> 16.6 us
    ppermute x6 -> x12, waiting for transfers between devices: 32.4 us -> 7.36 us  [over_col(): return lax.ppermute(value, 'col', z_shift(step))]
    ppermute x6 -> x12, starting transfers between devices: 28.1 us -> 46.3 us  [over_col(): return lax.ppermute(value, 'col', z_shift(step))]
    ppermute x2 -> x4, starting transfers between devices: 12.5 us -> 19.8 us  [near_two(): return lax.ppermute(value, ('row', 'col'), pairs)]
    dot_general x4 -> x8, matrix products: 5.82 us -> 10.4 us  [partial(): lax.dot_general(turned[step % 4], rows, (((1,), (1,)), ((), ())), preferr...]
    ppermute x2 -> x4, waiting for transfers between devices: 3.47 us -> 3.98 us  [near_two(): return lax.ppermute(value, ('row', 'col'), pairs)]
  transfers between devices with their start and end apart: 12 -> 20, of which waited for: 9 -> 4; matrix products, arithmetic and copies ran while one was open for 8% -> 12% of each run, Pallas kernels for 0% -> 0%
where the time goes in v7:
time: 173 us; the launch traced here: 172 us
  starting transfers between devices  70.3 us (41%)
  waiting for transfers between devices  57.1 us (33%)
  matrix products  16.6 us (10%)
  between operations  15.1 us (9%)
  blocking collectives  9.31 us (5%)
  other arithmetic  2.9 us (2%)
    ppermute x12, starting transfers between devices, over_col(): return lax.ppermute(value, 'col', z_shift(step))  46.3 us
    ppermute x1, waiting for transfers between devices, over_rep(): return lax.ppermute(value, 'rep', pairs)  32.8 us
    ppermute x4, starting transfers between devices, near_two(): return lax.ppermute(value, ('row', 'col'), pairs)  19.8 us
    all_gather x1, waiting for transfers between devices, gather_weight(): lax.all_gather(pair, 'rep', axis=1, tiled=True, axis_index_groups=Y_RINGS)  12.9 us
    dot_general x8, matrix products, partial(): lax.dot_general(turned[step % 4], rows, (((1,), (1,)), ((), ())), preferr...  10.4 us
    all_gather x1, blocking collectives, gather_weight(): lax.all_gather(w0, 'rep', axis=0, tiled=True, axis_index_groups=X_PAIRS)  9.31 us
    ppermute x12, waiting for transfers between devices, over_col(): return lax.ppermute(value, 'col', z_shift(step))  7.36 us
    ppermute x1, starting transfers between devices, over_rep(): return lax.ppermute(value, 'rep', pairs)  4.04 us
  transfers between devices with their start and end apart: 20, of which 4 were waited for; matrix products, arithmetic and copies ran while one was open for 12% of the time, Pallas kernels for 0%

profile of v7, /device:TPU:6, one launch (start us, length us, event | category | flops | bytes accessed | tf_op | source)
XLA Modules:
  0.0 171.7 jit_solution(11856165382550734583)
XLA Ops:
  7.2 9.3 %all_gather.6 = bf16[2,80,1152]{2,1,0:T(8,128)(2,1)} all-gather(bf16[1,80,1152]{2,1,0:T(8,128)(2,1)} %param.5), channel_id=1, replica_groups={{0,384},{48,432},{96,480},{144,528},{192,576},{240,624},{288,672},{336,..., dimensions={0}, use_global_device_ids=true | all-gather | bytes 552960 | tf_op jit(solution)/shard_map/all_gather | solution.py:46
  17.4 1.5 broadcast_select_fusion
  18.8 1.1 fusion.2
  19.9 4.0 %collective-permute-start.16 = (bf16[640,1152]{1,0:T(8,128)(2,1)S(1)}, bf16[640,1152]{1,0:T(8,128)(2,1)S(1)}, u32[]{:S(2)}, u32[]{:S(2)}) collective-permute-start(bf16[640,1152]{1,0:T(8,128)(2,1)S(1)} %fusion.2), channel_id=1, source_target_pairs={{0,384},{48,432},{96,480},{144,528},{192,576},{240,624},{288,672},... | collective-permute-start | bytes 4423688 | tf_op jit(solution)/shard_map/ppermute | solution.py:23
  24.0 32.8 %collective-permute-done.16 = bf16[640,1152]{1,0:T(8,128)(2,1)S(1)} collective-permute-done((bf16[640,1152]{1,0:T(8,128)(2,1)S(1)}, bf16[640,1152]{1,0:T(8,128)(2,1)S(1)}, u32[]{:S(2)}, u32[]{:S(2)}) %collective-permute-start.16) | collective-permute-done | bytes 1474592 | tf_op jit(solution)/shard_map/ppermute | solution.py:23
  56.8 2.2 %add_convert_fusion = bf16[640,1152]{1,0:T(8,128)(2,1)} fusion(bf16[640,1152]{1,0:T(8,128)(2,1)S(1)} %collective-permute-done.16, bf16[512,1152]{1,0:T(8,128)(2,1)S(1)} %broadcast_select_fusion, pred[]{:T(512)S(6)} %lt.59, bf16[512,1280]{1,0:T(8,128)(2,1)S(1)} %copy-done.2), kind=kOutput, calls=%fused_computation.6 | convolution fusion | flops 759726080 | bytes 5439489 | tf_op jit(solution)/shard_map/dot_general | solution.py:56
  59.3 12.9 %all-gather.2.cloned.1.call-done = bf16[2,640,1152]{2,1,0:T(8,128)(2,1)} async-done(((bf16[2,80,1152]{2,1,0:T(8,128)(2,1)}), bf16[2,640,1152]{2,1,0:T(8,128)(2,1)}) %all-gather.2.cloned.1.call-update) | async-done | bytes 2949136 | tf_op jit(solution)/shard_map/all_gather | solution.py:47
  72.2 2.1 %convolution_convert_fusion.5 = bf16[128,640]{1,0:T(8,128)(2,1)S(1)} fusion(bf16[128,1152]{1,0:T(8,128)(2,1)S(1)} %get-tuple-element.10, bf16[2,640,1152]{2,1,0:T(8,128)(2,1)} %all-gather.2.cloned.1.call-done), kind=kOutput, calls=%fused_computation.16 | convolution fusion | flops 188825600 | bytes 1933312 | tf_op jit(solution)/shard_map/dot_general | solution.py:124
  74.3 6.6 %collective-permute-start.2 = (bf16[128,640]{1,0:T(8,128)(2,1)S(1)}, bf16[128,640]{1,0:T(8,128)(2,1)S(1)}, u32[]{:S(2)}, u32[]{:S(2)}) collective-permute-start(bf16[128,640]{1,0:T(8,128)(2,1)S(1)} %convolution_convert_fusion.5), channel_id=1, source_target_pairs={{0,11},{1,0},{2,1},{3,2},{4,3},{5,4},{6,5},{7,6},{8,7},{9,8},{10,9... | collective-permute-start | bytes 491528 | tf_op jit(solution)/shard_map/ppermute | solution.py:27
  80.9 1.9 %convolution_convert_fusion.1 = bf16[128,640]{1,0:T(8,128)(2,1)S(1)} fusion(bf16[128,1152]{1,0:T(8,128)(2,1)S(1)} %get-tuple-element.10, bf16[2,640,1152]{2,1,0:T(8,128)(2,1)} %all-gather.2.cloned.1.call-done), kind=kOutput, calls=%fused_computation.11 | convolution fusion | flops 188825600 | bytes 1933312 | tf_op jit(solution)/shard_map/dot_general | solution.py:124
  82.9 3.2 %collective-permute-start.10 = (bf16[128,640]{1,0:T(8,128)(2,1)S(1)}, bf16[128,640]{1,0:T(8,128)(2,1)S(1)}, u32[]{:S(2)}, u32[]{:S(2)}) collective-permute-start(bf16[128,640]{1,0:T(8,128)(2,1)S(1)} %convolution_convert_fusion.1), channel_id=1, source_target_pairs={{0,11},{1,0},{2,1},{3,2},{4,3},{5,4},{6,5},{7,6},{8,7},{9,8},{10,9... | collective-permute-start | bytes 491528 | tf_op jit(solution)/shard_map/ppermute | solution.py:27
  86.6 2.7 %collective-permute-start.1 = (bf16[128,640]{1,0:T(8,128)(2,1)S(1)}, bf16[128,640]{1,0:T(8,128)(2,1)S(1)}, u32[]{:S(2)}, u32[]{:S(2)}) collective-permute-start(bf16[128,640]{1,0:T(8,128)(2,1)S(1)} %convolution_convert_fusion.6), channel_id=1, source_target_pairs={{0,1},{1,2},{2,3},{3,4},{4,5},{5,6},{6,7},{7,8},{8,9},{9,10},{10,1... | collective-permute-start | bytes 491528 | tf_op jit(solution)/shard_map/ppermute | solution.py:27
  89.9 2.1 %collective-permute-start.9 = (bf16[128,640]{1,0:T(8,128)(2,1)S(1)}, bf16[128,640]{1,0:T(8,128)(2,1)S(1)}, u32[]{:S(2)}, u32[]{:S(2)}) collective-permute-start(bf16[128,640]{1,0:T(8,128)(2,1)S(1)} %convolution_convert_fusion.2), channel_id=1, source_target_pairs={{0,1},{1,2},{2,3},{3,4},{4,5},{5,6},{6,7},{7,8},{8,9},{9,10},{10,1... | collective-permute-start | bytes 491528 | tf_op jit(solution)/shard_map/ppermute | solution.py:27
  92.6 3.1 %collective-permute-start = (bf16[128,640]{1,0:T(8,128)(2,1)S(1)}, bf16[128,640]{1,0:T(8,128)(2,1)S(1)}, u32[]{:S(2)}, u32[]{:S(2)}) collective-permute-start(bf16[128,640]{1,0:T(8,128)(2,1)S(1)} %convolution_convert_fusion.7), channel_id=1, source_target_pairs={{0,2},{1,3},{2,4},{3,5},{4,6},{5,7},{6,8},{7,9},{8,10},{9,11},{10,... | collective-permute-start | bytes 491528 | tf_op jit(solution)/shard_map/ppermute | solution.py:35
  95.7 2.9 %convolution_convert_fusion = bf16[512,1152]{1,0:T(8,128)(2,1)} fusion(bf16[512,1280]{1,0:T(8,128)(2,1)S(1)} %copy-done.3, bf16[1280,1152]{1,0:T(8,128)(2,1)S(1)} %bitcast.62), kind=kOutput, calls=%fused_computation.5 | convolution fusion | flops 1510539264 | bytes 5439488 | tf_op jit(solution)/shard_map/dot_general | solution.py:139
  98.7 2.1 %convolution_convert_fusion.3 = bf16[128,640]{1,0:T(8,128)(2,1)S(1)} fusion(bf16[128,1152]{1,0:T(8,128)(2,1)S(1)} %get-tuple-element.8, bf16[2,640,1152]{2,1,0:T(8,128)(2,1)} %all-gather.2.cloned.1.call-done), kind=kOutput, calls=%fused_computation.13 | convolution fusion | flops 188825600 | bytes 1933312 | tf_op jit(solution)/shard_map/dot_general | solution.py:124
  100.8 4.7 %collective-permute-start.8 = (bf16[128,640]{1,0:T(8,128)(2,1)S(1)}, bf16[128,640]{1,0:T(8,128)(2,1)S(1)}, u32[]{:S(2)}, u32[]{:S(2)}) collective-permute-start(bf16[128,640]{1,0:T(8,128)(2,1)S(1)} %convolution_convert_fusion.3), channel_id=1, source_target_pairs={{0,2},{1,3},{2,4},{3,5},{4,6},{5,7},{6,8},{7,9},{8,10},{9,11},{10,... | collective-permute-start | bytes 491528 | tf_op jit(solution)/shard_map/ppermute | solution.py:35
  105.5 2.0 %add_convert_fusion.4 = bf16[128,640]{1,0:T(8,128)(2,1)S(1)} fusion(bf16[128,640]{1,0:T(8,128)(2,1)S(1)} %collective-permute-done.2, bf16[128,640]{1,0:T(8,128)(2,1)S(1)} %collective-permute-done.1, bf16[128,640]{1,0:T(8,128)(2,1)S(1)} %collective-permute-done, bf16[128,1152]{1,0:T(8,128)(2,1)S(1)} %get-tuple-element.7, ...), kind=kOutput, calls=%fused_computation.32 | convolution fusion | flops 189480960 | bytes 2424832 | tf_op jit(solution)/shard_map/dot_general | solution.py:124
  107.5 4.4 %collective-permute-start.4 = (bf16[128,640]{1,0:T(8,128)(2,1)S(1)}, bf16[128,640]{1,0:T(8,128)(2,1)S(1)}, u32[]{:S(2)}, u32[]{:S(2)}) collective-permute-start(bf16[128,640]{1,0:T(8,128)(2,1)S(1)} %add_convert_fusion.4), channel_id=1, source_target_pairs={{0,8},{1,9},{2,10},{3,11},{4,0},{5,1},{6,2},{7,3},{8,4},{9,5},{10,... | collective-permute-start | bytes 491528 | tf_op jit(solution)/shard_map/ppermute | solution.py:27
  111.9 5.3 %collective-permute-start.3 = (bf16[128,640]{1,0:T(8,128)(2,1)S(1)}, bf16[128,640]{1,0:T(8,128)(2,1)S(1)}, u32[]{:S(2)}, u32[]{:S(2)}) collective-permute-start(bf16[128,640]{1,0:T(8,128)(2,1)S(1)} %add_convert_fusion.4), channel_id=1, source_target_pairs={{0,4},{1,5},{2,6},{3,7},{4,8},{5,9},{6,10},{7,11},{8,0},{9,1},{10,... | collective-permute-start | bytes 491528 | tf_op jit(solution)/shard_map/ppermute | solution.py:27
  117.3 0.6 add_convert_fusion.2
  117.9 4.4 %collective-permute-start.12 = (bf16[128,640]{1,0:T(8,128)(2,1)S(1)}, bf16[128,640]{1,0:T(8,128)(2,1)S(1)}, u32[]{:S(2)}, u32[]{:S(2)}) collective-permute-start(bf16[128,640]{1,0:T(8,128)(2,1)S(1)} %add_convert_fusion.2), channel_id=1, source_target_pairs={{0,8},{1,9},{2,10},{3,11},{4,0},{5,1},{6,2},{7,3},{8,4},{9,5},{10,... | collective-permute-start | bytes 491528 | tf_op jit(solution)/shard_map/ppermute | solution.py:27
  122.3 5.3 %collective-permute-start.11 = (bf16[128,640]{1,0:T(8,128)(2,1)S(1)}, bf16[128,640]{1,0:T(8,128)(2,1)S(1)}, u32[]{:S(2)}, u32[]{:S(2)}) collective-permute-start(bf16[128,640]{1,0:T(8,128)(2,1)S(1)} %add_convert_fusion.2), channel_id=1, source_target_pairs={{0,4},{1,5},{2,6},{3,7},{4,8},{5,9},{6,10},{7,11},{8,0},{9,1},{10,... | collective-permute-start | bytes 491528 | tf_op jit(solution)/shard_map/ppermute | solution.py:27
  127.7 7.3 %collective-permute-done.3 = bf16[128,640]{1,0:T(8,128)(2,1)S(1)} collective-permute-done((bf16[128,640]{1,0:T(8,128)(2,1)S(1)}, bf16[128,640]{1,0:T(8,128)(2,1)S(1)}, u32[]{:S(2)}, u32[]{:S(2)}) %collective-permute-start.3) | collective-permute-done | bytes 163872 | tf_op jit(solution)/shard_map/ppermute | solution.py:27
  135.2 1.9 %collective-permute-start.6 = (bf16[128,640]{1,0:T(8,128)(2,1)S(1)}, bf16[128,640]{1,0:T(8,128)(2,1)S(1)}, u32[]{:S(2)}, u32[]{:S(2)}) collective-permute-start(bf16[128,640]{1,0:T(8,128)(2,1)S(1)} %get-tuple-element.12), channel_id=1, source_target_pairs={{0,1},{1,2},{2,3},{3,4},{4,5},{5,6},{6,7},{7,8},{8,9},{9,10},{10,1... | collective-permute-start | bytes 491528 | tf_op jit(solution)/shard_map/ppermute | solution.py:27
  137.1 10.1 %collective-permute-start.5 = (bf16[128,640]{1,0:T(8,128)(2,1)S(1)}, bf16[128,640]{1,0:T(8,128)(2,1)S(1)}, u32[]{:S(2)}, u32[]{:S(2)}) collective-permute-start(bf16[128,640]{1,0:T(8,128)(2,1)S(1)} %get-tuple-element.12), channel_id=1, source_target_pairs={{0,2},{1,3},{2,4},{3,5},{4,6},{5,7},{6,8},{7,9},{8,10},{9,11},{10,... | collective-permute-start | bytes 491528 | tf_op jit(solution)/shard_map/ppermute | solution.py:35
  147.2 1.9 %collective-permute-start.7 = (bf16[128,640]{1,0:T(8,128)(2,1)S(1)}, bf16[128,640]{1,0:T(8,128)(2,1)S(1)}, u32[]{:S(2)}, u32[]{:S(2)}) collective-permute-start(bf16[128,640]{1,0:T(8,128)(2,1)S(1)} %get-tuple-element.12), channel_id=1, source_target_pairs={{0,11},{1,0},{2,1},{3,2},{4,3},{5,4},{6,5},{7,6},{8,7},{9,8},{10,9... | collective-permute-start | bytes 491528 | tf_op jit(solution)/shard_map/ppermute | solution.py:27
  149.3 3.9 %collective-permute-start.14 = (bf16[128,640]{1,0:T(8,128)(2,1)S(1)}, bf16[128,640]{1,0:T(8,128)(2,1)S(1)}, u32[]{:S(2)}, u32[]{:S(2)}) collective-permute-start(bf16[128,640]{1,0:T(8,128)(2,1)S(1)} %get-tuple-element.14), channel_id=1, source_target_pairs={{0,1},{1,2},{2,3},{3,4},{4,5},{5,6},{6,7},{7,8},{8,9},{9,10},{10,1... | collective-permute-start | bytes 491528 | tf_op jit(solution)/shard_map/ppermute | solution.py:27
  153.2 1.9 %collective-permute-start.13 = (bf16[128,640]{1,0:T(8,128)(2,1)S(1)}, bf16[128,640]{1,0:T(8,128)(2,1)S(1)}, u32[]{:S(2)}, u32[]{:S(2)}) collective-permute-start(bf16[128,640]{1,0:T(8,128)(2,1)S(1)} %get-tuple-element.14), channel_id=1, source_target_pairs={{0,2},{1,3},{2,4},{3,5},{4,6},{5,7},{6,8},{7,9},{8,10},{9,11},{10,... | collective-permute-start | bytes 491528 | tf_op jit(solution)/shard_map/ppermute | solution.py:35
  155.2 4.6 %collective-permute-start.15 = (bf16[128,640]{1,0:T(8,128)(2,1)S(1)}, bf16[128,640]{1,0:T(8,128)(2,1)S(1)}, u32[]{:S(2)}, u32[]{:S(2)}) collective-permute-start(bf16[128,640]{1,0:T(8,128)(2,1)S(1)} %get-tuple-element.14), channel_id=1, source_target_pairs={{0,11},{1,0},{2,1},{3,2},{4,3},{5,4},{6,5},{7,6},{8,7},{9,8},{10,9... | collective-permute-start | bytes 491528 | tf_op jit(solution)/shard_map/ppermute | solution.py:27
  159.8 4.0 %collective-permute-done.13 = bf16[128,640]{1,0:T(8,128)(2,1)S(1)} collective-permute-done((bf16[128,640]{1,0:T(8,128)(2,1)S(1)}, bf16[128,640]{1,0:T(8,128)(2,1)S(1)}, u32[]{:S(2)}, u32[]{:S(2)}) %collective-permute-start.13) | collective-permute-done | bytes 163872 | tf_op jit(solution)/shard_map/ppermute | solution.py:35
  164.0 1.2 pad_maximum_fusion
  (45 shorter events, 2.6 us)
Async XLA Ops:
  7.2 65.1 %all-gather.2.cloned.1.call-start = ((), (), s32[]{:S(2)}) async-start(), calls=%async_computation.2 | async-start | bytes 3317760 | tf_op jit(solution)/shard_map/all_gather | solution.py:47
  16.5 2.3 %copy-start.2 = (bf16[512,1280]{1,0:T(8,128)(2,1)S(1)}, bf16[512,1280]{1,0:T(8,128)(2,1)}, u32[]{:S(2)}) copy-start(bf16[512,1280]{1,0:T(8,128)(2,1)} %param.4) | copy-start | bytes 3932164
  16.6 148.6 %reduce-scatter.5.cloned.1.call-start = ((), (), s32[]{:S(2)}) async-start(), calls=%async_computation.4 | async-start | bytes 1658880 | tf_op jit(solution)/shard_map/reduce_scatter | solution.py:63
  19.9 36.9 %collective-permute-start.16 = (bf16[640,1152]{1,0:T(8,128)(2,1)S(1)}, bf16[640,1152]{1,0:T(8,128)(2,1)S(1)}, u32[]{:S(2)}, u32[]{:S(2)}) collective-permute-start(bf16[640,1152]{1,0:T(8,128)(2,1)S(1)} %fusion.2), channel_id=1, source_target_pairs={{0,384},{48,432},{96,480},{144,528},{192,576},{240,624},{288,672},... | collective-permute-start | bytes 4423688 | tf_op jit(solution)/shard_map/ppermute | solution.py:23
  59.0 106.1 %reduce-scatter.3.cloned.1.call-start = ((), (), s32[]{:S(2)}) async-start(), calls=%async_computation.3 | async-start | bytes 1474560 | tf_op jit(solution)/shard_map/reduce_scatter | solution.py:140
  72.2 13.8 %copy-start = (bf16[2,640,1152]{2,1,0:T(8,128)(2,1)S(1)}, bf16[2,640,1152]{2,1,0:T(8,128)(2,1)}, u32[]{:S(2)}) copy-start(bf16[2,640,1152]{2,1,0:T(8,128)(2,1)} %all-gather.2.cloned.1.call-done) | copy-start | bytes 8847364
  74.3 26.4 %collective-permute-start.2 = (bf16[128,640]{1,0:T(8,128)(2,1)S(1)}, bf16[128,640]{1,0:T(8,128)(2,1)S(1)}, u32[]{:S(2)}, u32[]{:S(2)}) collective-permute-start(bf16[128,640]{1,0:T(8,128)(2,1)S(1)} %convolution_convert_fusion.5), channel_id=1, source_target_pairs={{0,11},{1,0},{2,1},{3,2},{4,3},{5,4},{6,5},{7,6},{8,7},{9,8},{10,9... | collective-permute-start | bytes 491528 | tf_op jit(solution)/shard_map/ppermute | solution.py:27
  82.9 34.4 %collective-permute-start.10 = (bf16[128,640]{1,0:T(8,128)(2,1)S(1)}, bf16[128,640]{1,0:T(8,128)(2,1)S(1)}, u32[]{:S(2)}, u32[]{:S(2)}) collective-permute-start(bf16[128,640]{1,0:T(8,128)(2,1)S(1)} %convolution_convert_fusion.1), channel_id=1, source_target_pairs={{0,11},{1,0},{2,1},{3,2},{4,3},{5,4},{6,5},{7,6},{8,7},{9,8},{10,9... | collective-permute-start | bytes 491528 | tf_op jit(solution)/shard_map/ppermute | solution.py:27
  86.6 18.8 %collective-permute-start.1 = (bf16[128,640]{1,0:T(8,128)(2,1)S(1)}, bf16[128,640]{1,0:T(8,128)(2,1)S(1)}, u32[]{:S(2)}, u32[]{:S(2)}) collective-permute-start(bf16[128,640]{1,0:T(8,128)(2,1)S(1)} %convolution_convert_fusion.6), channel_id=1, source_target_pairs={{0,1},{1,2},{2,3},{3,4},{4,5},{5,6},{6,7},{7,8},{8,9},{9,10},{10,1... | collective-permute-start | bytes 491528 | tf_op jit(solution)/shard_map/ppermute | solution.py:27
  89.9 5.8 %copy-start.3 = (bf16[512,1280]{1,0:T(8,128)(2,1)S(1)}, bf16[512,1280]{1,0:T(8,128)(2,1)}, u32[]{:S(2)}) copy-start(bf16[512,1280]{1,0:T(8,128)(2,1)} %param.4) | copy-start | bytes 3932164
  89.9 27.3 %collective-permute-start.9 = (bf16[128,640]{1,0:T(8,128)(2,1)S(1)}, bf16[128,640]{1,0:T(8,128)(2,1)S(1)}, u32[]{:S(2)}, u32[]{:S(2)}) collective-permute-start(bf16[128,640]{1,0:T(8,128)(2,1)S(1)} %convolution_convert_fusion.2), channel_id=1, source_target_pairs={{0,1},{1,2},{2,3},{3,4},{4,5},{5,6},{6,7},{7,8},{8,9},{9,10},{10,1... | collective-permute-start | bytes 491528 | tf_op jit(solution)/shard_map/ppermute | solution.py:27
  92.6 12.9 %collective-permute-start = (bf16[128,640]{1,0:T(8,128)(2,1)S(1)}, bf16[128,640]{1,0:T(8,128)(2,1)S(1)}, u32[]{:S(2)}, u32[]{:S(2)}) collective-permute-start(bf16[128,640]{1,0:T(8,128)(2,1)S(1)} %convolution_convert_fusion.7), channel_id=1, source_target_pairs={{0,2},{1,3},{2,4},{3,5},{4,6},{5,7},{6,8},{7,9},{8,10},{9,11},{10,... | collective-permute-start | bytes 491528 | tf_op jit(solution)/shard_map/ppermute | solution.py:35
  98.7 18.6 %copy-start.1 = (bf16[2,640,1152]{2,1,0:T(8,128)(2,1)S(1)}, bf16[2,640,1152]{2,1,0:T(8,128)(2,1)}, u32[]{:S(2)}) copy-start(bf16[2,640,1152]{2,1,0:T(8,128)(2,1)} %all-gather.2.cloned.1.call-done) | copy-start | bytes 8847364
  100.8 16.5 %collective-permute-start.8 = (bf16[128,640]{1,0:T(8,128)(2,1)S(1)}, bf16[128,640]{1,0:T(8,128)(2,1)S(1)}, u32[]{:S(2)}, u32[]{:S(2)}) collective-permute-start(bf16[128,640]{1,0:T(8,128)(2,1)S(1)} %convolution_convert_fusion.3), channel_id=1, source_target_pairs={{0,2},{1,3},{2,4},{3,5},{4,6},{5,7},{6,8},{7,9},{8,10},{9,11},{10,... | collective-permute-start | bytes 491528 | tf_op jit(solution)/shard_map/ppermute | solution.py:35
  107.5 20.2 %collective-permute-start.4 = (bf16[128,640]{1,0:T(8,128)(2,1)S(1)}, bf16[128,640]{1,0:T(8,128)(2,1)S(1)}, u32[]{:S(2)}, u32[]{:S(2)}) collective-permute-start(bf16[128,640]{1,0:T(8,128)(2,1)S(1)} %add_convert_fusion.4), channel_id=1, source_target_pairs={{0,8},{1,9},{2,10},{3,11},{4,0},{5,1},{6,2},{7,3},{8,4},{9,5},{10,... | collective-permute-start | bytes 491528 | tf_op jit(solution)/shard_map/ppermute | solution.py:27
  111.9 23.1 %collective-permute-start.3 = (bf16[128,640]{1,0:T(8,128)(2,1)S(1)}, bf16[128,640]{1,0:T(8,128)(2,1)S(1)}, u32[]{:S(2)}, u32[]{:S(2)}) collective-permute-start(bf16[128,640]{1,0:T(8,128)(2,1)S(1)} %add_convert_fusion.4), channel_id=1, source_target_pairs={{0,4},{1,5},{2,6},{3,7},{4,8},{5,9},{6,10},{7,11},{8,0},{9,1},{10,... | collective-permute-start | bytes 491528 | tf_op jit(solution)/shard_map/ppermute | solution.py:27
  117.9 31.2 %collective-permute-start.12 = (bf16[128,640]{1,0:T(8,128)(2,1)S(1)}, bf16[128,640]{1,0:T(8,128)(2,1)S(1)}, u32[]{:S(2)}, u32[]{:S(2)}) collective-permute-start(bf16[128,640]{1,0:T(8,128)(2,1)S(1)} %add_convert_fusion.2), channel_id=1, source_target_pairs={{0,8},{1,9},{2,10},{3,11},{4,0},{5,1},{6,2},{7,3},{8,4},{9,5},{10,... | collective-permute-start | bytes 491528 | tf_op jit(solution)/shard_map/ppermute | solution.py:27
  122.3 26.8 %collective-permute-start.11 = (bf16[128,640]{1,0:T(8,128)(2,1)S(1)}, bf16[128,640]{1,0:T(8,128)(2,1)S(1)}, u32[]{:S(2)}, u32[]{:S(2)}) collective-permute-start(bf16[128,640]{1,0:T(8,128)(2,1)S(1)} %add_convert_fusion.2), channel_id=1, source_target_pairs={{0,4},{1,5},{2,6},{3,7},{4,8},{5,9},{6,10},{7,11},{8,0},{9,1},{10,... | collective-permute-start | bytes 491528 | tf_op jit(solution)/shard_map/ppermute | solution.py:27
  135.2 28.6 %collective-permute-start.6 = (bf16[128,640]{1,0:T(8,128)(2,1)S(1)}, bf16[128,640]{1,0:T(8,128)(2,1)S(1)}, u32[]{:S(2)}, u32[]{:S(2)}) collective-permute-start(bf16[128,640]{1,0:T(8,128)(2,1)S(1)} %get-tuple-element.12), channel_id=1, source_target_pairs={{0,1},{1,2},{2,3},{3,4},{4,5},{5,6},{6,7},{7,8},{8,9},{9,10},{10,1... | collective-permute-start | bytes 491528 | tf_op jit(solution)/shard_map/ppermute | solution.py:27
  137.1 18.1 %collective-permute-start.5 = (bf16[128,640]{1,0:T(8,128)(2,1)S(1)}, bf16[128,640]{1,0:T(8,128)(2,1)S(1)}, u32[]{:S(2)}, u32[]{:S(2)}) collective-permute-start(bf16[128,640]{1,0:T(8,128)(2,1)S(1)} %get-tuple-element.12), channel_id=1, source_target_pairs={{0,2},{1,3},{2,4},{3,5},{4,6},{5,7},{6,8},{7,9},{8,10},{9,11},{10,... | collective-permute-start | bytes 491528 | tf_op jit(solution)/shard_map/ppermute | solution.py:35
  147.2 16.7 %collective-permute-start.7 = (bf16[128,640]{1,0:T(8,128)(2,1)S(1)}, bf16[128,640]{1,0:T(8,128)(2,1)S(1)}, u32[]{:S(2)}, u32[]{:S(2)}) collective-permute-start(bf16[128,640]{1,0:T(8,128)(2,1)S(1)} %get-tuple-element.12), channel_id=1, source_target_pairs={{0,11},{1,0},{2,1},{3,2},{4,3},{5,4},{6,5},{7,6},{8,7},{9,8},{10,9... | collective-permute-start | bytes 491528 | tf_op jit(solution)/shard_map/ppermute | solution.py:27
  149.3 14.5 %collective-permute-start.14 = (bf16[128,640]{1,0:T(8,128)(2,1)S(1)}, bf16[128,640]{1,0:T(8,128)(2,1)S(1)}, u32[]{:S(2)}, u32[]{:S(2)}) collective-permute-start(bf16[128,640]{1,0:T(8,128)(2,1)S(1)} %get-tuple-element.14), channel_id=1, source_target_pairs={{0,1},{1,2},{2,3},{3,4},{4,5},{5,6},{6,7},{7,8},{8,9},{9,10},{10,1... | collective-permute-start | bytes 491528 | tf_op jit(solution)/shard_map/ppermute | solution.py:27
  153.2 10.5 %collective-permute-start.13 = (bf16[128,640]{1,0:T(8,128)(2,1)S(1)}, bf16[128,640]{1,0:T(8,128)(2,1)S(1)}, u32[]{:S(2)}, u32[]{:S(2)}) collective-permute-start(bf16[128,640]{1,0:T(8,128)(2,1)S(1)} %get-tuple-element.14), channel_id=1, source_target_pairs={{0,2},{1,3},{2,4},{3,5},{4,6},{5,7},{6,8},{7,9},{8,10},{9,11},{10,... | collective-permute-start | bytes 491528 | tf_op jit(solution)/shard_map/ppermute | solution.py:35
  155.2 8.8 %collective-permute-start.15 = (bf16[128,640]{1,0:T(8,128)(2,1)S(1)}, bf16[128,640]{1,0:T(8,128)(2,1)S(1)}, u32[]{:S(2)}, u32[]{:S(2)}) collective-permute-start(bf16[128,640]{1,0:T(8,128)(2,1)S(1)} %get-tuple-element.14), channel_id=1, source_target_pairs={{0,11},{1,0},{2,1},{3,2},{4,3},{5,4},{6,5},{7,6},{8,7},{9,8},{10,9... | collective-permute-start | bytes 491528 | tf_op jit(solution)/shard_map/ppermute | solution.py:27
Sparse Core Ops, SparseCore 0:
  16.7 55.5 all-gather.1
  75.9 44.1 reduce-scatter.4
  123.9 27.4 reduce-scatter.2

commit v8 on v6

--- a/solution.py
+++ b/solution.py
@@ -15,23 +15,15 @@
 X_SWAP = [(i, (i + NY) % (2 * NY)) for i in range(2 * NY)]
 
 
-def z_shift(step):
-    return [(z, (z + step) % NZ) for z in range(NZ)]
-
-
 def over_rep(value, pairs):
     return lax.ppermute(value, "rep", pairs)
 
 
 def over_col(value, step):
-    return lax.ppermute(value, "col", z_shift(step))
-
-
-def near_two(value):
     pairs = []
     for row in range(4):
-        step = 2 - 4 * (row % 2)
-        pairs += [(row * NZ + z, row * NZ + (z + step) % NZ) for z in range(NZ)]
+        signed = step - 2 * step * (row % 2)
+        pairs += [(row * NZ + z, row * NZ + (z + signed) % NZ) for z in range(NZ)]
     return lax.ppermute(value, ("row", "col"), pairs)
 
 
@@ -65,30 +57,35 @@
     )
 
 
-def sum_over_col(partial, z):
-    def residue(step):
-        return lax.rem(z + step + NZ, 4)
+def sum_over_col(turned, weight, z, up):
+    def partial(tokens):
+        value = lax.dot_general(
+            tokens, weight, (((1,), (1,)), ((), ())), preferred_element_type=F32
+        )
+        return value.astype(BF16)
 
-    def near(pieces):
-        return (
-            near_two(pieces[0]),
-            over_col(pieces[1], 1),
-            over_col(pieces[2], -1),
-        )
-
-    arrived = near((partial(2), partial(1), partial(-1)))
-    mine = add(partial(0), *arrived)
-    below = over_col(mine, 4)
-    above = over_col(mine, -4)
+    two_away = partial(turned[2])
+    ahead, behind, _ = lax.optimization_barrier((turned[1], turned[3], two_away))
+    arrived = (
+        over_col(two_away, 2),
+        over_col(partial(ahead), 1),
+        over_col(partial(behind), -1),
+    )
+    mine = add(partial(turned[0]), *arrived)
+    from_behind = over_col(mine, 4)
+    from_ahead = over_col(mine, -4)
+    below = jnp.where(up == 1, from_behind, from_ahead)
+    above = jnp.where(up == 1, from_ahead, from_behind)
     q = z // 4
     last = jnp.where(q == 0, below, jnp.where(q == 1, above, mine))
     one = jnp.where(q == 0, mine, below)
     two = jnp.where(q == 1, mine, above)
     total = add(one, two, last)
-    arrived = near((total, total, total))
+    arrived = (over_col(total, 2), over_col(total, 1), over_col(total, -1))
     result = jnp.zeros((4,) + total.shape, total.dtype)
     for step, value in ((0, total), (2, arrived[0]), (-1, arrived[1]), (1, arrived[2])):
-        result = lax.dynamic_update_slice(result, value[None], (residue(step), 0, 0))
+        place = lax.rem(z + step * up + NZ, 4)
+        result = lax.dynamic_update_slice(result, value[None], (place, 0, 0))
     return result.reshape(-1, total.shape[1])
 
 
@@ -112,23 +109,14 @@
 
     quarters = masked.reshape(4, row_count // 4, unit_count)
 
+    up = 1 - 2 * lax.rem(lax.axis_index("row"), 2)
     turned = lax.optimization_barrier(
         tuple(
-            lax.dynamic_index_in_dim(quarters, lax.rem(z + s, 4), 0, keepdims=False)
+            lax.dynamic_index_in_dim(quarters, lax.rem(z + s * up + NZ, 4), 0, keepdims=False)
             for s in range(4)
         )
     )
-
-    def partial_grad(step):
-        value = lax.dot_general(
-            turned[step % 4],
-            weight,
-            (((1,), (1,)), ((), ())),
-            preferred_element_type=F32,
-        )
-        return value.astype(BF16)
-
-    normed_grad = sum_over_col(partial_grad, z)
+    normed_grad = sum_over_col(turned, weight, z, up)
 
     up_partial = jnp.dot(normed, weight, preferred_element_type=F32)
     up_out = lax.psum_scatter(

time: 167 us -> 163 us (0.976)
  starting transfers between devices: 44.8 us -> 37.7 us
  waiting for transfers between devices: 81.8 us -> 83.8 us
    ppermute x8, starting transfers between devices: 40.6 us -> 33.5 us  [over_col(): return lax.ppermute(value, ('row', 'col'), pairs)]
    ppermute x8, waiting for transfers between devices: 35.9 us -> 37.9 us  [over_col(): return lax.ppermute(value, ('row', 'col'), pairs)]
  transfers between devices with their start and end apart: 12 -> 12, of which waited for: 9 -> 9; matrix products, arithmetic and copies ran while one was open for 8% -> 9% of each run, Pallas kernels for 0% -> 0%
where the time goes in v8:
time: 163 us; the launch traced here: 161 us
  waiting for transfers between devices  83.8 us (51%)
  starting transfers between devices  37.7 us (23%)
  between operations  14.8 us (9%)
  matrix products  12 us (7%)
  blocking collectives  9.31 us (6%)
  other arithmetic  1.73 us (1%)
    ppermute x8, waiting for transfers between devices, over_col(): return lax.ppermute(value, ('row', 'col'), pairs)  37.9 us
    ppermute x8, starting transfers between devices, over_col(): return lax.ppermute(value, ('row', 'col'), pairs)  33.5 us
    ppermute x1, waiting for transfers between devices, over_rep(): return lax.ppermute(value, 'rep', pairs)  32.8 us
    all_gather x1, waiting for transfers between devices, gather_weight(): lax.all_gather(pair, 'rep', axis=1, tiled=True, axis_index_groups=Y_RINGS)  13 us
    all_gather x1, blocking collectives, gather_weight(): lax.all_gather(w0, 'rep', axis=0, tiled=True, axis_index_groups=X_PAIRS)  9.31 us
    dot_general x4, matrix products, partial(): lax.dot_general(tokens, weight, (((1,), (1,)), ((), ())), preferred_eleme...  5.82 us
    ppermute x1, starting transfers between devices, over_rep(): return lax.ppermute(value, 'rep', pairs)  4.03 us
  transfers between devices with their start and end apart: 12, of which 9 were waited for; matrix products, arithmetic and copies ran while one was open for 9% of the time, Pallas kernels for 0%

profile of v8, /device:TPU:6, one launch (start us, length us, event | category | flops | bytes accessed | tf_op | source)
XLA Modules:
  0.0 160.6 jit_solution(6806111521341016850)
XLA Ops:
  7.2 9.3 %all_gather.6 = bf16[2,80,1152]{2,1,0:T(8,128)(2,1)} all-gather(bf16[1,80,1152]{2,1,0:T(8,128)(2,1)} %param.5), channel_id=1, replica_groups={{0,384},{48,432},{96,480},{144,528},{192,576},{240,624},{288,672},{336,..., dimensions={0}, use_global_device_ids=true | all-gather | bytes 552960 | tf_op jit(solution)/shard_map/all_gather | solution.py:38
  17.4 1.5 broadcast_select_fusion
  18.8 1.1 fusion.2
  19.9 4.0 %collective-permute-start.8 = (bf16[640,1152]{1,0:T(8,128)(2,1)S(1)}, bf16[640,1152]{1,0:T(8,128)(2,1)S(1)}, u32[]{:S(2)}, u32[]{:S(2)}) collective-permute-start(bf16[640,1152]{1,0:T(8,128)(2,1)S(1)} %fusion.2), channel_id=1, source_target_pairs={{0,384},{48,432},{96,480},{144,528},{192,576},{240,624},{288,672},... | collective-permute-start | bytes 4423688 | tf_op jit(solution)/shard_map/ppermute | solution.py:19
  23.9 32.8 %collective-permute-done.8 = bf16[640,1152]{1,0:T(8,128)(2,1)S(1)} collective-permute-done((bf16[640,1152]{1,0:T(8,128)(2,1)S(1)}, bf16[640,1152]{1,0:T(8,128)(2,1)S(1)}, u32[]{:S(2)}, u32[]{:S(2)}) %collective-permute-start.8) | collective-permute-done | bytes 1474592 | tf_op jit(solution)/shard_map/ppermute | solution.py:19
  56.8 2.2 %add_convert_fusion = bf16[640,1152]{1,0:T(8,128)(2,1)} fusion(bf16[640,1152]{1,0:T(8,128)(2,1)S(1)} %collective-permute-done.8, bf16[512,1152]{1,0:T(8,128)(2,1)S(1)} %broadcast_select_fusion, pred[]{:T(512)S(6)} %lt.46, bf16[512,1280]{1,0:T(8,128)(2,1)S(1)} %copy-done.2), kind=kOutput, calls=%fused_computation.6 | convolution fusion | flops 759726080 | bytes 5439489 | tf_op jit(solution)/shard_map/dot_general | solution.py:48
  59.0 0.0 reduce-scatter.3.cloned.1.call-start
  59.1 0.1 dynamic-slice_bitcast_fusion
  59.2 13.0 %all-gather.2.cloned.1.call-done = bf16[2,640,1152]{2,1,0:T(8,128)(2,1)} async-done(((bf16[2,80,1152]{2,1,0:T(8,128)(2,1)}), bf16[2,640,1152]{2,1,0:T(8,128)(2,1)}) %all-gather.2.cloned.1.call-update) | async-done | bytes 2949136 | tf_op jit(solution)/shard_map/all_gather | solution.py:39
  72.2 2.9 %convolution_convert_fusion.3 = bf16[128,1280]{1,0:T(8,128)(2,1)S(1)} fusion(bf16[128,1152]{1,0:T(8,128)(2,1)S(1)} %get-tuple-element.10, bf16[1280,1152]{1,0:T(8,128)(2,1)} %bitcast.34), kind=kOutput, calls=%fused_computation.9 | convolution fusion | flops 377651200 | bytes 3571712 | tf_op jit(solution)/shard_map/dot_general | solution.py:62
  75.2 1.0 convolution_convert_fusion.2
  76.1 1.0 convolution_convert_fusion.1
  77.1 6.7 %collective-permute-start.2 = (bf16[128,1280]{1,0:T(8,128)(2,1)S(1)}, bf16[128,1280]{1,0:T(8,128)(2,1)S(1)}, u32[]{:S(2)}, u32[]{:S(2)}) collective-permute-start(bf16[128,1280]{1,0:T(8,128)(2,1)S(1)} %convolution_convert_fusion.1), channel_id=1, source_target_pairs={{0,11},{1,0},{2,1},{3,2},{4,3},{5,4},{6,5},{7,6},{8,7},{9,8},{10,9... | collective-permute-start | bytes 983048 | tf_op jit(solution)/shard_map/ppermute | solution.py:27
  83.8 1.9 %collective-permute-start.1 = (bf16[128,1280]{1,0:T(8,128)(2,1)S(1)}, bf16[128,1280]{1,0:T(8,128)(2,1)S(1)}, u32[]{:S(2)}, u32[]{:S(2)}) collective-permute-start(bf16[128,1280]{1,0:T(8,128)(2,1)S(1)} %convolution_convert_fusion.2), channel_id=1, source_target_pairs={{0,1},{1,2},{2,3},{3,4},{4,5},{5,6},{6,7},{7,8},{8,9},{9,10},{10,1... | collective-permute-start | bytes 983048 | tf_op jit(solution)/shard_map/ppermute | solution.py:27
  85.8 2.0 %collective-permute-start = (bf16[128,1280]{1,0:T(8,128)(2,1)S(1)}, bf16[128,1280]{1,0:T(8,128)(2,1)S(1)}, u32[]{:S(2)}, u32[]{:S(2)}) collective-permute-start(bf16[128,1280]{1,0:T(8,128)(2,1)S(1)} %convolution_convert_fusion.3), channel_id=1, source_target_pairs={{0,2},{1,3},{2,4},{3,5},{4,6},{5,7},{6,8},{7,9},{8,10},{9,11},{10,... | collective-permute-start | bytes 983048 | tf_op jit(solution)/shard_map/ppermute | solution.py:27
  87.8 7.5 %collective-permute-done.2 = bf16[128,1280]{1,0:T(8,128)(2,1)S(1)} collective-permute-done((bf16[128,1280]{1,0:T(8,128)(2,1)S(1)}, bf16[128,1280]{1,0:T(8,128)(2,1)S(1)}, u32[]{:S(2)}, u32[]{:S(2)}) %collective-permute-start.2) | collective-permute-done | bytes 327712 | tf_op jit(solution)/shard_map/ppermute | solution.py:27
  95.3 0.1 collective-permute-done.1
  95.4 2.4 %collective-permute-done = bf16[128,1280]{1,0:T(8,128)(2,1)S(1)} collective-permute-done((bf16[128,1280]{1,0:T(8,128)(2,1)S(1)}, bf16[128,1280]{1,0:T(8,128)(2,1)S(1)}, u32[]{:S(2)}, u32[]{:S(2)}) %collective-permute-start) | collective-permute-done | bytes 327712 | tf_op jit(solution)/shard_map/ppermute | solution.py:27
  97.8 1.0 add_convert_fusion.2
  98.8 6.3 %collective-permute-start.4 = (bf16[128,1280]{1,0:T(8,128)(2,1)S(1)}, bf16[128,1280]{1,0:T(8,128)(2,1)S(1)}, u32[]{:S(2)}, u32[]{:S(2)}) collective-permute-start(bf16[128,1280]{1,0:T(8,128)(2,1)S(1)} %add_convert_fusion.2), channel_id=1, source_target_pairs={{0,8},{1,9},{2,10},{3,11},{4,0},{5,1},{6,2},{7,3},{8,4},{9,5},{10,... | collective-permute-start | bytes 983048 | tf_op jit(solution)/shard_map/ppermute | solution.py:27
  105.1 3.5 %collective-permute-start.3 = (bf16[128,1280]{1,0:T(8,128)(2,1)S(1)}, bf16[128,1280]{1,0:T(8,128)(2,1)S(1)}, u32[]{:S(2)}, u32[]{:S(2)}) collective-permute-start(bf16[128,1280]{1,0:T(8,128)(2,1)S(1)} %add_convert_fusion.2), channel_id=1, source_target_pairs={{0,4},{1,5},{2,6},{3,7},{4,8},{5,9},{6,10},{7,11},{8,0},{9,1},{10,... | collective-permute-start | bytes 983048 | tf_op jit(solution)/shard_map/ppermute | solution.py:27
  108.6 2.9 %convolution_convert_fusion = bf16[512,1152]{1,0:T(8,128)(2,1)} fusion(bf16[512,1280]{1,0:T(8,128)(2,1)S(1)} %copy-done.3, bf16[1280,1152]{1,0:T(8,128)(2,1)S(1)} %bitcast.38), kind=kOutput, calls=%fused_computation.5 | convolution fusion | flops 1510539264 | bytes 5439488 | tf_op jit(solution)/shard_map/dot_general | solution.py:121
  111.5 11.8 %collective-permute-done.4 = bf16[128,1280]{1,0:T(8,128)(2,1)S(1)} collective-permute-done((bf16[128,1280]{1,0:T(8,128)(2,1)S(1)}, bf16[128,1280]{1,0:T(8,128)(2,1)S(1)}, u32[]{:S(2)}, u32[]{:S(2)}) %collective-permute-start.4) | collective-permute-done | bytes 327712 | tf_op jit(solution)/shard_map/ppermute | solution.py:27
  123.4 8.6 %collective-permute-done.3 = bf16[128,1280]{1,0:T(8,128)(2,1)S(1)} collective-permute-done((bf16[128,1280]{1,0:T(8,128)(2,1)S(1)}, bf16[128,1280]{1,0:T(8,128)(2,1)S(1)}, u32[]{:S(2)}, u32[]{:S(2)}) %collective-permute-start.3) | collective-permute-done | bytes 327712 | tf_op jit(solution)/shard_map/ppermute | solution.py:27
  131.9 0.1 broadcast_in_dim.27
  132.0 0.3 bitcast_dynamic-update-slice_fusion.3
  132.3 1.9 %collective-permute-start.5 = (bf16[128,1280]{1,0:T(8,128)(2,1)S(1)}, bf16[128,1280]{1,0:T(8,128)(2,1)S(1)}, u32[]{:S(2)}, u32[]{:S(2)}) collective-permute-start(bf16[128,1280]{1,0:T(8,128)(2,1)S(1)} %get-tuple-element.16), channel_id=1, source_target_pairs={{0,2},{1,3},{2,4},{3,5},{4,6},{5,7},{6,8},{7,9},{8,10},{9,11},{10,... | collective-permute-start | bytes 983048 | tf_op jit(solution)/shard_map/ppermute | solution.py:27
  134.2 6.7 %collective-permute-start.6 = (bf16[128,1280]{1,0:T(8,128)(2,1)S(1)}, bf16[128,1280]{1,0:T(8,128)(2,1)S(1)}, u32[]{:S(2)}, u32[]{:S(2)}) collective-permute-start(bf16[128,1280]{1,0:T(8,128)(2,1)S(1)} %get-tuple-element.16), channel_id=1, source_target_pairs={{0,1},{1,2},{2,3},{3,4},{4,5},{5,6},{6,7},{7,8},{8,9},{9,10},{10,1... | collective-permute-start | bytes 983048 | tf_op jit(solution)/shard_map/ppermute | solution.py:27
  140.9 4.6 %collective-permute-start.7 = (bf16[128,1280]{1,0:T(8,128)(2,1)S(1)}, bf16[128,1280]{1,0:T(8,128)(2,1)S(1)}, u32[]{:S(2)}, u32[]{:S(2)}) collective-permute-start(bf16[128,1280]{1,0:T(8,128)(2,1)S(1)} %get-tuple-element.16), channel_id=1, source_target_pairs={{0,11},{1,0},{2,1},{3,2},{4,3},{5,4},{6,5},{7,6},{8,7},{9,8},{10,9... | collective-permute-start | bytes 983048 | tf_op jit(solution)/shard_map/ppermute | solution.py:27
  145.5 7.0 %collective-permute-done.6 = bf16[128,1280]{1,0:T(8,128)(2,1)S(1)} collective-permute-done((bf16[128,1280]{1,0:T(8,128)(2,1)S(1)}, bf16[128,1280]{1,0:T(8,128)(2,1)S(1)}, u32[]{:S(2)}, u32[]{:S(2)}) %collective-permute-start.6) | collective-permute-done | bytes 327712 | tf_op jit(solution)/shard_map/ppermute | solution.py:27
  152.5 0.4 collective-permute-done.7
  153.1 1.0 copy-done.1
  (19 shorter events, 0.3 us)
Async XLA Ops:
  7.2 65.1 %all-gather.2.cloned.1.call-start = ((), (), s32[]{:S(2)}) async-start(), calls=%async_computation.2 | async-start | bytes 3317760 | tf_op jit(solution)/shard_map/all_gather | solution.py:39
  16.5 2.3 %copy-start.2 = (bf16[512,1280]{1,0:T(8,128)(2,1)S(1)}, bf16[512,1280]{1,0:T(8,128)(2,1)}, u32[]{:S(2)}) copy-start(bf16[512,1280]{1,0:T(8,128)(2,1)} %param.4) | copy-start | bytes 3932164
  16.5 136.5 %reduce-scatter.5.cloned.1.call-start = ((), (), s32[]{:S(2)}) async-start(), calls=%async_computation.4 | async-start | bytes 1658880 | tf_op jit(solution)/shard_map/reduce_scatter | solution.py:55
  19.9 36.9 %collective-permute-start.8 = (bf16[640,1152]{1,0:T(8,128)(2,1)S(1)}, bf16[640,1152]{1,0:T(8,128)(2,1)S(1)}, u32[]{:S(2)}, u32[]{:S(2)}) collective-permute-start(bf16[640,1152]{1,0:T(8,128)(2,1)S(1)} %fusion.2), channel_id=1, source_target_pairs={{0,384},{48,432},{96,480},{144,528},{192,576},{240,624},{288,672},... | collective-permute-start | bytes 4423688 | tf_op jit(solution)/shard_map/ppermute | solution.py:19
  59.0 94.1 %reduce-scatter.3.cloned.1.call-start = ((), (), s32[]{:S(2)}) async-start(), calls=%async_computation.3 | async-start | bytes 1474560 | tf_op jit(solution)/shard_map/reduce_scatter | solution.py:122
  72.2 2.9 %copy-start = (bf16[2,640,1152]{2,1,0:T(8,128)(2,1)S(1)}, bf16[2,640,1152]{2,1,0:T(8,128)(2,1)}, u32[]{:S(2)}) copy-start(bf16[2,640,1152]{2,1,0:T(8,128)(2,1)} %all-gather.2.cloned.1.call-done) | copy-start | bytes 8847364
  77.1 31.5 %copy-start.3 = (bf16[512,1280]{1,0:T(8,128)(2,1)S(1)}, bf16[512,1280]{1,0:T(8,128)(2,1)}, u32[]{:S(2)}) copy-start(bf16[512,1280]{1,0:T(8,128)(2,1)} %param.4) | copy-start | bytes 3932164
  77.1 18.2 %collective-permute-start.2 = (bf16[128,1280]{1,0:T(8,128)(2,1)S(1)}, bf16[128,1280]{1,0:T(8,128)(2,1)S(1)}, u32[]{:S(2)}, u32[]{:S(2)}) collective-permute-start(bf16[128,1280]{1,0:T(8,128)(2,1)S(1)} %convolution_convert_fusion.1), channel_id=1, source_target_pairs={{0,11},{1,0},{2,1},{3,2},{4,3},{5,4},{6,5},{7,6},{8,7},{9,8},{10,9... | collective-permute-start | bytes 983048 | tf_op jit(solution)/shard_map/ppermute | solution.py:27
  83.8 11.5 %collective-permute-start.1 = (bf16[128,1280]{1,0:T(8,128)(2,1)S(1)}, bf16[128,1280]{1,0:T(8,128)(2,1)S(1)}, u32[]{:S(2)}, u32[]{:S(2)}) collective-permute-start(bf16[128,1280]{1,0:T(8,128)(2,1)S(1)} %convolution_convert_fusion.2), channel_id=1, source_target_pairs={{0,1},{1,2},{2,3},{3,4},{4,5},{5,6},{6,7},{7,8},{8,9},{9,10},{10,1... | collective-permute-start | bytes 983048 | tf_op jit(solution)/shard_map/ppermute | solution.py:27
  85.8 12.0 %collective-permute-start = (bf16[128,1280]{1,0:T(8,128)(2,1)S(1)}, bf16[128,1280]{1,0:T(8,128)(2,1)S(1)}, u32[]{:S(2)}, u32[]{:S(2)}) collective-permute-start(bf16[128,1280]{1,0:T(8,128)(2,1)S(1)} %convolution_convert_fusion.3), channel_id=1, source_target_pairs={{0,2},{1,3},{2,4},{3,5},{4,6},{5,7},{6,8},{7,9},{8,10},{9,11},{10,... | collective-permute-start | bytes 983048 | tf_op jit(solution)/shard_map/ppermute | solution.py:27
  98.8 24.6 %collective-permute-start.4 = (bf16[128,1280]{1,0:T(8,128)(2,1)S(1)}, bf16[128,1280]{1,0:T(8,128)(2,1)S(1)}, u32[]{:S(2)}, u32[]{:S(2)}) collective-permute-start(bf16[128,1280]{1,0:T(8,128)(2,1)S(1)} %add_convert_fusion.2), channel_id=1, source_target_pairs={{0,8},{1,9},{2,10},{3,11},{4,0},{5,1},{6,2},{7,3},{8,4},{9,5},{10,... | collective-permute-start | bytes 983048 | tf_op jit(solution)/shard_map/ppermute | solution.py:27
  105.1 26.8 %collective-permute-start.3 = (bf16[128,1280]{1,0:T(8,128)(2,1)S(1)}, bf16[128,1280]{1,0:T(8,128)(2,1)S(1)}, u32[]{:S(2)}, u32[]{:S(2)}) collective-permute-start(bf16[128,1280]{1,0:T(8,128)(2,1)S(1)} %add_convert_fusion.2), channel_id=1, source_target_pairs={{0,4},{1,5},{2,6},{3,7},{4,8},{5,9},{6,10},{7,11},{8,0},{9,1},{10,... | collective-permute-start | bytes 983048 | tf_op jit(solution)/shard_map/ppermute | solution.py:27
  132.3 13.2 %collective-permute-start.5 = (bf16[128,1280]{1,0:T(8,128)(2,1)S(1)}, bf16[128,1280]{1,0:T(8,128)(2,1)S(1)}, u32[]{:S(2)}, u32[]{:S(2)}) collective-permute-start(bf16[128,1280]{1,0:T(8,128)(2,1)S(1)} %get-tuple-element.16), channel_id=1, source_target_pairs={{0,2},{1,3},{2,4},{3,5},{4,6},{5,7},{6,8},{7,9},{8,10},{9,11},{10,... | collective-permute-start | bytes 983048 | tf_op jit(solution)/shard_map/ppermute | solution.py:27
  134.2 18.3 %collective-permute-start.6 = (bf16[128,1280]{1,0:T(8,128)(2,1)S(1)}, bf16[128,1280]{1,0:T(8,128)(2,1)S(1)}, u32[]{:S(2)}, u32[]{:S(2)}) collective-permute-start(bf16[128,1280]{1,0:T(8,128)(2,1)S(1)} %get-tuple-element.16), channel_id=1, source_target_pairs={{0,1},{1,2},{2,3},{3,4},{4,5},{5,6},{6,7},{7,8},{8,9},{9,10},{10,1... | collective-permute-start | bytes 983048 | tf_op jit(solution)/shard_map/ppermute | solution.py:27
  140.9 12.1 %collective-permute-start.7 = (bf16[128,1280]{1,0:T(8,128)(2,1)S(1)}, bf16[128,1280]{1,0:T(8,128)(2,1)S(1)}, u32[]{:S(2)}, u32[]{:S(2)}) collective-permute-start(bf16[128,1280]{1,0:T(8,128)(2,1)S(1)} %get-tuple-element.16), channel_id=1, source_target_pairs={{0,11},{1,0},{2,1},{3,2},{4,3},{5,4},{6,5},{7,6},{8,7},{9,8},{10,9... | collective-permute-start | bytes 983048 | tf_op jit(solution)/shard_map/ppermute | solution.py:27
  153.0 1.1 copy-start.1
Sparse Core Ops, SparseCore 0:
  16.7 55.5 all-gather.1
  75.9 44.1 reduce-scatter.4
  123.9 27.4 reduce-scatter.2

commit v9 on v8

--- a/solution.py
+++ b/solution.py
@@ -11,8 +11,11 @@
 BF16 = jnp.bfloat16
 
 Y_RINGS = [[h * NY + y for y in range(NY)] for h in range(2)]
-X_PAIRS = [[y, y + NY] for y in range(NY)]
 X_SWAP = [(i, (i + NY) % (2 * NY)) for i in range(2 * NY)]
+
+
+def y_shift(step):
+    return [(h * NY + y, h * NY + (y + step) % NY) for h in range(2) for y in range(NY)]
 
 
 def over_rep(value, pairs):
@@ -34,30 +37,53 @@
     return total.astype(BF16)
 
 
-def gather_weight(w0):
-    pair = lax.all_gather(w0, "rep", axis=0, tiled=True, axis_index_groups=X_PAIRS)
-    whole = lax.all_gather(pair, "rep", axis=1, tiled=True, axis_index_groups=Y_RINGS)
+def gather_weight(w0, y):
+    own = lax.all_gather(w0, "rep", axis=0, tiled=True, axis_index_groups=Y_RINGS)
+    there = over_rep(w0, X_SWAP)
+    from_m3 = over_rep(there, y_shift(3))
+    from_p3 = over_rep(there, y_shift(-3))
+    from_m1 = over_rep(jnp.concatenate([there, from_p3, from_m3]), y_shift(1))
+    from_p1 = over_rep(jnp.concatenate([there, from_m3]), y_shift(-1))
+    whole = jnp.zeros((2 * NY,) + w0.shape[1:], w0.dtype)
+    for source, steps in (
+        (there, (0,)),
+        (from_m3, (-3,)),
+        (from_p3, (3,)),
+        (from_m1, (-1, 2, 4)),
+        (from_p1, (1, -2)),
+    ):
+        for slot, step in enumerate(steps):
+            place = NY + lax.rem(y + step + NY, NY)
+            whole = lax.dynamic_update_slice(
+                whole, source[slot : slot + 1], (place, 0, 0)
+            )
+    whole = lax.dynamic_update_slice(whole, own, (0, 0, 0))
     return whole.reshape(-1, w0.shape[2])
 
 
-def scatter_wgrad(normed, masked, factor, first):
+def scatter_wgrad(normed, masked, factor, x_hi, keep_rows):
     half = normed.shape[1] // 2
-    left, right = normed[:, :half], normed[:, half:]
 
     def product(columns):
         value = lax.dot_general(
             columns, masked, (((0,), (0,)), ((), ())), preferred_element_type=F32
         )
-        return (value * factor).astype(BF16)
+        return (value * factor).astype(BF16).reshape(NY, keep_rows, -1)
 
-    came = over_rep(product(jnp.where(first, right, left)), X_SWAP)
-    both = add(product(jnp.where(first, left, right)), came)
-    return lax.psum_scatter(
-        both, "rep", scatter_dimension=0, tiled=True, axis_index_groups=Y_RINGS
+    value = jnp.stack([product(normed[:, :half]), product(normed[:, half:])], axis=1)
+    pair = lax.psum_scatter(
+        value.reshape(2 * NY, keep_rows, -1),
+        "rep",
+        scatter_dimension=0,
+        tiled=True,
+        axis_index_groups=Y_RINGS,
     )
+    kept = lax.dynamic_index_in_dim(pair, x_hi, 0)
+    sent = lax.dynamic_index_in_dim(pair, 1 - x_hi, 0)
+    return kept, over_rep(sent, X_SWAP)
 
 
-def sum_over_col(turned, weight, z, up):
+def sum_over_col(turned, weight, z, up, in_order, ready):
     def partial(tokens):
         value = lax.dot_general(
             tokens, weight, (((1,), (1,)), ((), ())), preferred_element_type=F32
@@ -80,7 +106,8 @@
     last = jnp.where(q == 0, below, jnp.where(q == 1, above, mine))
     one = jnp.where(q == 0, mine, below)
     two = jnp.where(q == 1, mine, above)
-    total = add(one, two, last)
+    total = in_order(add(one, two, last))
+    total, _ = lax.optimization_barrier((total, ready))
     arrived = (over_col(total, 2), over_col(total, 1), over_col(total, -1))
     result = jnp.zeros((4,) + total.shape, total.dtype)
     for step, value in ((0, total), (2, arrived[0]), (-1, arrived[1]), (1, arrived[2])):
@@ -94,18 +121,25 @@
     pair_count = lengths.shape[0]
     pair_len = row_count // pair_count
     keep_rows, unit_count = up_weight.shape[1:]
-    first = lax.axis_index("rep") < NY
+    rep = lax.axis_index("rep")
+    first = rep < NY
     z = lax.axis_index("col")
 
-    weight = gather_weight(up_weight)
+    def swap_halves(columns):
+        left, right = columns[:, : width // 2], columns[:, width // 2 :]
+        return jnp.concatenate(
+            [jnp.where(first, left, right), jnp.where(first, right, left)], axis=1
+        )
+
+    weight = gather_weight(up_weight, lax.rem(rep, NY))
 
     positions = lax.broadcasted_iota(jnp.int32, (pair_count, pair_len), 1)
     valid_rows = (positions < lengths[:, None]).reshape(row_count, 1)
     masked = jnp.where(valid_rows, cotangent, jnp.zeros_like(cotangent))
 
     factor = 1.0 / math.sqrt(row_count * lax.axis_size("rep"))
-    weight_grad = scatter_wgrad(normed, masked, factor, first)
-    weight_grad = weight_grad.reshape(1, keep_rows, unit_count)
+    kept, came = scatter_wgrad(normed, masked, factor, rep // NY, keep_rows)
+    weight_grad = add(kept, came)
 
     quarters = masked.reshape(4, row_count // 4, unit_count)
 
@@ -116,9 +150,9 @@
             for s in range(4)
         )
     )
-    normed_grad = sum_over_col(turned, weight, z, up)
+    normed_grad = sum_over_col(turned, weight, z, up, swap_halves, came)
 
-    up_partial = jnp.dot(normed, weight, preferred_element_type=F32)
+    up_partial = jnp.dot(swap_halves(normed), weight, preferred_element_type=F32)
     up_out = lax.psum_scatter(
         up_partial.astype(BF16), "row", scatter_dimension=0, tiled=True
     )

time: 163 us -> 191 us (1.17)
  the two profiles are of different devices: /device:TPU:6 before, /device:TPU:8 now
where the time goes in v9:
time: 191 us
  waiting for transfers between devices  90.6 us (47%)
  starting transfers between devices  57.4 us (30%)
  between operations  14.9 us (8%)
  matrix products  14.5 us (8%)
  local copies, waits for them, and re-layouts  7.78 us (4%)
  other arithmetic  5.39 us (3%)
    ppermute x6, waiting for transfers between devices, over_rep(): return lax.ppermute(value, 'rep', pairs)  47.3 us
    ppermute x8, waiting for transfers between devices, over_col(): return lax.ppermute(value, ('row', 'col'), pairs)  42.5 us
    ppermute x8, starting transfers between devices, over_col(): return lax.ppermute(value, ('row', 'col'), pairs)  35.7 us
    ppermute x6, starting transfers between devices, over_rep(): return lax.ppermute(value, 'rep', pairs)  21.5 us
    dot_general x4, matrix products, partial(): lax.dot_general(tokens, weight, (((1,), (1,)), ((), ())), preferred_eleme...  8.26 us
  transfers between devices with their start and end apart: 17, of which 9 were waited for; matrix products, arithmetic and copies ran while one was open for 14% of the time, Pallas kernels for 0%

profile of v9, /device:TPU:8, one launch (start us, length us, event | category | flops | bytes accessed | tf_op | source)
XLA Modules:
  0.0 190.6 jit_solution(7792004804005092763)
XLA Ops:
  7.9 4.9 %collective-permute-start = (bf16[1,80,1152]{2,1,0:T(8,128)(2,1)}, bf16[1,80,1152]{2,1,0:T(8,128)(2,1)S(1)}, u32[]{:S(2)}, u32[]{:S(2)}) collective-permute-start(bf16[1,80,1152]{2,1,0:T(8,128)(2,1)} %param.5), channel_id=1, source_target_pairs={{0,384},{48,432},{96,480},{144,528},{192,576},{240,624},{288,672},... | collective-permute-start | bytes 552968 | tf_op jit(solution)/shard_map/ppermute | solution.py:22
  13.5 1.5 broadcast_select_fusion
  15.0 2.3 %fusion.1 = bf16[1152,640]{0,1:T(8,128)(2,1)S(1)} fusion(bf16[512,1152]{1,0:T(8,128)(2,1)S(1)} %broadcast_select_fusion, bf16[512,1280]{1,0:T(8,128)(2,1)} %param.4), kind=kOutput, calls=%fused_computation.3 | convolution fusion | flops 756449280 | bytes 3309568 | tf_op jit(solution)/shard_map/dot_general | solution.py:68
  18.7 1.8 copy.8
  21.6 6.7 %collective-permute-start.1 = (bf16[1,80,1152]{2,1,0:T(8,128)(2,1)S(1)}, bf16[1,80,1152]{2,1,0:T(8,128)(2,1)S(1)}, u32[]{:S(2)}, u32[]{:S(2)}) collective-permute-start(bf16[1,80,1152]{2,1,0:T(8,128)(2,1)S(1)} %collective-permute-done), channel_id=1, source_target_pairs={{0,144},{48,192},{96,240},{144,288},{192,336},{240,0},{288,48},{33... | collective-permute-start | bytes 552968 | tf_op jit(solution)/shard_map/ppermute | solution.py:22
  28.3 2.1 %collective-permute-start.2 = (bf16[1,80,1152]{2,1,0:T(8,128)(2,1)S(1)}, bf16[1,80,1152]{2,1,0:T(8,128)(2,1)S(1)}, u32[]{:S(2)}, u32[]{:S(2)}) collective-permute-start(bf16[1,80,1152]{2,1,0:T(8,128)(2,1)S(1)} %collective-permute-done), channel_id=1, source_target_pairs={{0,240},{48,288},{96,336},{144,0},{192,48},{240,96},{288,144},{336... | collective-permute-start | bytes 552968 | tf_op jit(solution)/shard_map/ppermute | solution.py:22
  30.7 11.0 %collective-permute-done.1 = bf16[1,80,1152]{2,1,0:T(8,128)(2,1)S(1)} collective-permute-done((bf16[1,80,1152]{2,1,0:T(8,128)(2,1)S(1)}, bf16[1,80,1152]{2,1,0:T(8,128)(2,1)S(1)}, u32[]{:S(2)}, u32[]{:S(2)}) %collective-permute-start.1) | collective-permute-done | bytes 184352 | tf_op jit(solution)/shard_map/ppermute | solution.py:22
  41.7 8.6 %collective-permute-done.2 = bf16[1,80,1152]{2,1,0:T(8,128)(2,1)S(1)} collective-permute-done((bf16[1,80,1152]{2,1,0:T(8,128)(2,1)S(1)}, bf16[1,80,1152]{2,1,0:T(8,128)(2,1)S(1)}, u32[]{:S(2)}, u32[]{:S(2)}) %collective-permute-start.2) | collective-permute-done | bytes 184352 | tf_op jit(solution)/shard_map/ppermute | solution.py:22
  50.4 2.3 %collective-permute-start.3 = (bf16[3,80,1152]{2,1,0:T(8,128)(2,1)S(1)}, bf16[3,80,1152]{2,1,0:T(8,128)(2,1)S(1)}, u32[]{:S(2)}, u32[]{:S(2)}) collective-permute-start(bf16[3,80,1152]{2,1,0:T(8,128)(2,1)S(1)} %pad_maximum_fusion.1), channel_id=1, source_target_pairs={{0,48},{48,96},{96,144},{144,192},{192,240},{240,288},{288,336},{3... | collective-permute-start | bytes 1658888 | tf_op jit(solution)/shard_map/ppermute | solution.py:22
  52.8 3.5 %collective-permute-start.4 = (bf16[2,80,1152]{2,1,0:T(8,128)(2,1)S(1)}, bf16[2,80,1152]{2,1,0:T(8,128)(2,1)S(1)}, u32[]{:S(2)}, u32[]{:S(2)}) collective-permute-start(bf16[2,80,1152]{2,1,0:T(8,128)(2,1)S(1)} %pad_maximum_fusion.2), channel_id=1, source_target_pairs={{0,336},{48,0},{96,48},{144,96},{192,144},{240,192},{288,240},{336... | collective-permute-start | bytes 1105928 | tf_op jit(solution)/shard_map/ppermute | solution.py:22
  56.4 15.3 %collective-permute-done.3 = bf16[3,80,1152]{2,1,0:T(8,128)(2,1)S(1)} collective-permute-done((bf16[3,80,1152]{2,1,0:T(8,128)(2,1)S(1)}, bf16[3,80,1152]{2,1,0:T(8,128)(2,1)S(1)}, u32[]{:S(2)}, u32[]{:S(2)}) %collective-permute-start.3) | collective-permute-done | bytes 552992 | tf_op jit(solution)/shard_map/ppermute | solution.py:22
  71.9 1.6 constant_dynamic-update-slice_fusion
  73.5 2.6 %convolution_convert_fusion.3 = bf16[128,1280]{1,0:T(8,128)(2,1)} fusion(bf16[128,1152]{1,0:T(8,128)(2,1)} %get-tuple-element.11, bf16[1280,1152]{1,0:T(8,128)(2,1)S(1)} %bitcast.39), kind=kOutput, calls=%fused_computation.8 | convolution fusion | flops 377651200 | bytes 3571712 | tf_op jit(solution)/shard_map/dot_general | solution.py:88
  76.2 1.7 convolution_convert_fusion.1
  77.8 12.8 %collective-permute-start.7 = (bf16[128,1280]{1,0:T(8,128)(2,1)}, bf16[128,1280]{1,0:T(8,128)(2,1)}, u32[]{:S(2)}, u32[]{:S(2)}) collective-permute-start(bf16[128,1280]{1,0:T(8,128)(2,1)} %convolution_convert_fusion.1), channel_id=1, source_target_pairs={{0,11},{1,0},{2,1},{3,2},{4,3},{5,4},{6,5},{7,6},{8,7},{9,8},{10,9... | collective-permute-start | bytes 983048 | tf_op jit(solution)/shard_map/ppermute | solution.py:30
  90.7 1.7 convolution_convert_fusion.2
  92.4 1.9 %collective-permute-start.6 = (bf16[128,1280]{1,0:T(8,128)(2,1)}, bf16[128,1280]{1,0:T(8,128)(2,1)S(1)}, u32[]{:S(2)}, u32[]{:S(2)}) collective-permute-start(bf16[128,1280]{1,0:T(8,128)(2,1)} %convolution_convert_fusion.2), channel_id=1, source_target_pairs={{0,1},{1,2},{2,3},{3,4},{4,5},{5,6},{6,7},{7,8},{8,9},{9,10},{10,1... | collective-permute-start | bytes 983048 | tf_op jit(solution)/shard_map/ppermute | solution.py:30
  94.3 1.9 %collective-permute-start.5 = (bf16[128,1280]{1,0:T(8,128)(2,1)}, bf16[128,1280]{1,0:T(8,128)(2,1)}, u32[]{:S(2)}, u32[]{:S(2)}) collective-permute-start(bf16[128,1280]{1,0:T(8,128)(2,1)} %convolution_convert_fusion.3), channel_id=1, source_target_pairs={{0,2},{1,3},{2,4},{3,5},{4,6},{5,7},{6,8},{7,9},{8,10},{9,11},{10,... | collective-permute-start | bytes 983048 | tf_op jit(solution)/shard_map/ppermute | solution.py:30
  97.7 7.6 %collective-permute-done.6 = bf16[128,1280]{1,0:T(8,128)(2,1)S(1)} collective-permute-done((bf16[128,1280]{1,0:T(8,128)(2,1)}, bf16[128,1280]{1,0:T(8,128)(2,1)S(1)}, u32[]{:S(2)}, u32[]{:S(2)}) %collective-permute-start.6) | collective-permute-done | bytes 327712 | tf_op jit(solution)/shard_map/ppermute | solution.py:30
  106.1 2.3 %collective-permute-done.5 = bf16[128,1280]{1,0:T(8,128)(2,1)} collective-permute-done((bf16[128,1280]{1,0:T(8,128)(2,1)}, bf16[128,1280]{1,0:T(8,128)(2,1)}, u32[]{:S(2)}, u32[]{:S(2)}) %collective-permute-start.5) | collective-permute-done | bytes 327712 | tf_op jit(solution)/shard_map/ppermute | solution.py:30
  108.4 2.3 %fusion.6 = bf16[128,1280]{1,0:T(8,128)(2,1)S(1)} fusion(bf16[128,1152]{1,0:T(8,128)(2,1)} %get-tuple-element.10, bf16[1280,1152]{1,0:T(8,128)(2,1)S(1)} %bitcast.42, bf16[128,1280]{1,0:T(8,128)(2,1)} %collective-permute-done.7, bf16[128,1280]{1,0:T(8,128)(2,1)} %copy-done.4, bf16[128,1280]{1,0:T(8,128)(2,1)} %collective-permute-done.5), kind=kOutput, calls=%fused_computation.14 | convolution fusion | flops 378961920 | bytes 4554752 | tf_op jit(solution)/shard_map/dot_general | solution.py:88
  110.6 5.3 %collective-permute-start.9 = (bf16[128,1280]{1,0:T(8,128)(2,1)S(1)}, bf16[128,1280]{1,0:T(8,128)(2,1)}, u32[]{:S(2)}, u32[]{:S(2)}) collective-permute-start(bf16[128,1280]{1,0:T(8,128)(2,1)S(1)} %fusion.6), channel_id=1, source_target_pairs={{0,8},{1,9},{2,10},{3,11},{4,0},{5,1},{6,2},{7,3},{8,4},{9,5},{10,... | collective-permute-start | bytes 983048 | tf_op jit(solution)/shard_map/ppermute | solution.py:30
  115.9 4.5 %collective-permute-start.8 = (bf16[128,1280]{1,0:T(8,128)(2,1)S(1)}, bf16[128,1280]{1,0:T(8,128)(2,1)}, u32[]{:S(2)}, u32[]{:S(2)}) collective-permute-start(bf16[128,1280]{1,0:T(8,128)(2,1)S(1)} %fusion.6), channel_id=1, source_target_pairs={{0,4},{1,5},{2,6},{3,7},{4,8},{5,9},{6,10},{7,11},{8,0},{9,1},{10,... | collective-permute-start | bytes 983048 | tf_op jit(solution)/shard_map/ppermute | solution.py:30
  120.4 2.9 %convolution_convert_fusion = bf16[512,1152]{1,0:T(8,128)(2,1)} fusion(bf16[1280,1152]{1,0:T(8,128)(2,1)S(1)} %bitcast.43, bf16[512,640]{1,0:T(8,128)(2,1)S(1)} %get-tuple-element.18, bf16[512,640]{1,0:T(8,128)(2,1)S(1)} %get-tuple-element.17), kind=kOutput, calls=%fused_computation.4 | convolution fusion | flops 1513160704 | bytes 5439488 | tf_op jit(solution)/shard_map/dot_general | solution.py:155
  123.3 21.8 %collective-permute-done.9 = bf16[128,1280]{1,0:T(8,128)(2,1)} collective-permute-done((bf16[128,1280]{1,0:T(8,128)(2,1)S(1)}, bf16[128,1280]{1,0:T(8,128)(2,1)}, u32[]{:S(2)}, u32[]{:S(2)}) %collective-permute-start.9) | collective-permute-done | bytes 327712 | tf_op jit(solution)/shard_map/ppermute | solution.py:30
  147.4 1.9 %collective-permute-start.10 = (bf16[1,80,1152]{2,1,0:T(8,128)(2,1)S(1)}, bf16[1,80,1152]{2,1,0:T(8,128)(2,1)S(1)}, u32[]{:S(2)}, u32[]{:S(2)}) collective-permute-start(bf16[1,80,1152]{2,1,0:T(8,128)(2,1)S(1)} %constant_dynamic-slice_fusion), channel_id=1, source_target_pairs={{0,384},{48,432},{96,480},{144,528},{192,576},{240,624},{288,672},... | collective-permute-start | bytes 552968 | tf_op jit(solution)/shard_map/ppermute | solution.py:22
  149.4 12.5 %collective-permute-done.10 = bf16[1,80,1152]{2,1,0:T(8,128)(2,1)S(1)} collective-permute-done((bf16[1,80,1152]{2,1,0:T(8,128)(2,1)S(1)}, bf16[1,80,1152]{2,1,0:T(8,128)(2,1)S(1)}, u32[]{:S(2)}, u32[]{:S(2)}) %collective-permute-start.10) | collective-permute-done | bytes 184352 | tf_op jit(solution)/shard_map/ppermute | solution.py:22
  161.8 1.9 %collective-permute-start.11 = (bf16[128,1280]{1,0:T(8,128)(2,1)S(1)}, bf16[128,1280]{1,0:T(8,128)(2,1)S(1)}, u32[]{:S(2)}, u32[]{:S(2)}) collective-permute-start(bf16[128,1280]{1,0:T(8,128)(2,1)S(1)} %pad_maximum_fusion.3), channel_id=1, source_target_pairs={{0,2},{1,3},{2,4},{3,5},{4,6},{5,7},{6,8},{7,9},{8,10},{9,11},{10,... | collective-permute-start | bytes 983048 | tf_op jit(solution)/shard_map/ppermute | solution.py:30
  163.8 2.8 %collective-permute-start.12 = (bf16[128,1280]{1,0:T(8,128)(2,1)S(1)}, bf16[128,1280]{1,0:T(8,128)(2,1)S(1)}, u32[]{:S(2)}, u32[]{:S(2)}) collective-permute-start(bf16[128,1280]{1,0:T(8,128)(2,1)S(1)} %pad_maximum_fusion.3), channel_id=1, source_target_pairs={{0,1},{1,2},{2,3},{3,4},{4,5},{5,6},{6,7},{7,8},{8,9},{9,10},{10,1... | collective-permute-start | bytes 983048 | tf_op jit(solution)/shard_map/ppermute | solution.py:30
  166.6 4.6 %collective-permute-start.13 = (bf16[128,1280]{1,0:T(8,128)(2,1)S(1)}, bf16[128,1280]{1,0:T(8,128)(2,1)S(1)}, u32[]{:S(2)}, u32[]{:S(2)}) collective-permute-start(bf16[128,1280]{1,0:T(8,128)(2,1)S(1)} %pad_maximum_fusion.3), channel_id=1, source_target_pairs={{0,11},{1,0},{2,1},{3,2},{4,3},{5,4},{6,5},{7,6},{8,7},{9,8},{10,9... | collective-permute-start | bytes 983048 | tf_op jit(solution)/shard_map/ppermute | solution.py:30
  172.1 5.9 %collective-permute-done.11 = bf16[128,1280]{1,0:T(8,128)(2,1)S(1)} collective-permute-done((bf16[128,1280]{1,0:T(8,128)(2,1)S(1)}, bf16[128,1280]{1,0:T(8,128)(2,1)S(1)}, u32[]{:S(2)}, u32[]{:S(2)}) %collective-permute-start.11) | collective-permute-done | bytes 327712 | tf_op jit(solution)/shard_map/ppermute | solution.py:30
  177.9 5.0 %collective-permute-done.12 = bf16[128,1280]{1,0:T(8,128)(2,1)S(1)} collective-permute-done((bf16[128,1280]{1,0:T(8,128)(2,1)S(1)}, bf16[128,1280]{1,0:T(8,128)(2,1)S(1)}, u32[]{:S(2)}, u32[]{:S(2)}) %collective-permute-start.12) | collective-permute-done | bytes 327712 | tf_op jit(solution)/shard_map/ppermute | solution.py:30
  (50 shorter events, 10.2 us)
Async XLA Ops:
  7.2 64.7 %all-gather.2.cloned.1.call-start = ((), (), s32[]{:S(2)}) async-start(), calls=%async_computation.2 | async-start | bytes 1658880 | tf_op jit(solution)/shard_map/all_gather | solution.py:41
  7.9 138.5 %reduce-scatter.5.cloned.1.call-start = ((), (), s32[]{:S(2)}) async-start(), calls=%async_computation.4 | async-start | bytes 3317760 | tf_op jit(solution)/shard_map/reduce_scatter | solution.py:74
  7.9 13.7 %collective-permute-start = (bf16[1,80,1152]{2,1,0:T(8,128)(2,1)}, bf16[1,80,1152]{2,1,0:T(8,128)(2,1)S(1)}, u32[]{:S(2)}, u32[]{:S(2)}) collective-permute-start(bf16[1,80,1152]{2,1,0:T(8,128)(2,1)} %param.5), channel_id=1, source_target_pairs={{0,384},{48,432},{96,480},{144,528},{192,576},{240,624},{288,672},... | collective-permute-start | bytes 552968 | tf_op jit(solution)/shard_map/ppermute | solution.py:22
  15.0 2.3 %copy-start.1 = (bf16[512,1280]{1,0:T(8,128)(2,1)S(1)}, bf16[512,1280]{1,0:T(8,128)(2,1)}, u32[]{:S(2)}) copy-start(bf16[512,1280]{1,0:T(8,128)(2,1)} %param.4) | copy-start | bytes 3932164
  20.5 162.5 %reduce-scatter.3.cloned.1.call-start = ((), (), s32[]{:S(2)}) async-start(), calls=%async_computation.3 | async-start | bytes 1474560 | tf_op jit(solution)/shard_map/reduce_scatter | solution.py:156
  21.6 20.1 %collective-permute-start.1 = (bf16[1,80,1152]{2,1,0:T(8,128)(2,1)S(1)}, bf16[1,80,1152]{2,1,0:T(8,128)(2,1)S(1)}, u32[]{:S(2)}, u32[]{:S(2)}) collective-permute-start(bf16[1,80,1152]{2,1,0:T(8,128)(2,1)S(1)} %collective-permute-done), channel_id=1, source_target_pairs={{0,144},{48,192},{96,240},{144,288},{192,336},{240,0},{288,48},{33... | collective-permute-start | bytes 552968 | tf_op jit(solution)/shard_map/ppermute | solution.py:22
  28.3 22.0 %collective-permute-start.2 = (bf16[1,80,1152]{2,1,0:T(8,128)(2,1)S(1)}, bf16[1,80,1152]{2,1,0:T(8,128)(2,1)S(1)}, u32[]{:S(2)}, u32[]{:S(2)}) collective-permute-start(bf16[1,80,1152]{2,1,0:T(8,128)(2,1)S(1)} %collective-permute-done), channel_id=1, source_target_pairs={{0,240},{48,288},{96,336},{144,0},{192,48},{240,96},{288,144},{336... | collective-permute-start | bytes 552968 | tf_op jit(solution)/shard_map/ppermute | solution.py:22
  50.4 21.3 %collective-permute-start.3 = (bf16[3,80,1152]{2,1,0:T(8,128)(2,1)S(1)}, bf16[3,80,1152]{2,1,0:T(8,128)(2,1)S(1)}, u32[]{:S(2)}, u32[]{:S(2)}) collective-permute-start(bf16[3,80,1152]{2,1,0:T(8,128)(2,1)S(1)} %pad_maximum_fusion.1), channel_id=1, source_target_pairs={{0,48},{48,96},{96,144},{144,192},{192,240},{240,288},{288,336},{3... | collective-permute-start | bytes 1658888 | tf_op jit(solution)/shard_map/ppermute | solution.py:22
  52.8 19.0 %collective-permute-start.4 = (bf16[2,80,1152]{2,1,0:T(8,128)(2,1)S(1)}, bf16[2,80,1152]{2,1,0:T(8,128)(2,1)S(1)}, u32[]{:S(2)}, u32[]{:S(2)}) collective-permute-start(bf16[2,80,1152]{2,1,0:T(8,128)(2,1)S(1)} %pad_maximum_fusion.2), channel_id=1, source_target_pairs={{0,336},{48,0},{96,48},{144,96},{192,144},{240,192},{288,240},{336... | collective-permute-start | bytes 1105928 | tf_op jit(solution)/shard_map/ppermute | solution.py:22
  71.9 4.3 %copy-start.2 = (bf16[128,1152]{1,0:T(8,128)(2,1)S(1)}, bf16[128,1152]{1,0:T(8,128)(2,1)}, u32[]{:S(2)}) copy-start(bf16[128,1152]{1,0:T(8,128)(2,1)} %get-tuple-element.15) | copy-start | bytes 884740
  77.8 19.9 %collective-permute-start.7 = (bf16[128,1280]{1,0:T(8,128)(2,1)}, bf16[128,1280]{1,0:T(8,128)(2,1)}, u32[]{:S(2)}, u32[]{:S(2)}) collective-permute-start(bf16[128,1280]{1,0:T(8,128)(2,1)} %convolution_convert_fusion.1), channel_id=1, source_target_pairs={{0,11},{1,0},{2,1},{3,2},{4,3},{5,4},{6,5},{7,6},{8,7},{9,8},{10,9... | collective-permute-start | bytes 983048 | tf_op jit(solution)/shard_map/ppermute | solution.py:30
  92.4 13.0 %collective-permute-start.6 = (bf16[128,1280]{1,0:T(8,128)(2,1)}, bf16[128,1280]{1,0:T(8,128)(2,1)S(1)}, u32[]{:S(2)}, u32[]{:S(2)}) collective-permute-start(bf16[128,1280]{1,0:T(8,128)(2,1)} %convolution_convert_fusion.2), channel_id=1, source_target_pairs={{0,1},{1,2},{2,3},{3,4},{4,5},{5,6},{6,7},{7,8},{8,9},{9,10},{10,1... | collective-permute-start | bytes 983048 | tf_op jit(solution)/shard_map/ppermute | solution.py:30
  94.3 14.1 %collective-permute-start.5 = (bf16[128,1280]{1,0:T(8,128)(2,1)}, bf16[128,1280]{1,0:T(8,128)(2,1)}, u32[]{:S(2)}, u32[]{:S(2)}) collective-permute-start(bf16[128,1280]{1,0:T(8,128)(2,1)} %convolution_convert_fusion.3), channel_id=1, source_target_pairs={{0,2},{1,3},{2,4},{3,5},{4,6},{5,7},{6,8},{7,9},{8,10},{9,11},{10,... | collective-permute-start | bytes 983048 | tf_op jit(solution)/shard_map/ppermute | solution.py:30
  105.3 0.7 copy-start.4
  110.6 34.5 %collective-permute-start.9 = (bf16[128,1280]{1,0:T(8,128)(2,1)S(1)}, bf16[128,1280]{1,0:T(8,128)(2,1)}, u32[]{:S(2)}, u32[]{:S(2)}) collective-permute-start(bf16[128,1280]{1,0:T(8,128)(2,1)S(1)} %fusion.6), channel_id=1, source_target_pairs={{0,8},{1,9},{2,10},{3,11},{4,0},{5,1},{6,2},{7,3},{8,4},{9,5},{10,... | collective-permute-start | bytes 983048 | tf_op jit(solution)/shard_map/ppermute | solution.py:30
  115.9 29.2 %collective-permute-start.8 = (bf16[128,1280]{1,0:T(8,128)(2,1)S(1)}, bf16[128,1280]{1,0:T(8,128)(2,1)}, u32[]{:S(2)}, u32[]{:S(2)}) collective-permute-start(bf16[128,1280]{1,0:T(8,128)(2,1)S(1)} %fusion.6), channel_id=1, source_target_pairs={{0,4},{1,5},{2,6},{3,7},{4,8},{5,9},{6,10},{7,11},{8,0},{9,1},{10,... | collective-permute-start | bytes 983048 | tf_op jit(solution)/shard_map/ppermute | solution.py:30
  146.4 24.9 %copy-start.3 = (bf16[2,80,1152]{2,1,0:T(8,128)(2,1)S(1)}, bf16[2,80,1152]{2,1,0:T(8,128)(2,1)}, u32[]{:S(2)}) copy-start(bf16[2,80,1152]{2,1,0:T(8,128)(2,1)} %reduce-scatter.5.cloned.1.call-done) | copy-start | bytes 1105924
  147.4 14.4 %collective-permute-start.10 = (bf16[1,80,1152]{2,1,0:T(8,128)(2,1)S(1)}, bf16[1,80,1152]{2,1,0:T(8,128)(2,1)S(1)}, u32[]{:S(2)}, u32[]{:S(2)}) collective-permute-start(bf16[1,80,1152]{2,1,0:T(8,128)(2,1)S(1)} %constant_dynamic-slice_fusion), channel_id=1, source_target_pairs={{0,384},{48,432},{96,480},{144,528},{192,576},{240,624},{288,672},... | collective-permute-start | bytes 552968 | tf_op jit(solution)/shard_map/ppermute | solution.py:22
  161.8 16.1 %collective-permute-start.11 = (bf16[128,1280]{1,0:T(8,128)(2,1)S(1)}, bf16[128,1280]{1,0:T(8,128)(2,1)S(1)}, u32[]{:S(2)}, u32[]{:S(2)}) collective-permute-start(bf16[128,1280]{1,0:T(8,128)(2,1)S(1)} %pad_maximum_fusion.3), channel_id=1, source_target_pairs={{0,2},{1,3},{2,4},{3,5},{4,6},{5,7},{6,8},{7,9},{8,10},{9,11},{10,... | collective-permute-start | bytes 983048 | tf_op jit(solution)/shard_map/ppermute | solution.py:30
  163.8 19.1 %collective-permute-start.12 = (bf16[128,1280]{1,0:T(8,128)(2,1)S(1)}, bf16[128,1280]{1,0:T(8,128)(2,1)S(1)}, u32[]{:S(2)}, u32[]{:S(2)}) collective-permute-start(bf16[128,1280]{1,0:T(8,128)(2,1)S(1)} %pad_maximum_fusion.3), channel_id=1, source_target_pairs={{0,1},{1,2},{2,3},{3,4},{4,5},{5,6},{6,7},{7,8},{8,9},{9,10},{10,1... | collective-permute-start | bytes 983048 | tf_op jit(solution)/shard_map/ppermute | solution.py:30
  166.6 16.3 %collective-permute-start.13 = (bf16[128,1280]{1,0:T(8,128)(2,1)S(1)}, bf16[128,1280]{1,0:T(8,128)(2,1)S(1)}, u32[]{:S(2)}, u32[]{:S(2)}) collective-permute-start(bf16[128,1280]{1,0:T(8,128)(2,1)S(1)} %pad_maximum_fusion.3), channel_id=1, source_target_pairs={{0,11},{1,0},{2,1},{3,2},{4,3},{5,4},{6,5},{7,6},{8,7},{9,8},{10,9... | collective-permute-start | bytes 983048 | tf_op jit(solution)/shard_map/ppermute | solution.py:30
  183.0 1.1 copy-start
Sparse Core Ops, SparseCore 0:
  10.4 59.9 all-gather.1
  73.5 51.2 reduce-scatter.4
  128.9 33.3 reduce-scatter.2

commit v10 on v8

--- a/solution.py
+++ b/solution.py
@@ -58,20 +58,12 @@
 
 
 def sum_over_col(turned, weight, z, up):
-    def partial(tokens):
-        value = lax.dot_general(
-            tokens, weight, (((1,), (1,)), ((), ())), preferred_element_type=F32
-        )
-        return value.astype(BF16)
-
-    two_away = partial(turned[2])
-    ahead, behind, _ = lax.optimization_barrier((turned[1], turned[3], two_away))
-    arrived = (
-        over_col(two_away, 2),
-        over_col(partial(ahead), 1),
-        over_col(partial(behind), -1),
+    products = lax.dot_general(
+        turned, weight, (((1,), (1,)), ((), ())), preferred_element_type=F32
     )
-    mine = add(partial(turned[0]), *arrived)
+    two_away, ahead, behind, kept = jnp.split(products.astype(BF16), 4)
+    arrived = (over_col(two_away, 2), over_col(ahead, 1), over_col(behind, -1))
+    mine = add(kept, *arrived)
     from_behind = over_col(mine, 4)
     from_ahead = over_col(mine, -4)
     below = jnp.where(up == 1, from_behind, from_ahead)
@@ -111,9 +103,13 @@
 
     up = 1 - 2 * lax.rem(lax.axis_index("row"), 2)
     turned = lax.optimization_barrier(
-        tuple(
-            lax.dynamic_index_in_dim(quarters, lax.rem(z + s * up + NZ, 4), 0, keepdims=False)
-            for s in range(4)
+        jnp.concatenate(
+            [
+                lax.dynamic_index_in_dim(
+                    quarters, lax.rem(z + s * up + NZ, 4), 0, keepdims=False
+                )
+                for s in (2, 1, -1, 0)
+            ]
         )
     )
     normed_grad = sum_over_col(turned, weight, z, up)

time: 163 us -> 164 us (level)
  waiting for transfers between devices: 83.8 us -> 91.3 us
  starting transfers between devices: 37.7 us -> 33.6 us
  matrix products: 12 us -> 9.91 us
    ppermute x8, waiting for transfers between devices: 37.9 us -> 45.5 us  [over_col(): return lax.ppermute(value, ('row', 'col'), pairs)]
    ppermute x8, starting transfers between devices: 33.5 us -> 29.5 us  [over_col(): return lax.ppermute(value, ('row', 'col'), pairs)]
    dot_general x4 -> x1, matrix products: 5.82 us -> 3.72 us  [sum_over_col(): lax.dot_general(turned, weight, (((1,), (1,)), ((), ())), preferred_eleme...]
  transfers between devices with their start and end apart: 12 -> 12, of which waited for: 9 -> 8; matrix products, arithmetic and copies ran while one was open for 9% -> 8% of each run, Pallas kernels for 0% -> 0%
where the time goes in v10:
time: 164 us; the launch traced here: 162 us
  waiting for transfers between devices  91.3 us (56%)
  starting transfers between devices  33.6 us (20%)
  between operations  14.8 us (9%)
  matrix products  9.91 us (6%)
  blocking collectives  9.31 us (6%)
  other arithmetic  1.99 us (1%)
    ppermute x8, waiting for transfers between devices, over_col(): return lax.ppermute(value, ('row', 'col'), pairs)  45.5 us
    ppermute x1, waiting for transfers between devices, over_rep(): return lax.ppermute(value, 'rep', pairs)  32.8 us
    ppermute x8, starting transfers between devices, over_col(): return lax.ppermute(value, ('row', 'col'), pairs)  29.5 us
    all_gather x1, waiting for transfers between devices, gather_weight(): lax.all_gather(pair, 'rep', axis=1, tiled=True, axis_index_groups=Y_RINGS)  12.9 us
    all_gather x1, blocking collectives, gather_weight(): lax.all_gather(w0, 'rep', axis=0, tiled=True, axis_index_groups=X_PAIRS)  9.31 us
    ppermute x1, starting transfers between devices, over_rep(): return lax.ppermute(value, 'rep', pairs)  4.03 us
    dot_general x1, matrix products, sum_over_col(): lax.dot_general(turned, weight, (((1,), (1,)), ((), ())), preferred_eleme...  3.72 us
  transfers between devices with their start and end apart: 12, of which 8 were waited for; matrix products, arithmetic and copies ran while one was open for 8% of the time, Pallas kernels for 0%

profile of v10, /device:TPU:6, one launch (start us, length us, event | category | flops | bytes accessed | tf_op | source)
XLA Modules:
  0.0 162.3 jit_solution(3373348429526072974)
XLA Ops:
  7.2 9.3 %all_gather.6 = bf16[2,80,1152]{2,1,0:T(8,128)(2,1)} all-gather(bf16[1,80,1152]{2,1,0:T(8,128)(2,1)} %param.5), channel_id=1, replica_groups={{0,384},{48,432},{96,480},{144,528},{192,576},{240,624},{288,672},{336,..., dimensions={0}, use_global_device_ids=true | all-gather | bytes 552960 | tf_op jit(solution)/shard_map/all_gather | solution.py:38
  16.5 0.0 reduce-scatter.5.cloned.1.call-start
  17.4 1.5 broadcast_select_fusion
  18.8 1.1 fusion.2
  19.9 4.0 %collective-permute-start.8 = (bf16[640,1152]{1,0:T(8,128)(2,1)S(1)}, bf16[640,1152]{1,0:T(8,128)(2,1)S(1)}, u32[]{:S(2)}, u32[]{:S(2)}) collective-permute-start(bf16[640,1152]{1,0:T(8,128)(2,1)S(1)} %fusion.2), channel_id=1, source_target_pairs={{0,384},{48,432},{96,480},{144,528},{192,576},{240,624},{288,672},... | collective-permute-start | bytes 4423688 | tf_op jit(solution)/shard_map/ppermute | solution.py:19
  23.9 32.8 %collective-permute-done.8 = bf16[640,1152]{1,0:T(8,128)(2,1)S(1)} collective-permute-done((bf16[640,1152]{1,0:T(8,128)(2,1)S(1)}, bf16[640,1152]{1,0:T(8,128)(2,1)S(1)}, u32[]{:S(2)}, u32[]{:S(2)}) %collective-permute-start.8) | collective-permute-done | bytes 1474592 | tf_op jit(solution)/shard_map/ppermute | solution.py:19
  56.8 2.2 %add_convert_fusion = bf16[640,1152]{1,0:T(8,128)(2,1)} fusion(bf16[640,1152]{1,0:T(8,128)(2,1)S(1)} %collective-permute-done.8, bf16[512,1152]{1,0:T(8,128)(2,1)S(1)} %broadcast_select_fusion, pred[]{:T(512)S(6)} %lt.43, bf16[512,1280]{1,0:T(8,128)(2,1)S(1)} %copy-done.2), kind=kOutput, calls=%fused_computation.7 | convolution fusion | flops 759726080 | bytes 5439489 | tf_op jit(solution)/shard_map/dot_general | solution.py:48
  59.0 0.0 reduce-scatter.3.cloned.1.call-start
  59.1 0.1 dynamic-slice_bitcast_fusion.3
  59.2 0.1 pad_maximum_fusion
  59.3 12.9 %all-gather.2.cloned.1.call-done = bf16[2,640,1152]{2,1,0:T(8,128)(2,1)} async-done(((bf16[2,80,1152]{2,1,0:T(8,128)(2,1)}), bf16[2,640,1152]{2,1,0:T(8,128)(2,1)}) %all-gather.2.cloned.1.call-update) | async-done | bytes 2949136 | tf_op jit(solution)/shard_map/all_gather | solution.py:39
  72.2 3.7 %convolution_convert_fusion = bf16[512,1280]{1,0:T(8,128)(2,1)S(1)} fusion(bf16[512,1152]{1,0:T(8,128)(2,1)S(1)} %pad_maximum_fusion, bf16[1280,1152]{1,0:T(8,128)(2,1)} %bitcast.30), kind=kOutput, calls=%fused_computation.5 | convolution fusion | flops 1510604800 | bytes 5439488 | tf_op jit(solution)/shard_map/dot_general | solution.py:61
  76.0 0.1 fusion.11
  76.0 4.9 %collective-permute-start = (bf16[128,1280]{1,0:T(8,128)(2,1)S(1)}, bf16[128,1280]{1,0:T(8,128)(2,1)S(1)}, u32[]{:S(2)}, u32[]{:S(2)}) collective-permute-start(bf16[128,1280]{1,0:T(8,128)(2,1)S(1)} %get-tuple-element.5), channel_id=1, source_target_pairs={{0,2},{1,3},{2,4},{3,5},{4,6},{5,7},{6,8},{7,9},{8,10},{9,11},{10,... | collective-permute-start | bytes 983048 | tf_op jit(solution)/shard_map/ppermute | solution.py:27
  81.0 3.9 %collective-permute-start.2 = (bf16[128,1280]{1,0:T(8,128)(2,1)S(1)}, bf16[128,1280]{1,0:T(8,128)(2,1)S(1)}, u32[]{:S(2)}, u32[]{:S(2)}) collective-permute-start(bf16[128,1280]{1,0:T(8,128)(2,1)S(1)} %get-tuple-element.6), channel_id=1, source_target_pairs={{0,11},{1,0},{2,1},{3,2},{4,3},{5,4},{6,5},{7,6},{8,7},{9,8},{10,9... | collective-permute-start | bytes 983048 | tf_op jit(solution)/shard_map/ppermute | solution.py:27
  84.8 2.0 %collective-permute-start.1 = (bf16[128,1280]{1,0:T(8,128)(2,1)S(1)}, bf16[128,1280]{1,0:T(8,128)(2,1)S(1)}, u32[]{:S(2)}, u32[]{:S(2)}) collective-permute-start(bf16[128,1280]{1,0:T(8,128)(2,1)S(1)} %get-tuple-element.7), channel_id=1, source_target_pairs={{0,1},{1,2},{2,3},{3,4},{4,5},{5,6},{6,7},{7,8},{8,9},{9,10},{10,1... | collective-permute-start | bytes 983048 | tf_op jit(solution)/shard_map/ppermute | solution.py:27
  86.8 5.8 %collective-permute-done = bf16[128,1280]{1,0:T(8,128)(2,1)S(1)} collective-permute-done((bf16[128,1280]{1,0:T(8,128)(2,1)S(1)}, bf16[128,1280]{1,0:T(8,128)(2,1)S(1)}, u32[]{:S(2)}, u32[]{:S(2)}) %collective-permute-start) | collective-permute-done | bytes 327712 | tf_op jit(solution)/shard_map/ppermute | solution.py:27
  92.7 2.2 %collective-permute-done.2 = bf16[128,1280]{1,0:T(8,128)(2,1)S(1)} collective-permute-done((bf16[128,1280]{1,0:T(8,128)(2,1)S(1)}, bf16[128,1280]{1,0:T(8,128)(2,1)S(1)}, u32[]{:S(2)}, u32[]{:S(2)}) %collective-permute-start.2) | collective-permute-done | bytes 327712 | tf_op jit(solution)/shard_map/ppermute | solution.py:27
  94.8 3.6 %collective-permute-done.1 = bf16[128,1280]{1,0:T(8,128)(2,1)S(1)} collective-permute-done((bf16[128,1280]{1,0:T(8,128)(2,1)S(1)}, bf16[128,1280]{1,0:T(8,128)(2,1)S(1)}, u32[]{:S(2)}, u32[]{:S(2)}) %collective-permute-start.1) | collective-permute-done | bytes 327712 | tf_op jit(solution)/shard_map/ppermute | solution.py:27
  98.5 0.2 add_convert_fusion.2
  98.6 7.4 %collective-permute-start.4 = (bf16[128,1280]{1,0:T(8,128)(2,1)S(1)}, bf16[128,1280]{1,0:T(8,128)(2,1)S(1)}, u32[]{:S(2)}, u32[]{:S(2)}) collective-permute-start(bf16[128,1280]{1,0:T(8,128)(2,1)S(1)} %add_convert_fusion.2), channel_id=1, source_target_pairs={{0,8},{1,9},{2,10},{3,11},{4,0},{5,1},{6,2},{7,3},{8,4},{9,5},{10,... | collective-permute-start | bytes 983048 | tf_op jit(solution)/shard_map/ppermute | solution.py:27
  106.0 2.4 %collective-permute-start.3 = (bf16[128,1280]{1,0:T(8,128)(2,1)S(1)}, bf16[128,1280]{1,0:T(8,128)(2,1)S(1)}, u32[]{:S(2)}, u32[]{:S(2)}) collective-permute-start(bf16[128,1280]{1,0:T(8,128)(2,1)S(1)} %add_convert_fusion.2), channel_id=1, source_target_pairs={{0,4},{1,5},{2,6},{3,7},{4,8},{5,9},{6,10},{7,11},{8,0},{9,1},{10,... | collective-permute-start | bytes 983048 | tf_op jit(solution)/shard_map/ppermute | solution.py:27
  108.4 2.9 %convolution_convert_fusion.1 = bf16[512,1152]{1,0:T(8,128)(2,1)} fusion(bf16[512,1280]{1,0:T(8,128)(2,1)S(1)} %copy-done.2, bf16[1280,1152]{1,0:T(8,128)(2,1)S(1)} %bitcast.31), kind=kOutput, calls=%fused_computation.6 | convolution fusion | flops 1510539264 | bytes 5439488 | tf_op jit(solution)/shard_map/dot_general | solution.py:117
  111.4 24.1 %collective-permute-done.4 = bf16[128,1280]{1,0:T(8,128)(2,1)S(1)} collective-permute-done((bf16[128,1280]{1,0:T(8,128)(2,1)S(1)}, bf16[128,1280]{1,0:T(8,128)(2,1)S(1)}, u32[]{:S(2)}, u32[]{:S(2)}) %collective-permute-start.4) | collective-permute-done | bytes 327712 | tf_op jit(solution)/shard_map/ppermute | solution.py:27
  135.5 0.1 broadcast_in_dim.27
  135.6 0.3 bitcast_dynamic-update-slice_fusion.3
  135.9 1.9 %collective-permute-start.5 = (bf16[128,1280]{1,0:T(8,128)(2,1)S(1)}, bf16[128,1280]{1,0:T(8,128)(2,1)S(1)}, u32[]{:S(2)}, u32[]{:S(2)}) collective-permute-start(bf16[128,1280]{1,0:T(8,128)(2,1)S(1)} %get-tuple-element.4), channel_id=1, source_target_pairs={{0,2},{1,3},{2,4},{3,5},{4,6},{5,7},{6,8},{7,9},{8,10},{9,11},{10,... | collective-permute-start | bytes 983048 | tf_op jit(solution)/shard_map/ppermute | solution.py:27
  137.8 1.9 %collective-permute-start.6 = (bf16[128,1280]{1,0:T(8,128)(2,1)S(1)}, bf16[128,1280]{1,0:T(8,128)(2,1)S(1)}, u32[]{:S(2)}, u32[]{:S(2)}) collective-permute-start(bf16[128,1280]{1,0:T(8,128)(2,1)S(1)} %get-tuple-element.4), channel_id=1, source_target_pairs={{0,1},{1,2},{2,3},{3,4},{4,5},{5,6},{6,7},{7,8},{8,9},{9,10},{10,1... | collective-permute-start | bytes 983048 | tf_op jit(solution)/shard_map/ppermute | solution.py:27
  139.7 5.1 %collective-permute-start.7 = (bf16[128,1280]{1,0:T(8,128)(2,1)S(1)}, bf16[128,1280]{1,0:T(8,128)(2,1)S(1)}, u32[]{:S(2)}, u32[]{:S(2)}) collective-permute-start(bf16[128,1280]{1,0:T(8,128)(2,1)S(1)} %get-tuple-element.4), channel_id=1, source_target_pairs={{0,11},{1,0},{2,1},{3,2},{4,3},{5,4},{6,5},{7,6},{8,7},{9,8},{10,9... | collective-permute-start | bytes 983048 | tf_op jit(solution)/shard_map/ppermute | solution.py:27
  144.9 3.3 %collective-permute-done.5 = bf16[128,1280]{1,0:T(8,128)(2,1)S(1)} collective-permute-done((bf16[128,1280]{1,0:T(8,128)(2,1)S(1)}, bf16[128,1280]{1,0:T(8,128)(2,1)S(1)}, u32[]{:S(2)}, u32[]{:S(2)}) %collective-permute-start.5) | collective-permute-done | bytes 327712 | tf_op jit(solution)/shard_map/ppermute | solution.py:27
  148.2 6.5 %collective-permute-done.6 = bf16[128,1280]{1,0:T(8,128)(2,1)S(1)} collective-permute-done((bf16[128,1280]{1,0:T(8,128)(2,1)S(1)}, bf16[128,1280]{1,0:T(8,128)(2,1)S(1)}, u32[]{:S(2)}, u32[]{:S(2)}) %collective-permute-start.6) | collective-permute-done | bytes 327712 | tf_op jit(solution)/shard_map/ppermute | solution.py:27
  154.8 1.0 copy-done
  (17 shorter events, 0.2 us)
Async XLA Ops:
  7.2 65.1 %all-gather.2.cloned.1.call-start = ((), (), s32[]{:S(2)}) async-start(), calls=%async_computation.2 | async-start | bytes 3317760 | tf_op jit(solution)/shard_map/all_gather | solution.py:39
  16.5 2.3 %copy-start.2 = (bf16[512,1280]{1,0:T(8,128)(2,1)S(1)}, bf16[512,1280]{1,0:T(8,128)(2,1)}, u32[]{:S(2)}) copy-start(bf16[512,1280]{1,0:T(8,128)(2,1)} %param.4) | copy-start | bytes 3932164
  16.5 138.2 %reduce-scatter.5.cloned.1.call-start = ((), (), s32[]{:S(2)}) async-start(), calls=%async_computation.4 | async-start | bytes 1658880 | tf_op jit(solution)/shard_map/reduce_scatter | solution.py:55
  19.9 36.9 %collective-permute-start.8 = (bf16[640,1152]{1,0:T(8,128)(2,1)S(1)}, bf16[640,1152]{1,0:T(8,128)(2,1)S(1)}, u32[]{:S(2)}, u32[]{:S(2)}) collective-permute-start(bf16[640,1152]{1,0:T(8,128)(2,1)S(1)} %fusion.2), channel_id=1, source_target_pairs={{0,384},{48,432},{96,480},{144,528},{192,576},{240,624},{288,672},... | collective-permute-start | bytes 4423688 | tf_op jit(solution)/shard_map/ppermute | solution.py:19
  59.0 95.8 %reduce-scatter.3.cloned.1.call-start = ((), (), s32[]{:S(2)}) async-start(), calls=%async_computation.3 | async-start | bytes 1474560 | tf_op jit(solution)/shard_map/reduce_scatter | solution.py:118
  76.0 32.5 %copy-start.1 = (bf16[2,640,1152]{2,1,0:T(8,128)(2,1)S(1)}, bf16[2,640,1152]{2,1,0:T(8,128)(2,1)}, u32[]{:S(2)}) copy-start(bf16[2,640,1152]{2,1,0:T(8,128)(2,1)} %all-gather.2.cloned.1.call-done) | copy-start | bytes 8847364
  76.0 16.6 %collective-permute-start = (bf16[128,1280]{1,0:T(8,128)(2,1)S(1)}, bf16[128,1280]{1,0:T(8,128)(2,1)S(1)}, u32[]{:S(2)}, u32[]{:S(2)}) collective-permute-start(bf16[128,1280]{1,0:T(8,128)(2,1)S(1)} %get-tuple-element.5), channel_id=1, source_target_pairs={{0,2},{1,3},{2,4},{3,5},{4,6},{5,7},{6,8},{7,9},{8,10},{9,11},{10,... | collective-permute-start | bytes 983048 | tf_op jit(solution)/shard_map/ppermute | solution.py:27
  81.0 13.9 %collective-permute-start.2 = (bf16[128,1280]{1,0:T(8,128)(2,1)S(1)}, bf16[128,1280]{1,0:T(8,128)(2,1)S(1)}, u32[]{:S(2)}, u32[]{:S(2)}) collective-permute-start(bf16[128,1280]{1,0:T(8,128)(2,1)S(1)} %get-tuple-element.6), channel_id=1, source_target_pairs={{0,11},{1,0},{2,1},{3,2},{4,3},{5,4},{6,5},{7,6},{8,7},{9,8},{10,9... | collective-permute-start | bytes 983048 | tf_op jit(solution)/shard_map/ppermute | solution.py:27
  84.8 13.6 %collective-permute-start.1 = (bf16[128,1280]{1,0:T(8,128)(2,1)S(1)}, bf16[128,1280]{1,0:T(8,128)(2,1)S(1)}, u32[]{:S(2)}, u32[]{:S(2)}) collective-permute-start(bf16[128,1280]{1,0:T(8,128)(2,1)S(1)} %get-tuple-element.7), channel_id=1, source_target_pairs={{0,1},{1,2},{2,3},{3,4},{4,5},{5,6},{6,7},{7,8},{8,9},{9,10},{10,1... | collective-permute-start | bytes 983048 | tf_op jit(solution)/shard_map/ppermute | solution.py:27
  98.6 36.9 %collective-permute-start.4 = (bf16[128,1280]{1,0:T(8,128)(2,1)S(1)}, bf16[128,1280]{1,0:T(8,128)(2,1)S(1)}, u32[]{:S(2)}, u32[]{:S(2)}) collective-permute-start(bf16[128,1280]{1,0:T(8,128)(2,1)S(1)} %add_convert_fusion.2), channel_id=1, source_target_pairs={{0,8},{1,9},{2,10},{3,11},{4,0},{5,1},{6,2},{7,3},{8,4},{9,5},{10,... | collective-permute-start | bytes 983048 | tf_op jit(solution)/shard_map/ppermute | solution.py:27
  106.0 29.5 %collective-permute-start.3 = (bf16[128,1280]{1,0:T(8,128)(2,1)S(1)}, bf16[128,1280]{1,0:T(8,128)(2,1)S(1)}, u32[]{:S(2)}, u32[]{:S(2)}) collective-permute-start(bf16[128,1280]{1,0:T(8,128)(2,1)S(1)} %add_convert_fusion.2), channel_id=1, source_target_pairs={{0,4},{1,5},{2,6},{3,7},{4,8},{5,9},{6,10},{7,11},{8,0},{9,1},{10,... | collective-permute-start | bytes 983048 | tf_op jit(solution)/shard_map/ppermute | solution.py:27
  135.9 12.3 %collective-permute-start.5 = (bf16[128,1280]{1,0:T(8,128)(2,1)S(1)}, bf16[128,1280]{1,0:T(8,128)(2,1)S(1)}, u32[]{:S(2)}, u32[]{:S(2)}) collective-permute-start(bf16[128,1280]{1,0:T(8,128)(2,1)S(1)} %get-tuple-element.4), channel_id=1, source_target_pairs={{0,2},{1,3},{2,4},{3,5},{4,6},{5,7},{6,8},{7,9},{8,10},{9,11},{10,... | collective-permute-start | bytes 983048 | tf_op jit(solution)/shard_map/ppermute | solution.py:27
  137.8 16.9 %collective-permute-start.6 = (bf16[128,1280]{1,0:T(8,128)(2,1)S(1)}, bf16[128,1280]{1,0:T(8,128)(2,1)S(1)}, u32[]{:S(2)}, u32[]{:S(2)}) collective-permute-start(bf16[128,1280]{1,0:T(8,128)(2,1)S(1)} %get-tuple-element.4), channel_id=1, source_target_pairs={{0,1},{1,2},{2,3},{3,4},{4,5},{5,6},{6,7},{7,8},{8,9},{9,10},{10,1... | collective-permute-start | bytes 983048 | tf_op jit(solution)/shard_map/ppermute | solution.py:27
  139.7 15.0 %collective-permute-start.7 = (bf16[128,1280]{1,0:T(8,128)(2,1)S(1)}, bf16[128,1280]{1,0:T(8,128)(2,1)S(1)}, u32[]{:S(2)}, u32[]{:S(2)}) collective-permute-start(bf16[128,1280]{1,0:T(8,128)(2,1)S(1)} %get-tuple-element.4), channel_id=1, source_target_pairs={{0,11},{1,0},{2,1},{3,2},{4,3},{5,4},{6,5},{7,6},{8,7},{9,8},{10,9... | collective-permute-start | bytes 983048 | tf_op jit(solution)/shard_map/ppermute | solution.py:27
  154.8 1.1 copy-start
Sparse Core Ops, SparseCore 0:
  16.7 55.5 all-gather.1
  75.9 44.1 reduce-scatter.4
  123.8 27.6 reduce-scatter.2

commit v11 on v10

--- a/solution.py
+++ b/solution.py
@@ -64,21 +64,29 @@
     two_away, ahead, behind, kept = jnp.split(products.astype(BF16), 4)
     arrived = (over_col(two_away, 2), over_col(ahead, 1), over_col(behind, -1))
     mine = add(kept, *arrived)
-    from_behind = over_col(mine, 4)
-    from_ahead = over_col(mine, -4)
-    below = jnp.where(up == 1, from_behind, from_ahead)
-    above = jnp.where(up == 1, from_ahead, from_behind)
     q = z // 4
-    last = jnp.where(q == 0, below, jnp.where(q == 1, above, mine))
-    one = jnp.where(q == 0, mine, below)
-    two = jnp.where(q == 1, mine, above)
-    total = add(one, two, last)
-    arrived = (over_col(total, 2), over_col(total, 1), over_col(total, -1))
-    result = jnp.zeros((4,) + total.shape, total.dtype)
-    for step, value in ((0, total), (2, arrived[0]), (-1, arrived[1]), (1, arrived[2])):
-        place = lax.rem(z + step * up + NZ, 4)
-        result = lax.dynamic_update_slice(result, value[None], (place, 0, 0))
-    return result.reshape(-1, total.shape[1])
+    half = mine.shape[1] // 2
+    parts = (mine[:, :half], mine[:, half:])
+    moved = [(over_col(part, 4), over_col(part, -4)) for part in parts]
+    results = []
+    for part, (from_behind, from_ahead) in zip(parts, moved):
+        below = jnp.where(up == 1, from_behind, from_ahead)
+        above = jnp.where(up == 1, from_ahead, from_behind)
+        last = jnp.where(q == 0, below, jnp.where(q == 1, above, part))
+        one = jnp.where(q == 0, part, below)
+        two = jnp.where(q == 1, part, above)
+        total = add(one, two, last)
+        result = jnp.zeros((4,) + total.shape, total.dtype)
+        for step, value in (
+            (0, total),
+            (2, over_col(total, 2)),
+            (-1, over_col(total, 1)),
+            (1, over_col(total, -1)),
+        ):
+            place = lax.rem(z + step * up + NZ, 4)
+            result = lax.dynamic_update_slice(result, value[None], (place, 0, 0))
+        results.append(result.reshape(-1, half))
+    return jnp.concatenate(results, axis=1)
 
 
 def body(normed, up_weight, cotangent, lengths):

time: 164 us -> 169 us (1.030)
  starting transfers between devices: 33.6 us -> 72.3 us
  waiting for transfers between devices: 91.3 us -> 57.2 us
    ppermute x8 -> x13, starting transfers between devices: 29.5 us -> 68.2 us  [over_col(): return lax.ppermute(value, ('row', 'col'), pairs)]
    ppermute x8 -> x13, waiting for transfers between devices: 45.5 us -> 11.5 us  [over_col(): return lax.ppermute(value, ('row', 'col'), pairs)]
  transfers between devices with their start and end apart: 12 -> 17, of which waited for: 8 -> 8; matrix products, arithmetic and copies ran while one was open for 8% -> 8% of each run, Pallas kernels for 0% -> 0%
where the time goes in v11:
time: 169 us; the launch traced here: 167 us
  starting transfers between devices  72.3 us (43%)
  waiting for transfers between devices  57.2 us (34%)
  between operations  14.9 us (9%)
  matrix products  10.1 us (6%)
  blocking collectives  9.31 us (6%)
  other arithmetic  3.19 us (2%)
    ppermute x13, starting transfers between devices, over_col(): return lax.ppermute(value, ('row', 'col'), pairs)  68.2 us
    ppermute x1, waiting for transfers between devices, over_rep(): return lax.ppermute(value, 'rep', pairs)  32.8 us
    all_gather x1, waiting for transfers between devices, gather_weight(): lax.all_gather(pair, 'rep', axis=1, tiled=True, axis_index_groups=Y_RINGS)  12.9 us
    ppermute x13, waiting for transfers between devices, over_col(): return lax.ppermute(value, ('row', 'col'), pairs)  11.5 us
    all_gather x1, blocking collectives, gather_weight(): lax.all_gather(w0, 'rep', axis=0, tiled=True, axis_index_groups=X_PAIRS)  9.31 us
    ppermute x1, starting transfers between devices, over_rep(): return lax.ppermute(value, 'rep', pairs)  4.05 us
    dot_general x1, matrix products, sum_over_col(): lax.dot_general(turned, weight, (((1,), (1,)), ((), ())), preferred_eleme...  3.87 us
  transfers between devices with their start and end apart: 17, of which 8 were waited for; matrix products, arithmetic and copies ran while one was open for 8% of the time, Pallas kernels for 0%

profile of v11, /device:TPU:6, one launch (start us, length us, event | category | flops | bytes accessed | tf_op | source)
XLA Modules:
  0.0 167.5 jit_solution(928118499511671940)
XLA Ops:
  7.2 9.3 %all_gather.6 = bf16[2,80,1152]{2,1,0:T(8,128)(2,1)} all-gather(bf16[1,80,1152]{2,1,0:T(8,128)(2,1)} %param.5), channel_id=1, replica_groups={{0,384},{48,432},{96,480},{144,528},{192,576},{240,624},{288,672},{336,..., dimensions={0}, use_global_device_ids=true | all-gather | bytes 552960 | tf_op jit(solution)/shard_map/all_gather | solution.py:38
  17.4 1.5 broadcast_select_fusion
  18.8 1.1 fusion.2
  19.9 4.0 %collective-permute-start.13 = (bf16[640,1152]{1,0:T(8,128)(2,1)S(1)}, bf16[640,1152]{1,0:T(8,128)(2,1)S(1)}, u32[]{:S(2)}, u32[]{:S(2)}) collective-permute-start(bf16[640,1152]{1,0:T(8,128)(2,1)S(1)} %fusion.2), channel_id=1, source_target_pairs={{0,384},{48,432},{96,480},{144,528},{192,576},{240,624},{288,672},... | collective-permute-start | bytes 4423688 | tf_op jit(solution)/shard_map/ppermute | solution.py:19
  24.0 32.8 %collective-permute-done.13 = bf16[640,1152]{1,0:T(8,128)(2,1)S(1)} collective-permute-done((bf16[640,1152]{1,0:T(8,128)(2,1)S(1)}, bf16[640,1152]{1,0:T(8,128)(2,1)S(1)}, u32[]{:S(2)}, u32[]{:S(2)}) %collective-permute-start.13) | collective-permute-done | bytes 1474592 | tf_op jit(solution)/shard_map/ppermute | solution.py:19
  56.8 2.2 %add_convert_fusion = bf16[640,1152]{1,0:T(8,128)(2,1)} fusion(bf16[640,1152]{1,0:T(8,128)(2,1)S(1)} %collective-permute-done.13, bf16[512,1152]{1,0:T(8,128)(2,1)S(1)} %broadcast_select_fusion, pred[]{:T(512)S(6)} %lt.47, bf16[512,1280]{1,0:T(8,128)(2,1)S(1)} %copy-done.1), kind=kOutput, calls=%fused_computation.7 | convolution fusion | flops 759726080 | bytes 5439489 | tf_op jit(solution)/shard_map/dot_general | solution.py:48
  59.1 0.1 dynamic-slice_bitcast_fusion.3
  59.3 12.9 %all-gather.2.cloned.1.call-done = bf16[2,640,1152]{2,1,0:T(8,128)(2,1)} async-done(((bf16[2,80,1152]{2,1,0:T(8,128)(2,1)}), bf16[2,640,1152]{2,1,0:T(8,128)(2,1)}) %all-gather.2.cloned.1.call-update) | async-done | bytes 2949136 | tf_op jit(solution)/shard_map/all_gather | solution.py:39
  72.2 3.9 %convolution_convert_fusion = bf16[512,1280]{1,0:T(8,128)(2,1)S(1)} fusion(bf16[512,1152]{1,0:T(8,128)(2,1)S(1)} %pad_maximum_fusion.1, bf16[1280,1152]{1,0:T(8,128)(2,1)} %bitcast.40), kind=kOutput, calls=%fused_computation.5 | convolution fusion | flops 1510604800 | bytes 5439488 | tf_op jit(solution)/shard_map/dot_general | solution.py:61
  76.2 6.7 %collective-permute-start.2 = (bf16[128,1280]{1,0:T(8,128)(2,1)S(1)}, bf16[128,1280]{1,0:T(8,128)(2,1)S(1)}, u32[]{:S(2)}, u32[]{:S(2)}) collective-permute-start(bf16[128,1280]{1,0:T(8,128)(2,1)S(1)} %get-tuple-element.8), channel_id=1, source_target_pairs={{0,11},{1,0},{2,1},{3,2},{4,3},{5,4},{6,5},{7,6},{8,7},{9,8},{10,9... | collective-permute-start | bytes 983048 | tf_op jit(solution)/shard_map/ppermute | solution.py:27
  82.9 1.9 %collective-permute-start.1 = (bf16[128,1280]{1,0:T(8,128)(2,1)S(1)}, bf16[128,1280]{1,0:T(8,128)(2,1)S(1)}, u32[]{:S(2)}, u32[]{:S(2)}) collective-permute-start(bf16[128,1280]{1,0:T(8,128)(2,1)S(1)} %get-tuple-element.9), channel_id=1, source_target_pairs={{0,1},{1,2},{2,3},{3,4},{4,5},{5,6},{6,7},{7,8},{8,9},{9,10},{10,1... | collective-permute-start | bytes 983048 | tf_op jit(solution)/shard_map/ppermute | solution.py:27
  84.9 2.0 %collective-permute-start = (bf16[128,1280]{1,0:T(8,128)(2,1)S(1)}, bf16[128,1280]{1,0:T(8,128)(2,1)S(1)}, u32[]{:S(2)}, u32[]{:S(2)}) collective-permute-start(bf16[128,1280]{1,0:T(8,128)(2,1)S(1)} %get-tuple-element.7), channel_id=1, source_target_pairs={{0,2},{1,3},{2,4},{3,5},{4,6},{5,7},{6,8},{7,9},{8,10},{9,11},{10,... | collective-permute-start | bytes 983048 | tf_op jit(solution)/shard_map/ppermute | solution.py:27
  86.9 2.9 %convolution_convert_fusion.1 = bf16[512,1152]{1,0:T(8,128)(2,1)} fusion(bf16[512,1280]{1,0:T(8,128)(2,1)S(1)} %copy-done.2, bf16[1280,1152]{1,0:T(8,128)(2,1)S(1)} %bitcast.41), kind=kOutput, calls=%fused_computation.6 | convolution fusion | flops 1510539264 | bytes 5439488 | tf_op jit(solution)/shard_map/dot_general | solution.py:125
  89.8 4.5 %collective-permute-done.2 = bf16[128,1280]{1,0:T(8,128)(2,1)S(1)} collective-permute-done((bf16[128,1280]{1,0:T(8,128)(2,1)S(1)}, bf16[128,1280]{1,0:T(8,128)(2,1)S(1)}, u32[]{:S(2)}, u32[]{:S(2)}) %collective-permute-start.2) | collective-permute-done | bytes 327712 | tf_op jit(solution)/shard_map/ppermute | solution.py:27
  94.5 2.4 %collective-permute-done = bf16[128,1280]{1,0:T(8,128)(2,1)S(1)} collective-permute-done((bf16[128,1280]{1,0:T(8,128)(2,1)S(1)}, bf16[128,1280]{1,0:T(8,128)(2,1)S(1)}, u32[]{:S(2)}, u32[]{:S(2)}) %collective-permute-start) | collective-permute-done | bytes 327712 | tf_op jit(solution)/shard_map/ppermute | solution.py:27
  96.9 0.2 add_convert_fusion.1
  97.1 6.3 %collective-permute-start.9 = (bf16[128,640]{1,0:T(8,128)(2,1)S(1)}, bf16[128,640]{1,0:T(8,128)(2,1)S(1)}, u32[]{:S(2)}, u32[]{:S(2)}) collective-permute-start(bf16[128,640]{1,0:T(8,128)(2,1)S(1)} %get-tuple-element.15), channel_id=1, source_target_pairs={{0,8},{1,9},{2,10},{3,11},{4,0},{5,1},{6,2},{7,3},{8,4},{9,5},{10,... | collective-permute-start | bytes 491528 | tf_op jit(solution)/shard_map/ppermute | solution.py:27
  103.4 3.5 %collective-permute-start.8 = (bf16[128,640]{1,0:T(8,128)(2,1)S(1)}, bf16[128,640]{1,0:T(8,128)(2,1)S(1)}, u32[]{:S(2)}, u32[]{:S(2)}) collective-permute-start(bf16[128,640]{1,0:T(8,128)(2,1)S(1)} %get-tuple-element.15), channel_id=1, source_target_pairs={{0,4},{1,5},{2,6},{3,7},{4,8},{5,9},{6,10},{7,11},{8,0},{9,1},{10,... | collective-permute-start | bytes 491528 | tf_op jit(solution)/shard_map/ppermute | solution.py:27
  106.9 6.3 %collective-permute-start.4 = (bf16[128,640]{1,0:T(8,128)(2,1)S(1)}, bf16[128,640]{1,0:T(8,128)(2,1)S(1)}, u32[]{:S(2)}, u32[]{:S(2)}) collective-permute-start(bf16[128,640]{1,0:T(8,128)(2,1)S(1)} %get-tuple-element.14), channel_id=1, source_target_pairs={{0,8},{1,9},{2,10},{3,11},{4,0},{5,1},{6,2},{7,3},{8,4},{9,5},{10,... | collective-permute-start | bytes 491528 | tf_op jit(solution)/shard_map/ppermute | solution.py:27
  113.2 3.5 %collective-permute-start.3 = (bf16[128,640]{1,0:T(8,128)(2,1)S(1)}, bf16[128,640]{1,0:T(8,128)(2,1)S(1)}, u32[]{:S(2)}, u32[]{:S(2)}) collective-permute-start(bf16[128,640]{1,0:T(8,128)(2,1)S(1)} %get-tuple-element.14), channel_id=1, source_target_pairs={{0,4},{1,5},{2,6},{3,7},{4,8},{5,9},{6,10},{7,11},{8,0},{9,1},{10,... | collective-permute-start | bytes 491528 | tf_op jit(solution)/shard_map/ppermute | solution.py:27
  116.7 0.5 collective-permute-done.8
  117.2 0.1 bitcast_dynamic-update-slice_fusion.3
  117.4 1.9 %collective-permute-start.10 = (bf16[128,640]{1,0:T(8,128)(2,1)S(1)}, bf16[128,640]{1,0:T(8,128)(2,1)S(1)}, u32[]{:S(2)}, u32[]{:S(2)}) collective-permute-start(bf16[128,640]{1,0:T(8,128)(2,1)S(1)} %get-tuple-element.6), channel_id=1, source_target_pairs={{0,2},{1,3},{2,4},{3,5},{4,6},{5,7},{6,8},{7,9},{8,10},{9,11},{10,... | collective-permute-start | bytes 491528 | tf_op jit(solution)/shard_map/ppermute | solution.py:27
  119.3 20.0 %collective-permute-start.11 = (bf16[128,640]{1,0:T(8,128)(2,1)S(1)}, bf16[128,640]{1,0:T(8,128)(2,1)S(1)}, u32[]{:S(2)}, u32[]{:S(2)}) collective-permute-start(bf16[128,640]{1,0:T(8,128)(2,1)S(1)} %get-tuple-element.6), channel_id=1, source_target_pairs={{0,1},{1,2},{2,3},{3,4},{4,5},{5,6},{6,7},{7,8},{8,9},{9,10},{10,1... | collective-permute-start | bytes 491528 | tf_op jit(solution)/shard_map/ppermute | solution.py:27
  139.3 4.6 %collective-permute-start.12 = (bf16[128,640]{1,0:T(8,128)(2,1)S(1)}, bf16[128,640]{1,0:T(8,128)(2,1)S(1)}, u32[]{:S(2)}, u32[]{:S(2)}) collective-permute-start(bf16[128,640]{1,0:T(8,128)(2,1)S(1)} %get-tuple-element.6), channel_id=1, source_target_pairs={{0,11},{1,0},{2,1},{3,2},{4,3},{5,4},{6,5},{7,6},{8,7},{9,8},{10,9... | collective-permute-start | bytes 491528 | tf_op jit(solution)/shard_map/ppermute | solution.py:27
  144.0 0.2 bitcast_dynamic-update-slice_fusion.7
  144.1 4.5 %collective-permute-start.5 = (bf16[128,640]{1,0:T(8,128)(2,1)S(1)}, bf16[128,640]{1,0:T(8,128)(2,1)S(1)}, u32[]{:S(2)}, u32[]{:S(2)}) collective-permute-start(bf16[128,640]{1,0:T(8,128)(2,1)S(1)} %get-tuple-element.4), channel_id=1, source_target_pairs={{0,2},{1,3},{2,4},{3,5},{4,6},{5,7},{6,8},{7,9},{8,10},{9,11},{10,... | collective-permute-start | bytes 491528 | tf_op jit(solution)/shard_map/ppermute | solution.py:27
  148.6 3.9 %collective-permute-start.6 = (bf16[128,640]{1,0:T(8,128)(2,1)S(1)}, bf16[128,640]{1,0:T(8,128)(2,1)S(1)}, u32[]{:S(2)}, u32[]{:S(2)}) collective-permute-start(bf16[128,640]{1,0:T(8,128)(2,1)S(1)} %get-tuple-element.4), channel_id=1, source_target_pairs={{0,1},{1,2},{2,3},{3,4},{4,5},{5,6},{6,7},{7,8},{8,9},{9,10},{10,1... | collective-permute-start | bytes 491528 | tf_op jit(solution)/shard_map/ppermute | solution.py:27
  152.6 3.1 %collective-permute-start.7 = (bf16[128,640]{1,0:T(8,128)(2,1)S(1)}, bf16[128,640]{1,0:T(8,128)(2,1)S(1)}, u32[]{:S(2)}, u32[]{:S(2)}) collective-permute-start(bf16[128,640]{1,0:T(8,128)(2,1)S(1)} %get-tuple-element.4), channel_id=1, source_target_pairs={{0,11},{1,0},{2,1},{3,2},{4,3},{5,4},{6,5},{7,6},{8,7},{9,8},{10,9... | collective-permute-start | bytes 491528 | tf_op jit(solution)/shard_map/ppermute | solution.py:27
  155.9 1.4 collective-permute-done.6
  157.3 2.4 %collective-permute-done.7 = bf16[128,640]{1,0:T(8,128)(2,1)S(1)} collective-permute-done((bf16[128,640]{1,0:T(8,128)(2,1)S(1)}, bf16[128,640]{1,0:T(8,128)(2,1)S(1)}, u32[]{:S(2)}, u32[]{:S(2)}) %collective-permute-start.7) | collective-permute-done | bytes 163872 | tf_op jit(solution)/shard_map/ppermute | solution.py:27
  159.8 1.2 pad_maximum_fusion
  (34 shorter events, 0.8 us)
Async XLA Ops:
  7.2 65.1 %all-gather.2.cloned.1.call-start = ((), (), s32[]{:S(2)}) async-start(), calls=%async_computation.2 | async-start | bytes 3317760 | tf_op jit(solution)/shard_map/all_gather | solution.py:39
  16.5 2.3 %copy-start.1 = (bf16[512,1280]{1,0:T(8,128)(2,1)S(1)}, bf16[512,1280]{1,0:T(8,128)(2,1)}, u32[]{:S(2)}) copy-start(bf16[512,1280]{1,0:T(8,128)(2,1)} %param.4) | copy-start | bytes 3932164
  16.5 144.4 %reduce-scatter.5.cloned.1.call-start = ((), (), s32[]{:S(2)}) async-start(), calls=%async_computation.4 | async-start | bytes 1658880 | tf_op jit(solution)/shard_map/reduce_scatter | solution.py:55
  19.9 36.9 %collective-permute-start.13 = (bf16[640,1152]{1,0:T(8,128)(2,1)S(1)}, bf16[640,1152]{1,0:T(8,128)(2,1)S(1)}, u32[]{:S(2)}, u32[]{:S(2)}) collective-permute-start(bf16[640,1152]{1,0:T(8,128)(2,1)S(1)} %fusion.2), channel_id=1, source_target_pairs={{0,384},{48,432},{96,480},{144,528},{192,576},{240,624},{288,672},... | collective-permute-start | bytes 4423688 | tf_op jit(solution)/shard_map/ppermute | solution.py:19
  59.0 102.0 %reduce-scatter.3.cloned.1.call-start = ((), (), s32[]{:S(2)}) async-start(), calls=%async_computation.3 | async-start | bytes 1474560 | tf_op jit(solution)/shard_map/reduce_scatter | solution.py:126
  72.2 14.6 %copy-start = (bf16[2,640,1152]{2,1,0:T(8,128)(2,1)S(1)}, bf16[2,640,1152]{2,1,0:T(8,128)(2,1)}, u32[]{:S(2)}) copy-start(bf16[2,640,1152]{2,1,0:T(8,128)(2,1)} %all-gather.2.cloned.1.call-done) | copy-start | bytes 8847364
  76.1 10.8 %copy-start.2 = (bf16[512,1280]{1,0:T(8,128)(2,1)S(1)}, bf16[512,1280]{1,0:T(8,128)(2,1)}, u32[]{:S(2)}) copy-start(bf16[512,1280]{1,0:T(8,128)(2,1)} %param.4) | copy-start | bytes 3932164
  76.2 18.2 %collective-permute-start.2 = (bf16[128,1280]{1,0:T(8,128)(2,1)S(1)}, bf16[128,1280]{1,0:T(8,128)(2,1)S(1)}, u32[]{:S(2)}, u32[]{:S(2)}) collective-permute-start(bf16[128,1280]{1,0:T(8,128)(2,1)S(1)} %get-tuple-element.8), channel_id=1, source_target_pairs={{0,11},{1,0},{2,1},{3,2},{4,3},{5,4},{6,5},{7,6},{8,7},{9,8},{10,9... | collective-permute-start | bytes 983048 | tf_op jit(solution)/shard_map/ppermute | solution.py:27
  82.9 11.5 %collective-permute-start.1 = (bf16[128,1280]{1,0:T(8,128)(2,1)S(1)}, bf16[128,1280]{1,0:T(8,128)(2,1)S(1)}, u32[]{:S(2)}, u32[]{:S(2)}) collective-permute-start(bf16[128,1280]{1,0:T(8,128)(2,1)S(1)} %get-tuple-element.9), channel_id=1, source_target_pairs={{0,1},{1,2},{2,3},{3,4},{4,5},{5,6},{6,7},{7,8},{8,9},{9,10},{10,1... | collective-permute-start | bytes 983048 | tf_op jit(solution)/shard_map/ppermute | solution.py:27
  84.9 12.0 %collective-permute-start = (bf16[128,1280]{1,0:T(8,128)(2,1)S(1)}, bf16[128,1280]{1,0:T(8,128)(2,1)S(1)}, u32[]{:S(2)}, u32[]{:S(2)}) collective-permute-start(bf16[128,1280]{1,0:T(8,128)(2,1)S(1)} %get-tuple-element.7), channel_id=1, source_target_pairs={{0,2},{1,3},{2,4},{3,5},{4,6},{5,7},{6,8},{7,9},{8,10},{9,11},{10,... | collective-permute-start | bytes 983048 | tf_op jit(solution)/shard_map/ppermute | solution.py:27
  97.1 19.6 %collective-permute-start.9 = (bf16[128,640]{1,0:T(8,128)(2,1)S(1)}, bf16[128,640]{1,0:T(8,128)(2,1)S(1)}, u32[]{:S(2)}, u32[]{:S(2)}) collective-permute-start(bf16[128,640]{1,0:T(8,128)(2,1)S(1)} %get-tuple-element.15), channel_id=1, source_target_pairs={{0,8},{1,9},{2,10},{3,11},{4,0},{5,1},{6,2},{7,3},{8,4},{9,5},{10,... | collective-permute-start | bytes 491528 | tf_op jit(solution)/shard_map/ppermute | solution.py:27
  103.4 13.8 %collective-permute-start.8 = (bf16[128,640]{1,0:T(8,128)(2,1)S(1)}, bf16[128,640]{1,0:T(8,128)(2,1)S(1)}, u32[]{:S(2)}, u32[]{:S(2)}) collective-permute-start(bf16[128,640]{1,0:T(8,128)(2,1)S(1)} %get-tuple-element.15), channel_id=1, source_target_pairs={{0,4},{1,5},{2,6},{3,7},{4,8},{5,9},{6,10},{7,11},{8,0},{9,1},{10,... | collective-permute-start | bytes 491528 | tf_op jit(solution)/shard_map/ppermute | solution.py:27
  106.9 37.0 %collective-permute-start.4 = (bf16[128,640]{1,0:T(8,128)(2,1)S(1)}, bf16[128,640]{1,0:T(8,128)(2,1)S(1)}, u32[]{:S(2)}, u32[]{:S(2)}) collective-permute-start(bf16[128,640]{1,0:T(8,128)(2,1)S(1)} %get-tuple-element.14), channel_id=1, source_target_pairs={{0,8},{1,9},{2,10},{3,11},{4,0},{5,1},{6,2},{7,3},{8,4},{9,5},{10,... | collective-permute-start | bytes 491528 | tf_op jit(solution)/shard_map/ppermute | solution.py:27
  113.2 30.7 %collective-permute-start.3 = (bf16[128,640]{1,0:T(8,128)(2,1)S(1)}, bf16[128,640]{1,0:T(8,128)(2,1)S(1)}, u32[]{:S(2)}, u32[]{:S(2)}) collective-permute-start(bf16[128,640]{1,0:T(8,128)(2,1)S(1)} %get-tuple-element.14), channel_id=1, source_target_pairs={{0,4},{1,5},{2,6},{3,7},{4,8},{5,9},{6,10},{7,11},{8,0},{9,1},{10,... | collective-permute-start | bytes 491528 | tf_op jit(solution)/shard_map/ppermute | solution.py:27
  117.4 35.2 %collective-permute-start.10 = (bf16[128,640]{1,0:T(8,128)(2,1)S(1)}, bf16[128,640]{1,0:T(8,128)(2,1)S(1)}, u32[]{:S(2)}, u32[]{:S(2)}) collective-permute-start(bf16[128,640]{1,0:T(8,128)(2,1)S(1)} %get-tuple-element.6), channel_id=1, source_target_pairs={{0,2},{1,3},{2,4},{3,5},{4,6},{5,7},{6,8},{7,9},{8,10},{9,11},{10,... | collective-permute-start | bytes 491528 | tf_op jit(solution)/shard_map/ppermute | solution.py:27
  119.3 36.4 %collective-permute-start.11 = (bf16[128,640]{1,0:T(8,128)(2,1)S(1)}, bf16[128,640]{1,0:T(8,128)(2,1)S(1)}, u32[]{:S(2)}, u32[]{:S(2)}) collective-permute-start(bf16[128,640]{1,0:T(8,128)(2,1)S(1)} %get-tuple-element.6), channel_id=1, source_target_pairs={{0,1},{1,2},{2,3},{3,4},{4,5},{5,6},{6,7},{7,8},{8,9},{9,10},{10,1... | collective-permute-start | bytes 491528 | tf_op jit(solution)/shard_map/ppermute | solution.py:27
  139.3 16.5 %collective-permute-start.12 = (bf16[128,640]{1,0:T(8,128)(2,1)S(1)}, bf16[128,640]{1,0:T(8,128)(2,1)S(1)}, u32[]{:S(2)}, u32[]{:S(2)}) collective-permute-start(bf16[128,640]{1,0:T(8,128)(2,1)S(1)} %get-tuple-element.6), channel_id=1, source_target_pairs={{0,11},{1,0},{2,1},{3,2},{4,3},{5,4},{6,5},{7,6},{8,7},{9,8},{10,9... | collective-permute-start | bytes 491528 | tf_op jit(solution)/shard_map/ppermute | solution.py:27
  144.1 11.7 %collective-permute-start.5 = (bf16[128,640]{1,0:T(8,128)(2,1)S(1)}, bf16[128,640]{1,0:T(8,128)(2,1)S(1)}, u32[]{:S(2)}, u32[]{:S(2)}) collective-permute-start(bf16[128,640]{1,0:T(8,128)(2,1)S(1)} %get-tuple-element.4), channel_id=1, source_target_pairs={{0,2},{1,3},{2,4},{3,5},{4,6},{5,7},{6,8},{7,9},{8,10},{9,11},{10,... | collective-permute-start | bytes 491528 | tf_op jit(solution)/shard_map/ppermute | solution.py:27
  148.6 8.7 %collective-permute-start.6 = (bf16[128,640]{1,0:T(8,128)(2,1)S(1)}, bf16[128,640]{1,0:T(8,128)(2,1)S(1)}, u32[]{:S(2)}, u32[]{:S(2)}) collective-permute-start(bf16[128,640]{1,0:T(8,128)(2,1)S(1)} %get-tuple-element.4), channel_id=1, source_target_pairs={{0,1},{1,2},{2,3},{3,4},{4,5},{5,6},{6,7},{7,8},{8,9},{9,10},{10,1... | collective-permute-start | bytes 491528 | tf_op jit(solution)/shard_map/ppermute | solution.py:27
  152.6 7.2 %collective-permute-start.7 = (bf16[128,640]{1,0:T(8,128)(2,1)S(1)}, bf16[128,640]{1,0:T(8,128)(2,1)S(1)}, u32[]{:S(2)}, u32[]{:S(2)}) collective-permute-start(bf16[128,640]{1,0:T(8,128)(2,1)S(1)} %get-tuple-element.4), channel_id=1, source_target_pairs={{0,11},{1,0},{2,1},{3,2},{4,3},{5,4},{6,5},{7,6},{8,7},{9,8},{10,9... | collective-permute-start | bytes 491528 | tf_op jit(solution)/shard_map/ppermute | solution.py:27
Sparse Core Ops, SparseCore 0:
  16.7 55.5 all-gather.1
  75.9 44.0 reduce-scatter.4
  123.7 27.4 reduce-scatter.2

commit v12 on v8

--- a/solution.py
+++ b/solution.py
@@ -66,11 +66,9 @@
 
     two_away = partial(turned[2])
     ahead, behind, _ = lax.optimization_barrier((turned[1], turned[3], two_away))
-    arrived = (
-        over_col(two_away, 2),
-        over_col(partial(ahead), 1),
-        over_col(partial(behind), -1),
-    )
+    from_back = over_col(partial(behind), -1)
+    from_front = over_col(partial(ahead), 1)
+    arrived = (over_col(two_away, 2), from_front, from_back)
     mine = add(partial(turned[0]), *arrived)
     from_behind = over_col(mine, 4)
     from_ahead = over_col(mine, -4)

time: 163 us -> 163 us (level)
  no operation moved by 1% of the time
where the time goes in v12:
time: 163 us; the launch traced here: 161 us
  waiting for transfers between devices  83.8 us (51%)
  starting transfers between devices  37.7 us (23%)
  between operations  14.8 us (9%)
  matrix products  12 us (7%)
  blocking collectives  9.31 us (6%)
  other arithmetic  1.73 us (1%)
    ppermute x8, waiting for transfers between devices, over_col(): return lax.ppermute(value, ('row', 'col'), pairs)  37.9 us
    ppermute x8, starting transfers between devices, over_col(): return lax.ppermute(value, ('row', 'col'), pairs)  33.5 us
    ppermute x1, waiting for transfers between devices, over_rep(): return lax.ppermute(value, 'rep', pairs)  32.8 us
    all_gather x1, waiting for transfers between devices, gather_weight(): lax.all_gather(pair, 'rep', axis=1, tiled=True, axis_index_groups=Y_RINGS)  13 us
    all_gather x1, blocking collectives, gather_weight(): lax.all_gather(w0, 'rep', axis=0, tiled=True, axis_index_groups=X_PAIRS)  9.31 us
    dot_general x4, matrix products, partial(): lax.dot_general(tokens, weight, (((1,), (1,)), ((), ())), preferred_eleme...  5.82 us
    ppermute x1, starting transfers between devices, over_rep(): return lax.ppermute(value, 'rep', pairs)  4.03 us
  transfers between devices with their start and end apart: 12, of which 9 were waited for; matrix products, arithmetic and copies ran while one was open for 9% of the time, Pallas kernels for 0%

profile of v12, /device:TPU:6, one launch (start us, length us, event | category | flops | bytes accessed | tf_op | source)
XLA Modules:
  0.0 160.6 jit_solution(6806111521341016850)
XLA Ops:
  7.2 9.3 %all_gather.6 = bf16[2,80,1152]{2,1,0:T(8,128)(2,1)} all-gather(bf16[1,80,1152]{2,1,0:T(8,128)(2,1)} %param.5), channel_id=1, replica_groups={{0,384},{48,432},{96,480},{144,528},{192,576},{240,624},{288,672},{336,..., dimensions={0}, use_global_device_ids=true | all-gather | bytes 552960 | tf_op jit(solution)/shard_map/all_gather | solution.py:38
  17.4 1.5 broadcast_select_fusion
  18.8 1.1 fusion.2
  19.9 4.0 %collective-permute-start.8 = (bf16[640,1152]{1,0:T(8,128)(2,1)S(1)}, bf16[640,1152]{1,0:T(8,128)(2,1)S(1)}, u32[]{:S(2)}, u32[]{:S(2)}) collective-permute-start(bf16[640,1152]{1,0:T(8,128)(2,1)S(1)} %fusion.2), channel_id=1, source_target_pairs={{0,384},{48,432},{96,480},{144,528},{192,576},{240,624},{288,672},... | collective-permute-start | bytes 4423688 | tf_op jit(solution)/shard_map/ppermute | solution.py:19
  23.9 32.8 %collective-permute-done.8 = bf16[640,1152]{1,0:T(8,128)(2,1)S(1)} collective-permute-done((bf16[640,1152]{1,0:T(8,128)(2,1)S(1)}, bf16[640,1152]{1,0:T(8,128)(2,1)S(1)}, u32[]{:S(2)}, u32[]{:S(2)}) %collective-permute-start.8) | collective-permute-done | bytes 1474592 | tf_op jit(solution)/shard_map/ppermute | solution.py:19
  56.8 2.2 %add_convert_fusion = bf16[640,1152]{1,0:T(8,128)(2,1)} fusion(bf16[640,1152]{1,0:T(8,128)(2,1)S(1)} %collective-permute-done.8, bf16[512,1152]{1,0:T(8,128)(2,1)S(1)} %broadcast_select_fusion, pred[]{:T(512)S(6)} %lt.46, bf16[512,1280]{1,0:T(8,128)(2,1)S(1)} %copy-done.2), kind=kOutput, calls=%fused_computation.6 | convolution fusion | flops 759726080 | bytes 5439489 | tf_op jit(solution)/shard_map/dot_general | solution.py:48
  59.0 0.0 reduce-scatter.3.cloned.1.call-start
  59.1 0.1 dynamic-slice_bitcast_fusion
  59.2 13.0 %all-gather.2.cloned.1.call-done = bf16[2,640,1152]{2,1,0:T(8,128)(2,1)} async-done(((bf16[2,80,1152]{2,1,0:T(8,128)(2,1)}), bf16[2,640,1152]{2,1,0:T(8,128)(2,1)}) %all-gather.2.cloned.1.call-update) | async-done | bytes 2949136 | tf_op jit(solution)/shard_map/all_gather | solution.py:39
  72.2 2.9 %convolution_convert_fusion.3 = bf16[128,1280]{1,0:T(8,128)(2,1)S(1)} fusion(bf16[128,1152]{1,0:T(8,128)(2,1)S(1)} %get-tuple-element.10, bf16[1280,1152]{1,0:T(8,128)(2,1)} %bitcast.34), kind=kOutput, calls=%fused_computation.9 | convolution fusion | flops 377651200 | bytes 3571712 | tf_op jit(solution)/shard_map/dot_general | solution.py:62
  75.2 1.0 convolution_convert_fusion.2
  76.1 1.0 convolution_convert_fusion.1
  77.1 6.7 %collective-permute-start.2 = (bf16[128,1280]{1,0:T(8,128)(2,1)S(1)}, bf16[128,1280]{1,0:T(8,128)(2,1)S(1)}, u32[]{:S(2)}, u32[]{:S(2)}) collective-permute-start(bf16[128,1280]{1,0:T(8,128)(2,1)S(1)} %convolution_convert_fusion.1), channel_id=1, source_target_pairs={{0,11},{1,0},{2,1},{3,2},{4,3},{5,4},{6,5},{7,6},{8,7},{9,8},{10,9... | collective-permute-start | bytes 983048 | tf_op jit(solution)/shard_map/ppermute | solution.py:27
  83.8 1.9 %collective-permute-start.1 = (bf16[128,1280]{1,0:T(8,128)(2,1)S(1)}, bf16[128,1280]{1,0:T(8,128)(2,1)S(1)}, u32[]{:S(2)}, u32[]{:S(2)}) collective-permute-start(bf16[128,1280]{1,0:T(8,128)(2,1)S(1)} %convolution_convert_fusion.2), channel_id=1, source_target_pairs={{0,1},{1,2},{2,3},{3,4},{4,5},{5,6},{6,7},{7,8},{8,9},{9,10},{10,1... | collective-permute-start | bytes 983048 | tf_op jit(solution)/shard_map/ppermute | solution.py:27
  85.8 2.0 %collective-permute-start = (bf16[128,1280]{1,0:T(8,128)(2,1)S(1)}, bf16[128,1280]{1,0:T(8,128)(2,1)S(1)}, u32[]{:S(2)}, u32[]{:S(2)}) collective-permute-start(bf16[128,1280]{1,0:T(8,128)(2,1)S(1)} %convolution_convert_fusion.3), channel_id=1, source_target_pairs={{0,2},{1,3},{2,4},{3,5},{4,6},{5,7},{6,8},{7,9},{8,10},{9,11},{10,... | collective-permute-start | bytes 983048 | tf_op jit(solution)/shard_map/ppermute | solution.py:27
  87.8 7.5 %collective-permute-done.2 = bf16[128,1280]{1,0:T(8,128)(2,1)S(1)} collective-permute-done((bf16[128,1280]{1,0:T(8,128)(2,1)S(1)}, bf16[128,1280]{1,0:T(8,128)(2,1)S(1)}, u32[]{:S(2)}, u32[]{:S(2)}) %collective-permute-start.2) | collective-permute-done | bytes 327712 | tf_op jit(solution)/shard_map/ppermute | solution.py:27
  95.3 0.1 collective-permute-done.1
  95.4 2.4 %collective-permute-done = bf16[128,1280]{1,0:T(8,128)(2,1)S(1)} collective-permute-done((bf16[128,1280]{1,0:T(8,128)(2,1)S(1)}, bf16[128,1280]{1,0:T(8,128)(2,1)S(1)}, u32[]{:S(2)}, u32[]{:S(2)}) %collective-permute-start) | collective-permute-done | bytes 327712 | tf_op jit(solution)/shard_map/ppermute | solution.py:27
  97.8 1.0 add_convert_fusion.2
  98.8 6.3 %collective-permute-start.4 = (bf16[128,1280]{1,0:T(8,128)(2,1)S(1)}, bf16[128,1280]{1,0:T(8,128)(2,1)S(1)}, u32[]{:S(2)}, u32[]{:S(2)}) collective-permute-start(bf16[128,1280]{1,0:T(8,128)(2,1)S(1)} %add_convert_fusion.2), channel_id=1, source_target_pairs={{0,8},{1,9},{2,10},{3,11},{4,0},{5,1},{6,2},{7,3},{8,4},{9,5},{10,... | collective-permute-start | bytes 983048 | tf_op jit(solution)/shard_map/ppermute | solution.py:27
  105.1 3.5 %collective-permute-start.3 = (bf16[128,1280]{1,0:T(8,128)(2,1)S(1)}, bf16[128,1280]{1,0:T(8,128)(2,1)S(1)}, u32[]{:S(2)}, u32[]{:S(2)}) collective-permute-start(bf16[128,1280]{1,0:T(8,128)(2,1)S(1)} %add_convert_fusion.2), channel_id=1, source_target_pairs={{0,4},{1,5},{2,6},{3,7},{4,8},{5,9},{6,10},{7,11},{8,0},{9,1},{10,... | collective-permute-start | bytes 983048 | tf_op jit(solution)/shard_map/ppermute | solution.py:27
  108.6 2.9 %convolution_convert_fusion = bf16[512,1152]{1,0:T(8,128)(2,1)} fusion(bf16[512,1280]{1,0:T(8,128)(2,1)S(1)} %copy-done.3, bf16[1280,1152]{1,0:T(8,128)(2,1)S(1)} %bitcast.38), kind=kOutput, calls=%fused_computation.5 | convolution fusion | flops 1510539264 | bytes 5439488 | tf_op jit(solution)/shard_map/dot_general | solution.py:119
  111.5 11.8 %collective-permute-done.4 = bf16[128,1280]{1,0:T(8,128)(2,1)S(1)} collective-permute-done((bf16[128,1280]{1,0:T(8,128)(2,1)S(1)}, bf16[128,1280]{1,0:T(8,128)(2,1)S(1)}, u32[]{:S(2)}, u32[]{:S(2)}) %collective-permute-start.4) | collective-permute-done | bytes 327712 | tf_op jit(solution)/shard_map/ppermute | solution.py:27
  123.4 8.6 %collective-permute-done.3 = bf16[128,1280]{1,0:T(8,128)(2,1)S(1)} collective-permute-done((bf16[128,1280]{1,0:T(8,128)(2,1)S(1)}, bf16[128,1280]{1,0:T(8,128)(2,1)S(1)}, u32[]{:S(2)}, u32[]{:S(2)}) %collective-permute-start.3) | collective-permute-done | bytes 327712 | tf_op jit(solution)/shard_map/ppermute | solution.py:27
  131.9 0.1 broadcast_in_dim.27
  132.0 0.3 bitcast_dynamic-update-slice_fusion.3
  132.3 1.9 %collective-permute-start.5 = (bf16[128,1280]{1,0:T(8,128)(2,1)S(1)}, bf16[128,1280]{1,0:T(8,128)(2,1)S(1)}, u32[]{:S(2)}, u32[]{:S(2)}) collective-permute-start(bf16[128,1280]{1,0:T(8,128)(2,1)S(1)} %get-tuple-element.16), channel_id=1, source_target_pairs={{0,2},{1,3},{2,4},{3,5},{4,6},{5,7},{6,8},{7,9},{8,10},{9,11},{10,... | collective-permute-start | bytes 983048 | tf_op jit(solution)/shard_map/ppermute | solution.py:27
  134.2 6.7 %collective-permute-start.6 = (bf16[128,1280]{1,0:T(8,128)(2,1)S(1)}, bf16[128,1280]{1,0:T(8,128)(2,1)S(1)}, u32[]{:S(2)}, u32[]{:S(2)}) collective-permute-start(bf16[128,1280]{1,0:T(8,128)(2,1)S(1)} %get-tuple-element.16), channel_id=1, source_target_pairs={{0,1},{1,2},{2,3},{3,4},{4,5},{5,6},{6,7},{7,8},{8,9},{9,10},{10,1... | collective-permute-start | bytes 983048 | tf_op jit(solution)/shard_map/ppermute | solution.py:27
  140.9 4.6 %collective-permute-start.7 = (bf16[128,1280]{1,0:T(8,128)(2,1)S(1)}, bf16[128,1280]{1,0:T(8,128)(2,1)S(1)}, u32[]{:S(2)}, u32[]{:S(2)}) collective-permute-start(bf16[128,1280]{1,0:T(8,128)(2,1)S(1)} %get-tuple-element.16), channel_id=1, source_target_pairs={{0,11},{1,0},{2,1},{3,2},{4,3},{5,4},{6,5},{7,6},{8,7},{9,8},{10,9... | collective-permute-start | bytes 983048 | tf_op jit(solution)/shard_map/ppermute | solution.py:27
  145.5 7.0 %collective-permute-done.6 = bf16[128,1280]{1,0:T(8,128)(2,1)S(1)} collective-permute-done((bf16[128,1280]{1,0:T(8,128)(2,1)S(1)}, bf16[128,1280]{1,0:T(8,128)(2,1)S(1)}, u32[]{:S(2)}, u32[]{:S(2)}) %collective-permute-start.6) | collective-permute-done | bytes 327712 | tf_op jit(solution)/shard_map/ppermute | solution.py:27
  152.5 0.4 collective-permute-done.7
  153.1 1.0 copy-done.1
  (19 shorter events, 0.3 us)
Async XLA Ops:
  7.2 65.1 %all-gather.2.cloned.1.call-start = ((), (), s32[]{:S(2)}) async-start(), calls=%async_computation.2 | async-start | bytes 3317760 | tf_op jit(solution)/shard_map/all_gather | solution.py:39
  16.5 2.3 %copy-start.2 = (bf16[512,1280]{1,0:T(8,128)(2,1)S(1)}, bf16[512,1280]{1,0:T(8,128)(2,1)}, u32[]{:S(2)}) copy-start(bf16[512,1280]{1,0:T(8,128)(2,1)} %param.4) | copy-start | bytes 3932164
  16.5 136.5 %reduce-scatter.5.cloned.1.call-start = ((), (), s32[]{:S(2)}) async-start(), calls=%async_computation.4 | async-start | bytes 1658880 | tf_op jit(solution)/shard_map/reduce_scatter | solution.py:55
  19.9 36.9 %collective-permute-start.8 = (bf16[640,1152]{1,0:T(8,128)(2,1)S(1)}, bf16[640,1152]{1,0:T(8,128)(2,1)S(1)}, u32[]{:S(2)}, u32[]{:S(2)}) collective-permute-start(bf16[640,1152]{1,0:T(8,128)(2,1)S(1)} %fusion.2), channel_id=1, source_target_pairs={{0,384},{48,432},{96,480},{144,528},{192,576},{240,624},{288,672},... | collective-permute-start | bytes 4423688 | tf_op jit(solution)/shard_map/ppermute | solution.py:19
  59.0 94.1 %reduce-scatter.3.cloned.1.call-start = ((), (), s32[]{:S(2)}) async-start(), calls=%async_computation.3 | async-start | bytes 1474560 | tf_op jit(solution)/shard_map/reduce_scatter | solution.py:120
  72.2 2.9 %copy-start = (bf16[2,640,1152]{2,1,0:T(8,128)(2,1)S(1)}, bf16[2,640,1152]{2,1,0:T(8,128)(2,1)}, u32[]{:S(2)}) copy-start(bf16[2,640,1152]{2,1,0:T(8,128)(2,1)} %all-gather.2.cloned.1.call-done) | copy-start | bytes 8847364
  77.1 31.5 %copy-start.3 = (bf16[512,1280]{1,0:T(8,128)(2,1)S(1)}, bf16[512,1280]{1,0:T(8,128)(2,1)}, u32[]{:S(2)}) copy-start(bf16[512,1280]{1,0:T(8,128)(2,1)} %param.4) | copy-start | bytes 3932164
  77.1 18.2 %collective-permute-start.2 = (bf16[128,1280]{1,0:T(8,128)(2,1)S(1)}, bf16[128,1280]{1,0:T(8,128)(2,1)S(1)}, u32[]{:S(2)}, u32[]{:S(2)}) collective-permute-start(bf16[128,1280]{1,0:T(8,128)(2,1)S(1)} %convolution_convert_fusion.1), channel_id=1, source_target_pairs={{0,11},{1,0},{2,1},{3,2},{4,3},{5,4},{6,5},{7,6},{8,7},{9,8},{10,9... | collective-permute-start | bytes 983048 | tf_op jit(solution)/shard_map/ppermute | solution.py:27
  83.8 11.5 %collective-permute-start.1 = (bf16[128,1280]{1,0:T(8,128)(2,1)S(1)}, bf16[128,1280]{1,0:T(8,128)(2,1)S(1)}, u32[]{:S(2)}, u32[]{:S(2)}) collective-permute-start(bf16[128,1280]{1,0:T(8,128)(2,1)S(1)} %convolution_convert_fusion.2), channel_id=1, source_target_pairs={{0,1},{1,2},{2,3},{3,4},{4,5},{5,6},{6,7},{7,8},{8,9},{9,10},{10,1... | collective-permute-start | bytes 983048 | tf_op jit(solution)/shard_map/ppermute | solution.py:27
  85.8 12.0 %collective-permute-start = (bf16[128,1280]{1,0:T(8,128)(2,1)S(1)}, bf16[128,1280]{1,0:T(8,128)(2,1)S(1)}, u32[]{:S(2)}, u32[]{:S(2)}) collective-permute-start(bf16[128,1280]{1,0:T(8,128)(2,1)S(1)} %convolution_convert_fusion.3), channel_id=1, source_target_pairs={{0,2},{1,3},{2,4},{3,5},{4,6},{5,7},{6,8},{7,9},{8,10},{9,11},{10,... | collective-permute-start | bytes 983048 | tf_op jit(solution)/shard_map/ppermute | solution.py:27
  98.8 24.6 %collective-permute-start.4 = (bf16[128,1280]{1,0:T(8,128)(2,1)S(1)}, bf16[128,1280]{1,0:T(8,128)(2,1)S(1)}, u32[]{:S(2)}, u32[]{:S(2)}) collective-permute-start(bf16[128,1280]{1,0:T(8,128)(2,1)S(1)} %add_convert_fusion.2), channel_id=1, source_target_pairs={{0,8},{1,9},{2,10},{3,11},{4,0},{5,1},{6,2},{7,3},{8,4},{9,5},{10,... | collective-permute-start | bytes 983048 | tf_op jit(solution)/shard_map/ppermute | solution.py:27
  105.1 26.8 %collective-permute-start.3 = (bf16[128,1280]{1,0:T(8,128)(2,1)S(1)}, bf16[128,1280]{1,0:T(8,128)(2,1)S(1)}, u32[]{:S(2)}, u32[]{:S(2)}) collective-permute-start(bf16[128,1280]{1,0:T(8,128)(2,1)S(1)} %add_convert_fusion.2), channel_id=1, source_target_pairs={{0,4},{1,5},{2,6},{3,7},{4,8},{5,9},{6,10},{7,11},{8,0},{9,1},{10,... | collective-permute-start | bytes 983048 | tf_op jit(solution)/shard_map/ppermute | solution.py:27
  132.3 13.2 %collective-permute-start.5 = (bf16[128,1280]{1,0:T(8,128)(2,1)S(1)}, bf16[128,1280]{1,0:T(8,128)(2,1)S(1)}, u32[]{:S(2)}, u32[]{:S(2)}) collective-permute-start(bf16[128,1280]{1,0:T(8,128)(2,1)S(1)} %get-tuple-element.16), channel_id=1, source_target_pairs={{0,2},{1,3},{2,4},{3,5},{4,6},{5,7},{6,8},{7,9},{8,10},{9,11},{10,... | collective-permute-start | bytes 983048 | tf_op jit(solution)/shard_map/ppermute | solution.py:27
  134.2 18.3 %collective-permute-start.6 = (bf16[128,1280]{1,0:T(8,128)(2,1)S(1)}, bf16[128,1280]{1,0:T(8,128)(2,1)S(1)}, u32[]{:S(2)}, u32[]{:S(2)}) collective-permute-start(bf16[128,1280]{1,0:T(8,128)(2,1)S(1)} %get-tuple-element.16), channel_id=1, source_target_pairs={{0,1},{1,2},{2,3},{3,4},{4,5},{5,6},{6,7},{7,8},{8,9},{9,10},{10,1... | collective-permute-start | bytes 983048 | tf_op jit(solution)/shard_map/ppermute | solution.py:27
  140.9 12.1 %collective-permute-start.7 = (bf16[128,1280]{1,0:T(8,128)(2,1)S(1)}, bf16[128,1280]{1,0:T(8,128)(2,1)S(1)}, u32[]{:S(2)}, u32[]{:S(2)}) collective-permute-start(bf16[128,1280]{1,0:T(8,128)(2,1)S(1)} %get-tuple-element.16), channel_id=1, source_target_pairs={{0,11},{1,0},{2,1},{3,2},{4,3},{5,4},{6,5},{7,6},{8,7},{9,8},{10,9... | collective-permute-start | bytes 983048 | tf_op jit(solution)/shard_map/ppermute | solution.py:27
  153.0 1.1 copy-start.1
Sparse Core Ops, SparseCore 0:
  16.7 55.5 all-gather.1
  75.9 44.1 reduce-scatter.4
  123.9 27.4 reduce-scatter.2
